TPU v7x, 256 devices: a whole 4x4x8 slice. The times are simulated.
256 devices in a mesh: member: 16 (over z, x_lo), lat: 8 (over y, core), lon: 2 (over x_hi).
Axes of the slice: x: 4 (x_hi: 2, x_lo: 2; x = x_hi * 2 + x_lo), y: 4, z: 8, core: 2. Of those that a mesh axis runs over, the one named last changes fastest.
Arguments:
- state: bfloat16 [100, 16, 720], P(None, 'lat', 'lon'), may hold values from -6 to 6
- target: bfloat16 [100, 16, 720], P(None, 'lat', 'lon'), may hold values from -6 to 6
- land_sea: int32 [16, 720], P('lat', 'lon'), may hold values 0 or 1
- seeds: int32 [16, 32], P('member'), may hold values from 0 to 65535
- w_in: bfloat16 [9, 100, 256], replicated, may hold values from -0.1875 to 0.1875
- w_mid: bfloat16 [9, 256, 256], replicated, may hold values from -0.125 to 0.125
- w_out: bfloat16 [100, 256], replicated, may hold values from -0.375 to 0.375
- w_noise: float32 [32, 256], replicated, may hold values from -1 to 1
Outputs:
- update_in: float32 [9, 100, 256], replicated
- update_mid: float32 [9, 256, 256], replicated
- update_out: float32 [100, 256], replicated
- update_noise: float32 [32, 256], replicated
- loss: float32 [], replicated
All inputs are finite; a program needn't handle non-finite values. No bound on the sum of `land_sea` on one device may be relied on, other than what follows from the above.
Results may differ from a plain program's by a relative error of at most 0.0014.
Values may be sent and summed in bfloat16 or wider, within the bound.
No kernel may reach another device: no remote copies, remote signals or barrier semaphores. Data moves between devices by JAX's collectives and lax.ppermute only.
A program may use at most 64 MiB of HBM per device.

v0:
```python
import jax
import jax.numpy as jnp
from jax import lax
from jax.sharding import PartitionSpec as P

SMOOTH = 0.25


def with_halo(block, sides, width):
    for axis, dim in sides:
        count = lax.axis_size(axis)
        forward = [(i, i + 1) for i in range(count - 1)]
        forward.append((count - 1, 0))
        backward = [(target, source) for source, target in forward]
        low = lax.ppermute(
            lax.slice_in_dim(block, block.shape[dim] - width, None, axis=dim), axis, forward
        )
        high = lax.ppermute(lax.slice_in_dim(block, 0, width, axis=dim), axis, backward)
        block = jnp.concatenate([low, block, high], axis=dim)
    return block


def shifted(padded, offset, row_count, col_count):
    row_shift = offset // 3
    col_shift = offset % 3
    window = padded[:, row_shift : row_shift + row_count, col_shift : col_shift + col_count]
    return window.reshape(padded.shape[0], row_count * col_count)


def conv_forward(weights, padded, row_count, col_count):
    summed = None
    for offset in range(9):
        window = shifted(padded, offset, row_count, col_count)
        part = lax.dot_general(
            weights[offset], window, (((0,), (0,)), ((), ())), preferred_element_type=jnp.float32
        )
        summed = part if summed is None else summed + part
    return summed


def conv_back(weights, padded, row_count, col_count):
    summed = None
    for offset in range(9):
        window = shifted(padded, 8 - offset, row_count, col_count)
        part = jnp.dot(weights[offset], window, preferred_element_type=jnp.float32)
        summed = part if summed is None else summed + part
    return summed


def weight_grad(padded, deltas, row_count, col_count):
    parts = []
    for offset in range(9):
        window = shifted(padded, offset, row_count, col_count)
        parts.append(
            lax.dot_general(
                window, deltas, (((1,), (1,)), ((), ())), preferred_element_type=jnp.float32
            )
        )
    return jnp.stack(parts)


def gelu_pair(pre):
    return jax.jvp(jax.nn.gelu, (pre,), (jnp.ones_like(pre),))


def clear_outside(padded, width, lat_index, lat_count):
    row_count = padded.shape[1] - 2 * width
    global_row = lat_index * row_count + jnp.arange(padded.shape[1], dtype=jnp.int32) - width
    inside = (global_row >= 0) & (global_row < row_count * lat_count)
    return jnp.where(inside[None, :, None], padded, jnp.zeros((), padded.dtype))


def combine(outputs, target_flat, weights, slope_sum, spread_sum, members):
    misses = outputs - target_flat[None]
    radius = jnp.sqrt(misses * misses + SMOOTH * SMOOTH)
    gradients = weights[None] * (misses / radius / members - slope_sum / (members * (members - 1)))
    loss_term = jnp.sum(
        weights[None] * ((radius - SMOOTH) / members - spread_sum / (2 * members * (members - 1)))
    )
    return (gradients, loss_term)


def pair_sums(outputs, others, running):

    def add_member(totals, member_out):
        gap_value = outputs - member_out.astype(jnp.float32)[None]
        radius = jnp.sqrt(gap_value * gap_value + SMOOTH * SMOOTH)
        return ((totals[0] + gap_value / radius, totals[1] + radius - SMOOTH), None)

    sums, _ = lax.scan(add_member, running, others)
    return sums


def normalize(gradient):
    return gradient / jnp.sqrt(jnp.mean(gradient * gradient) + 1e-06)


def body(state, target, land_sea, seeds, w_in, w_mid, w_out, w_noise):
    variables, row_count, col_count = state.shape
    channels = w_in.shape[2]
    cell_count = row_count * col_count
    lat_index = lax.axis_index("lat")
    lat_count = lax.axis_size("lat")
    members = lax.axis_size("member")
    latent = (seeds[0].astype(jnp.float32) - 32767.5) / 18918.0
    noise_bias = jnp.dot(latent, w_noise, precision=lax.Precision.HIGHEST)
    state_wide = with_halo(state, (("lat", 1), ("lon", 2)), 2)
    state_wide = clear_outside(state_wide, 2, lat_index, lat_count)
    pre_ext = conv_forward(w_in, state_wide, row_count + 2, col_count + 2) + noise_bias[:, None]
    act_ext, slope_ext = gelu_pair(pre_ext)
    hidden_pad = act_ext.astype(jnp.bfloat16).reshape(channels, row_count + 2, col_count + 2)
    hidden_pad = clear_outside(hidden_pad, 1, lat_index, lat_count)
    state_pad = state_wide[:, 1:-1, 1:-1]
    slope_in = slope_ext.reshape(channels, row_count + 2, col_count + 2)[:, 1:-1, 1:-1].reshape(
        channels, cell_count
    )
    hidden_in = hidden_pad[:, 1:-1, 1:-1].reshape(channels, cell_count)
    pre_mid = conv_forward(w_mid, hidden_pad, row_count, col_count)
    act_mid, slope_mid = gelu_pair(pre_mid)
    hidden_out = (act_mid + hidden_in.astype(jnp.float32)).astype(jnp.bfloat16)
    flat_state = state.reshape(variables, cell_count).astype(jnp.float32)
    output = (flat_state + jnp.dot(w_out, hidden_out, preferred_element_type=jnp.float32)).astype(
        jnp.bfloat16
    )
    target_flat = target.reshape(variables, cell_count).astype(jnp.float32)
    weights = 1.0 + land_sea.reshape(1, cell_count).astype(jnp.float32)
    share_cells = cell_count // members
    gathered = lax.all_to_all(output[None], "member", split_axis=2, concat_axis=0, tiled=True)
    first_cell = lax.axis_index("member") * share_cells
    own_target = lax.dynamic_slice_in_dim(target_flat, first_cell, share_cells, 1)
    own_weights = lax.dynamic_slice_in_dim(weights, first_cell, share_cells, 1)
    gathered_f = gathered.astype(jnp.float32)
    blank = jnp.zeros(gathered_f.shape, jnp.float32)
    slope_sum, spread_sum = pair_sums(gathered_f, gathered, (blank, blank))
    gradients, loss_term = combine(
        gathered_f, own_target, own_weights, slope_sum, spread_sum, members
    )
    returned = lax.all_to_all(
        gradients.astype(jnp.bfloat16), "member", split_axis=0, concat_axis=2, tiled=True
    )
    delta_out = returned[0]
    grad_out = lax.dot_general(
        delta_out, hidden_out, (((1,), (1,)), ((), ())), preferred_element_type=jnp.float32
    )
    upstream = lax.dot_general(
        w_out, delta_out, (((0,), (0,)), ((), ())), preferred_element_type=jnp.float32
    )
    delta_mid = (upstream * slope_mid).astype(jnp.bfloat16)
    delta_pad = with_halo(
        delta_mid.reshape(channels, row_count, col_count), (("lat", 1), ("lon", 2)), 1
    )
    delta_pad = clear_outside(delta_pad, 1, lat_index, lat_count)
    incoming = conv_back(w_mid, delta_pad, row_count, col_count) + upstream
    delta_in = (incoming * slope_in).astype(jnp.bfloat16)
    grad_mid = weight_grad(hidden_pad, delta_mid, row_count, col_count)
    grad_in = weight_grad(state_pad, delta_in, row_count, col_count)
    grad_noise = latent[:, None] * jnp.sum(delta_in.astype(jnp.float32), axis=1)[None, :]
    grad_in, grad_mid, grad_out, grad_noise, summed = lax.psum(
        (grad_in, grad_mid, grad_out, grad_noise, loss_term), ("member", "lat", "lon")
    )
    loss = summed / (variables * cell_count * lat_count * lax.axis_size("lon"))
    return (
        normalize(grad_in),
        normalize(grad_mid),
        normalize(grad_out),
        normalize(grad_noise),
        loss,
    )


def solution(mesh):
    placed = (
        P(None, "lat", "lon"),
        P(None, "lat", "lon"),
        P("lat", "lon"),
        P("member", None),
        P(),
        P(),
        P(),
        P(),
    )
    return jax.shard_map(
        body, mesh=mesh, in_specs=placed, out_specs=(P(), P(), P(), P(), P()), check_vma=False
    )
```

profile of v0, /device:TPU:33, one launch (start us, length us, event | category | flops | bytes accessed | tf_op | source)
XLA Modules:
  0.0 407.1 jit_solution(16598785984211095864)
XLA Ops:
  7.2 1.9 collective-permute-start
  9.1 0.9 fusion.108
  10.0 1.5 collective-permute-done
  11.5 2.4 collective-permute-done.1
  13.9 1.3 pad_maximum_fusion.2
  15.2 2.8 collective-permute-start.2
  18.3 1.0 reshape.240
  19.3 4.2 %collective-permute-done.2 = bf16[100,6,2]{2,1,0:T(8,128)(2,1)S(1)} collective-permute-done((bf16[100,6,2]{2,1,0:T(8,128)(2,1)S(1)}, bf16[100,6,2]{2,1,0:T(8,128)(2,1)S(1)}, u32[]{:S(2)}, u32[]{:S(2)}) %collective-permute-start.2) | collective-permute-done | bytes 2432 | tf_op jit(solution)/shard_map/ppermute | solution.py:15
  23.5 4.4 %collective-permute-done.3 = bf16[100,6,2]{2,1,0:T(8,128)(2,1)S(1)} collective-permute-done((bf16[100,6,2]{2,1,0:T(8,128)(2,1)S(1)}, bf16[100,6,2]{2,1,0:T(8,128)(2,1)S(1)}, u32[]{:S(2)}, u32[]{:S(2)}) %collective-permute-start.3) | collective-permute-done | bytes 2432 | tf_op jit(solution)/shard_map/ppermute | solution.py:18
  27.9 1.3 maximum_select_fusion.1
  29.2 2.1 fusion.116
  33.2 1.3 reshape.207
  34.4 2.0 reshape.208
  36.4 1.3 fusion.97
  41.0 2.4 multiply_convert_fusion
  44.1 0.8 copy-done.2
  47.2 1.3 add_convert_fusion
  49.5 1.1 copy.20
  51.2 1.9 reduce.2
  53.0 0.9 reshape.246
  53.9 8.9 %all-to-all-start = ((bf16[16,2,2250]{2,1,0:T(2,128)(2,1)}), bf16[16,2,2250]{2,1,0:T(2,128)(2,1)S(1)}, u32[]{:S(2)}, u32[]{:S(2)}) async-start(bf16[16,2,2250]{2,1,0:T(2,128)(2,1)} %reshape.246), calls=%async_computation | async-start | bytes 294912 | tf_op jit(solution)/shard_map/all_to_all | solution.py:128
  63.2 2.7 reshape.229
  65.9 2.0 slice.303
  67.9 2.5 all-to-all-done
  70.8 1.1 bitcast_reduce_fusion
  71.9 0.8 bitcast_convert_fusion.1
  72.7 1.3 copy.23
  74.0 12.8 %while.15 = (s32[]{:T(128)}, f32[16,100,45]{2,1,0:T(8,128)S(1)}, f32[16,100,45]{2,1,0:T(8,128)S(1)}, bf16[16,100,45]{1,2,0:T(8,128)(2,1)S(1)}, f32[16,100,45]{2,1,0:T(8,128)S(1)}, /*index=5*/s32[]{:T(128)}, s32[]{:T(128)}) while((s32[]{:T(128)}, f32[16,100,45]{2,1,0:T(8,128)S(1)}, f32[16,100,45]{2,1,0:T(8,128)S(1)}, ...), condition=%wide.region_1.2_spmd.clone, body=%wide.region_0.1_spmd.clone.sunk | while | flops 652503 | bytes 1521091 | solution.py:90
  87.5 1.6 multiply_reduce_fusion.2
  89.1 5.1 %all-to-all-start.1 = ((bf16[16,100,45]{1,2,0:T(8,128)(2,1)}), bf16[16,100,45]{1,2,0:T(8,128)(2,1)S(1)}, u32[]{:S(2)}, u32[]{:S(2)}) async-start(bf16[16,100,45]{1,2,0:T(8,128)(2,1)} %get-tuple-element.163), calls=%async_computation.1 | async-start | bytes 393216 | tf_op jit(solution)/shard_map/all_to_all | solution.py:138
  94.3 1.7 fusion.115
  97.4 5.0 %all-to-all-done.1 = bf16[16,100,45]{1,2,0:T(8,128)(2,1)S(1)} async-done(((bf16[16,100,45]{1,2,0:T(8,128)(2,1)}), bf16[16,100,45]{1,2,0:T(8,128)(2,1)S(1)}, u32[]{:S(2)}, u32[]{:S(2)}) %all-to-all-start.1) | async-done | bytes 144032 | tf_op jit(solution)/shard_map/all_to_all | solution.py:138
  103.9 3.0 collective-permute-start.4
  109.6 2.4 collective-permute-done.5
  112.1 2.8 collective-permute-start.6
  115.4 0.9 fusion.118
  116.3 2.5 collective-permute-done.7
  119.6 0.9 copy-done.3
  122.9 0.8 copy-done.19
  126.0 0.9 copy-done.28
  127.1 76.7 %all-reduce = (f32[32,256]{1,0:T(8,128)S(1)}, f32[]{:T(128)}) all-reduce(f32[32,256]{1,0:T(8,128)S(1)} %broadcast_multiply_fusion, f32[]{:T(128)} %get-tuple-element.162), channel_id=1, replica_groups=mesh['member'=16,'lat'=8,'lon'=2] {'member','lat','lon'}, use_global_device_ids=true, to_apply=%region_9.10 | all-reduce | flops 8193 | bytes 65544 | tf_op jit(solution)/shard_map/psum | solution.py:158
  206.4 181.0 %all-reduce.4.cloned.1.call-done = (f32[9,100,256]{2,1,0:T(8,128)}, f32[9,256,256]{2,1,0:T(8,128)}, f32[100,256]{1,0:T(8,128)}) async-done(((f32[9,100,256]{2,1,0:T(8,128)}, f32[9,256,256]{2,1,0:T(8,128)}, f32[100,256]{1,0:T(8,128)}), (f32[9,100,256]{2,1,0:T(8,128)}, f32[9,256,256]{2,1,0:T(8,128)}, f32[100,256]{1,0:T(8,128)})) %all-reduce.4.cloned.1.call-update) | async-done | bytes 3383312 | tf_op jit(solution)/shard_map/psum | solution.py:158
  387.4 1.7 multiply_reduce_fusion.3
  389.8 1.6 broadcast_divide_fusion.2
  391.3 2.9 multiply_reduce_fusion
  394.9 1.6 broadcast_divide_fusion
  396.5 0.8 multiply_reduce_fusion.1
  398.1 1.0 broadcast_divide_fusion.1
  (224 shorter events, 36.0 us)
Async XLA Ops:
  7.2 42.1 %copy-start = (bf16[100,256]{1,0:T(8,128)(2,1)S(1)}, bf16[100,256]{1,0:T(8,128)(2,1)}, u32[]{:S(2)}) copy-start(bf16[100,256]{1,0:T(8,128)(2,1)} %param.16) | copy-start | bytes 153604
  7.2 20.7 %copy-start.27 = (bf16[100,2,360]{2,1,0:T(2,128)(2,1)S(1)}, bf16[100,2,360]{2,1,0:T(2,128)(2,1)}, u32[]{:S(2)}) copy-start(bf16[100,2,360]{2,1,0:T(2,128)(2,1)} %param.10) | copy-start | bytes 432004
  7.2 4.3 %collective-permute-start = (bf16[100,2,360]{2,1,0:T(2,128)(2,1)}, bf16[100,2,360]{2,1,0:T(2,128)(2,1)S(1)}, u32[]{:S(2)}, u32[]{:S(2)}) collective-permute-start(bf16[100,2,360]{2,1,0:T(2,128)(2,1)} %param.10), channel_id=1, source_target_pairs={{0,2},{2,4},{4,6},{6,8},{8,10},{10,12},{12,14},{14,0},{1,3},{3,5},... | collective-permute-start | bytes 432008 | tf_op jit(solution)/shard_map/ppermute | solution.py:15
  9.1 4.8 %collective-permute-start.1 = (bf16[100,2,360]{2,1,0:T(2,128)(2,1)}, bf16[100,2,360]{2,1,0:T(2,128)(2,1)S(1)}, u32[]{:S(2)}, u32[]{:S(2)}) collective-permute-start(bf16[100,2,360]{2,1,0:T(2,128)(2,1)} %param.10), channel_id=1, source_target_pairs={{2,0},{4,2},{6,4},{8,6},{10,8},{12,10},{14,12},{0,14},{3,1},{5,3},... | collective-permute-start | bytes 432008 | tf_op jit(solution)/shard_map/ppermute | solution.py:18
  15.2 8.3 %collective-permute-start.2 = (bf16[100,6,2]{2,1,0:T(8,128)(2,1)S(1)}, bf16[100,6,2]{2,1,0:T(8,128)(2,1)S(1)}, u32[]{:S(2)}, u32[]{:S(2)}) collective-permute-start(bf16[100,6,2]{2,1,0:T(8,128)(2,1)S(1)} %get-tuple-element.158), channel_id=1, source_target_pairs={{0,1},{1,0},{2,3},{3,2},{4,5},{5,4},{6,7},{7,6},{8,9},{9,8},{10,11... | collective-permute-start | bytes 7208 | tf_op jit(solution)/shard_map/ppermute | solution.py:15
  18.1 9.8 %collective-permute-start.3 = (bf16[100,6,2]{2,1,0:T(8,128)(2,1)S(1)}, bf16[100,6,2]{2,1,0:T(8,128)(2,1)S(1)}, u32[]{:S(2)}, u32[]{:S(2)}) collective-permute-start(bf16[100,6,2]{2,1,0:T(8,128)(2,1)S(1)} %get-tuple-element.159), channel_id=1, source_target_pairs={{1,0},{0,1},{3,2},{2,3},{5,4},{4,5},{7,6},{6,7},{9,8},{8,9},{11,10... | collective-permute-start | bytes 7208 | tf_op jit(solution)/shard_map/ppermute | solution.py:18
  36.4 1.3 copy-start.29
  40.0 1.0 copy-start.30
  43.7 1.3 copy-start.2
  44.1 1.4 copy-start.17
  44.1 1.4 copy-start.23
  44.1 1.4 copy-start.15
  44.1 1.7 copy-start.13
  44.1 2.2 copy-start.9
  44.1 2.5 copy-start.7
  44.1 2.8 copy-start.5
  44.1 3.0 copy-start.11
  44.1 3.0 copy-start.25
  48.5 0.7 copy-start.21
  48.5 14.3 %copy-start.32 = (s32[2,360]{1,0:T(2,128)S(1)}, s32[2,360]{1,0:T(2,128)}, u32[]{:S(2)}) copy-start(s32[2,360]{1,0:T(2,128)} %param.12) | copy-start | bytes 8644
  48.5 14.4 %copy-start.31 = (bf16[100,2,360]{2,1,0:T(2,128)(2,1)S(1)}, bf16[100,2,360]{2,1,0:T(2,128)(2,1)}, u32[]{:S(2)}) copy-start(bf16[100,2,360]{2,1,0:T(2,128)(2,1)} %param.11) | copy-start | bytes 432004
  53.9 16.5 %all-to-all-start = ((bf16[16,2,2250]{2,1,0:T(2,128)(2,1)}), bf16[16,2,2250]{2,1,0:T(2,128)(2,1)S(1)}, u32[]{:S(2)}, u32[]{:S(2)}) async-start(bf16[16,2,2250]{2,1,0:T(2,128)(2,1)} %reshape.246), calls=%async_computation | async-start | bytes 294912 | tf_op jit(solution)/shard_map/all_to_all | solution.py:128
  89.1 13.3 %all-to-all-start.1 = ((bf16[16,100,45]{1,2,0:T(8,128)(2,1)}), bf16[16,100,45]{1,2,0:T(8,128)(2,1)S(1)}, u32[]{:S(2)}, u32[]{:S(2)}) async-start(bf16[16,100,45]{1,2,0:T(8,128)(2,1)} %get-tuple-element.163), calls=%async_computation.1 | async-start | bytes 393216 | tf_op jit(solution)/shard_map/all_to_all | solution.py:138
  94.2 293.2 %all-reduce.4.cloned.1.call-start = ((), (), s32[]{:S(2)}) async-start(), calls=%async_computation.2 | async-start | bytes 6848512 | tf_op jit(solution)/shard_map/psum | solution.py:158
  96.1 6.4 %copy-start.34 = (f32[256,720]{0,1:T(8,128)S(1)}, f32[256,720]{0,1:T(8,128)}, u32[]{:S(2)}) copy-start(f32[256,720]{0,1:T(8,128)} %get-tuple-element.165) | copy-start | bytes 2211844
  102.5 1.0 copy-start.24
  103.1 3.8 copy-start.18
  103.1 4.1 %copy-start.16 = (bf16[256,2,360]{0,2,1:T(8,128)(2,1)S(1)}, bf16[256,2,360]{0,2,1:T(8,128)(2,1)}, u32[]{:S(2)}) copy-start(bf16[256,2,360]{0,2,1:T(8,128)(2,1)} %copy-done.15) | copy-start | bytes 1105924
  103.8 3.7 copy-start.14
  103.9 5.8 %collective-permute-start.4 = (bf16[256,1,360]{0,2,1:T(8,128)(2,1)S(1)}, bf16[256,1,360]{0,2,1:T(8,128)(2,1)S(1)}, u32[]{:S(2)}, u32[]{:S(2)}) collective-permute-start(bf16[256,1,360]{0,2,1:T(8,128)(2,1)S(1)} %get-tuple-element.160), channel_id=1, source_target_pairs={{0,2},{2,4},{4,6},{6,8},{8,10},{10,12},{12,14},{14,0},{1,3},{3,5},... | collective-permute-start | bytes 552968 | tf_op jit(solution)/shard_map/ppermute | solution.py:15
  106.9 1.0 copy-start.12
  106.9 5.2 %collective-permute-start.5 = (bf16[256,1,360]{0,2,1:T(8,128)(2,1)S(1)}, bf16[256,1,360]{0,2,1:T(8,128)(2,1)S(1)}, u32[]{:S(2)}, u32[]{:S(2)}) collective-permute-start(bf16[256,1,360]{0,2,1:T(8,128)(2,1)S(1)} %get-tuple-element.161), channel_id=1, source_target_pairs={{2,0},{4,2},{6,4},{8,6},{10,8},{12,10},{14,12},{0,14},{3,1},{5,3},... | collective-permute-start | bytes 552968 | tf_op jit(solution)/shard_map/ppermute | solution.py:18
  107.2 1.0 copy-start.10
  107.6 1.0 copy-start.8
  107.9 1.0 copy-start.6
  108.2 1.0 copy-start.26
  108.9 6.4 %copy-start.22 = (bf16[256,720]{0,1:T(8,128)(2,1)S(1)}, bf16[256,720]{0,1:T(8,128)(2,1)}, u32[]{:S(2)}) copy-start(bf16[256,720]{0,1:T(8,128)(2,1)} %copy-done.21) | copy-start | bytes 1105924
  109.6 10.0 %copy-start.20 = (f32[9,256,256]{2,1,0:T(8,128)}, f32[9,256,256]{2,1,0:T(8,128)S(1)}, u32[]{:S(2)}) copy-start(f32[9,256,256]{2,1,0:T(8,128)S(1)} %fusion.19) | copy-start | bytes 7077892
  112.1 4.3 %collective-permute-start.6 = (bf16[256,4,1]{0,2,1:T(2,128)(2,1)S(1)}, bf16[256,4,1]{0,2,1:T(2,128)(2,1)S(1)}, u32[]{:S(2)}, u32[]{:S(2)}) collective-permute-start(bf16[256,4,1]{0,2,1:T(2,128)(2,1)S(1)} %get-tuple-element.138), channel_id=1, source_target_pairs={{0,1},{1,0},{2,3},{3,2},{4,5},{5,4},{6,7},{7,6},{8,9},{9,8},{10,11... | collective-permute-start | bytes 6152 | tf_op jit(solution)/shard_map/ppermute | solution.py:15
  114.9 4.0 collective-permute-start.7
  119.2 1.3 copy-start.3
  122.6 1.1 copy-start.19
  126.0 0.9 copy-start.28
  126.0 1.0 copy-start.33
  387.4 7.5 %copy-start.1 = (f32[9,256,256]{2,1,0:T(8,128)S(1)}, f32[9,256,256]{2,1,0:T(8,128)}, u32[]{:S(2)}) copy-start(f32[9,256,256]{2,1,0:T(8,128)} %get-tuple-element.114) | copy-start | bytes 7077892
  394.9 1.6 copy-start.4
Sparse Core Ops, SparseCore 0:
  127.1 260.2 all-reduce.3
where the time goes:
time: 412 us; the launch traced here: 407 us
  waiting for transfers between devices  206 us (50%)
  blocking collectives  76.7 us (19%)
  local copies, waits for them, and re-layouts  30.9 us (8%)
  other arithmetic  28.4 us (7%)
  starting transfers between devices  25.3 us (6%)
  matrix products  19.7 us (5%)
  between operations  19.6 us (5%)
    psum x1, waiting for transfers between devices, body(): lax.psum((grad_in, grad_mid, grad_out, grad_noise, loss_term), ('member',...  181 us
    psum x1, blocking collectives, body(): lax.psum((grad_in, grad_mid, grad_out, grad_noise, loss_term), ('member',...  76.7 us
    ppermute x4, waiting for transfers between devices, with_halo(): lax.ppermute(lax.slice_in_dim(block, 0, width, axis=dim), axis, backward)  11.7 us
    ppermute x4, starting transfers between devices, with_halo(): lax.ppermute(lax.slice_in_dim(block, block.shape[dim] - width, None, axis...  10.5 us
    sub x16, other arithmetic, add_member(): return ((totals[0] + gap_value / radius, totals[1] + radius - SMOOTH), None)  10 us
    dot_general x18, matrix products, conv_forward(): lax.dot_general(weights[offset], window, (((0,), (0,)), ((), ())), prefer...  9.7 us
    all_to_all x1, starting transfers between devices, body(): lax.all_to_all(output[None], 'member', split_axis=2, concat_axis=0, tiled...  8.93 us
    unnamed x74, local copies, waits for them, and re-layouts  8.48 us
  transfers between devices with their start and end apart: 11, of which 10 were waited for; matrix products, arithmetic and copies ran while one was open for 4% of the time, Pallas kernels for 0%

commit v1 on v0

v1 whole, which is shorter than its diff:
```python
import jax
import jax.numpy as jnp
from jax import lax
from jax.experimental import pallas as pl
from jax.experimental.pallas import tpu as pltpu
from jax.sharding import Mesh, PartitionSpec as P

f32 = jnp.float32
bf16 = jnp.bfloat16
SQ = 0.0625
GC = 0.7978845608028654
GA = 0.044715
V = 100
C = 256
M = 16
TC = 360
WP = 32
WH = 27
ROWS = 104
BR = 112
NB = 32
AX = ("z", "xl", "y", "c", "xh")
VMEM = 56 * 1024 * 1024


def perm(f, keep=None):
    out = []
    for i in range(256):
        z, xl, lat, xh = i >> 5, (i >> 4) & 1, (i >> 1) & 7, i & 1
        t = f(z, xl, lat, xh)
        if t is None:
            continue
        z2, xl2, lat2, xh2 = t
        out.append((i, (z2 % 8) * 32 + xl2 * 16 + lat2 * 2 + xh2))
    return out


def send(v, f):
    return lax.ppermute(v, AX, perm(f))


def lat_shift(v, d):
    def f(z, xl, lat, xh):
        return (z, xl, lat + d, xh) if 0 <= lat + d < 8 else None

    return send(v, f)


def params():
    return pltpu.CompilerParams(vmem_limit_bytes=VMEM)


def gelu(x):
    t = jnp.tanh(GC * (x + GA * x * x * x))
    return 0.5 * x * (1.0 + t)


def gelu_both(x):
    x2 = x * x
    t = jnp.tanh(GC * (x + GA * x2 * x))
    h = 0.5 * (1.0 + t)
    slope = h + 0.5 * x * (1.0 - t * t) * (GC * (1.0 + 3.0 * GA * x2))
    return x * h, slope


def gelu_slope(x):
    return gelu_both(x)[1]


def prep_kernel(state, target, land, x_out, edge_out, sc):
    sc[...] = jnp.zeros(sc.shape, f32)
    edge_out[...] = jnp.zeros(edge_out.shape, f32)
    for r in range(2):
        sc[0:V, 0:TC] = state[:, r, :].astype(f32)
        sc[104:105, 0:TC] = 1.0 + land[r : r + 1, :].astype(f32)
        x_out[r, :, 0:128] = sc[...].T
        sc[0:V, 0:TC] = target[:, r, :].astype(f32)
        x_out[r, :, 128:256] = sc[...].T
        edge_out[r, 0:3, :] = x_out[r, TC - 3 : TC, :]
        edge_out[r, 3:6, :] = x_out[r, 0:3, :]


def window_kernel(info, x, edge, win, ws):
    start = info[1]
    for r in range(2):
        ws[r, 8 : 8 + TC, :] = x[r, 0:TC, :]
        ws[r, 5:8, :] = edge[r, 0:3, :]
        ws[r, 8 + TC : 11 + TC, :] = edge[r, 3:6, :]
        ws[r, 11 + TC : 16 + TC, :] = jnp.zeros((5, 256), f32)
        base = pl.multiple_of(((start + 5) // 8) * 8, 8)
        near = ws[r, pl.ds(base, WP + 8), :]
        win[r, :, :] = pltpu.roll(near, WP + 8 - (start + 5 - base), 0)[0:WP].astype(bf16)


def main_kernel(
    info, n2, n1, own, s1, s2, seeds, w_in, w_mid, w_out, w_noise, g_out,
    S, T, SB, PB, HID, HO, SL, UP, OUT, DO, DM, INC, DS, QB, BIAS,
):
    own22 = info[2]
    lat = info[3]
    rows = (n2[1], n1[0], n1[1], own[0], own[1], s1[0], s1[1], s2[0])
    for k, row in enumerate(rows):
        S[32 * k : 32 * k + 32, :] = row[:, 0:128].astype(f32)
        T[32 * k : 32 * k + 32, :] = row[:, 128:256].astype(f32)
    S[256:264, :] = jnp.zeros((8, 128), f32)
    T[256:264, :] = jnp.zeros((8, 128), f32)
    QB[...] = jnp.broadcast_to(S[:, 104:105], QB.shape)
    for b in range(3):
        SB[b] = S[b : b + 256, :].astype(bf16)
    latents = (seeds[...].astype(f32) - 32767.5) / 18918.0
    BIAS[...] = jnp.dot(
        latents, w_noise[...], precision=lax.Precision.HIGHEST, preferred_element_type=f32
    )
    acc = None
    for a in range(3):
        for b in range(3):
            part = jnp.dot(
                SB[b, a * 32 : a * 32 + 192, 0:V], w_in[3 * a + b], preferred_element_type=f32
            )
            acc = part if acc is None else acc + part
    PB[...] = acc

    bias = BIAS[...]
    HID[162 * M : 164 * M, :] = jnp.zeros((2 * M, C), bf16)
    for r in range(6):
        gr = lat * 2 - 2 + r
        valid = jnp.where((gr >= 0) & (gr < 16), 1.0, 0.0).astype(f32)

        def hid_cell(i, carry, r=r, valid=valid):
            row = PB[pl.ds(r * 32 + i, 1), :]
            h = gelu(jnp.broadcast_to(row, (M, C)) + bias) * valid
            HID[pl.ds(pl.multiple_of((r * WH + i) * M, M), M), :] = h.astype(bf16)
            return carry

        lax.fori_loop(0, WH, hid_cell, 0, unroll=9)

    NR = WH * M

    def mid_row(r, carry):
        lhs = jnp.concatenate(
            [
                HID[pl.ds(pl.multiple_of(((r + a) * WH + b) * M, M), NR), :]
                for a in range(3)
                for b in range(3)
            ],
            axis=1,
        )
        pre = jnp.dot(lhs, w_mid[...].reshape(9 * C, C), preferred_element_type=f32)
        act, slope = gelu_both(pre)
        hid = HID[pl.ds(pl.multiple_of(((r + 1) * WH + 1) * M, M), NR), :].astype(f32)
        base = pl.multiple_of(r * NR, M)
        ho = (act + hid).astype(bf16)
        HO[pl.ds(base, NR), :] = ho
        SL[pl.ds(base, NR), :] = slope
        OUT[pl.ds(base, NR), 0:V] = lax.dot_general(
            ho, w_out[...], (((1,), (1,)), ((), ())), preferred_element_type=f32
        )
        return carry

    lax.fori_loop(0, 4, mid_row, 0)

    def cell_terms(r, i, with_loss):
        base = pl.multiple_of((r * WH + i) * M, M)
        srow = (r + 2) * 32 + i + 2
        st = S[pl.ds(srow, 1), :]
        tg = T[pl.ds(srow, 1), :]
        q = QB[pl.ds(srow, 1), :]
        o = (OUT[pl.ds(base, M), :] + st).astype(bf16).astype(f32)
        miss = o - tg
        e = miss * miss + SQ
        inv = lax.rsqrt(e)
        slope = miss * inv
        dist = e * inv - 0.25 if with_loss else None
        total = None
        spread = None
        for k in range(1, 9):
            u = o - pltpu.roll(o, k, 0)
            e = u * u + SQ
            inv = lax.rsqrt(e)
            s = u * inv
            if k < 8:
                s = s - pltpu.roll(s, M - k, 0)
            total = s if total is None else total + s
            if with_loss:
                d = e * inv - 0.25
                if k == 8:
                    d = 0.5 * d
                spread = d if spread is None else spread + d
        g = q * (slope * (1.0 / M) - total * (1.0 / (M * (M - 1))))
        DO[pl.ds(base, M), :] = g.astype(bf16)
        if with_loss:
            return q * (dist * (1.0 / M) - spread * (1.0 / (M * (M - 1))))
        return None

    loss = jnp.zeros((M, 128), f32)
    for r in (1, 2):

        def loss_cell(i, total, r=r):
            term = cell_terms(r, i, True)
            mine = (i >= 1) & ((i < 23) | ((i == 23) & (own22 > 0)))
            return total + jnp.where(mine, 1.0, 0.0) * term

        loss = lax.fori_loop(0, WH, loss_cell, loss, unroll=3)
    for r in (0, 3):

        def grad_cell(i, carry, r=r):
            cell_terms(r, i, False)
            return carry

        lax.fori_loop(0, WH, grad_cell, 0, unroll=3)
    lane = lax.broadcasted_iota(jnp.int32, (M, 128), 1)
    loss = jnp.sum(jnp.sum(jnp.where(lane < V, loss, 0.0), axis=0, keepdims=True), axis=1, keepdims=True)

    def up_row(r, carry):
        base = pl.multiple_of(r * NR, M)
        up = jnp.dot(DO[pl.ds(base, NR), 0:V], w_out[...], preferred_element_type=f32)
        UP[pl.ds(base, NR), :] = up
        DM[pl.ds(base, NR), :] = (up * SL[pl.ds(base, NR), :]).astype(bf16)
        return carry

    lax.fori_loop(0, 4, up_row, 0)
    DM[108 * M : 112 * M, :] = jnp.zeros((4 * M, C), bf16)

    wcat = jnp.concatenate([w_mid[t] for t in range(9)], axis=1)
    for r in range(2):
        lhs = jnp.concatenate(
            [
                DM[((r + 2 - a) * WH + 2 - b) * M : ((r + 2 - a) * WH + 2 - b) * M + NR, :]
                for a in range(3)
                for b in range(3)
            ],
            axis=1,
        )
        INC[r * NR : (r + 1) * NR, :] = lax.dot_general(
            lhs, wcat, (((1,), (1,)), ((), ())), preferred_element_type=f32
        )
    DS[...] = jnp.zeros(DS.shape, f32)
    dsum = jnp.zeros((M, C), f32)
    for r in range(2):

        def in_cell(i, total, r=r):
            x = jnp.broadcast_to(PB[pl.ds((r + 2) * 32 + i + 2, 1), :], (M, C)) + bias
            base = pl.multiple_of((r * WH + i) * M, M)
            upb = pl.multiple_of(((r + 1) * WH + 1 + i) * M, M)
            d = (INC[pl.ds(base, M), :] + UP[pl.ds(upb, M), :]) * gelu_slope(x)
            mine = jnp.where((i < 22) | (own22 > 0), 1.0, 0.0)
            d = d.astype(bf16).astype(f32) * mine
            DS[pl.ds(r * 32 + i + 2, 1), :] = jnp.sum(d, axis=0, keepdims=True)
            return total + d

        dsum = lax.fori_loop(0, 23, in_cell, dsum)

    g_out[:, ROWS:BR, :] = jnp.zeros((NB, BR - ROWS, C), f32)

    def put(row, value):
        done = 0
        n = value.shape[0]
        while done < n:
            k, i = divmod(row + done, ROWS)
            take = min(n - done, ROWS - i)
            g_out[k, i : i + take, :] = value[done : done + take, :]
            done += take

    cell = lax.broadcasted_iota(jnp.int32, (NR, C), 0) >> 4
    mine = (cell < 22) | ((cell == 22) & (own22 > 0))
    start = (WH + 1) * M
    dmc = jnp.concatenate(
        [
            jnp.where(mine, DM[start + r * NR : start + (r + 1) * NR, :].astype(f32), 0.0)
            for r in range(2)
        ],
        axis=0,
    )
    dmt = dmc.T.astype(bf16)
    for a in range(3):
        for b in range(3):
            hs = ((a + 1) * WH + b + 1) * M
            g = jnp.dot(dmt, HID[hs : hs + 2 * NR, :], preferred_element_type=f32)
            put((3 * a + b) * C, g.T)
    doc = jnp.concatenate(
        [
            jnp.where(
                mine[:, 0:128], DO[start + r * NR : start + (r + 1) * NR, :].astype(f32), 0.0
            )
            for r in range(2)
        ],
        axis=0,
    )
    dot_ = doc.T.astype(bf16)
    go = jnp.dot(dot_, HO[start : start + 2 * NR, :], preferred_element_type=f32)
    ds = DS[...]
    hi = ds.astype(bf16)
    lo = (ds - hi.astype(f32)).astype(bf16)
    both = jnp.concatenate([hi, lo], axis=1)
    for a in range(3):
        for b in range(3):
            g = lax.dot_general(
                SB[b, (a + 2) * 32 : (a + 2) * 32 + 64, :], both,
                (((0,), (0,)), ((), ())), preferred_element_type=f32,
            )
            put(9 * C + V * (3 * a + b), (g[:, 0:C] + g[:, C : 2 * C])[0:V, :])
    put(9 * C + 9 * V, go[0:V, :])
    put(9 * C + 10 * V, jnp.zeros((NB * ROWS - 9 * C - 10 * V, C), f32))
    gn = lax.dot_general(
        latents, dsum, (((0,), (0,)), ((), ())),
        precision=lax.Precision.HIGHEST, preferred_element_type=f32,
    )
    for k in range(NB):
        g_out[k, ROWS : ROWS + 1, :] = gn[k : k + 1, :]
    g_out[0, ROWS + 1 : ROWS + 2, :] = jnp.broadcast_to(loss, (1, C))


def final_kernel(t, o_in, o_mid, o_out, o_noise, o_loss):
    def get(row, n):
        parts = []
        done = 0
        while done < n:
            k, i = divmod(row + done, ROWS)
            take = min(n - done, ROWS - i)
            parts.append((done, take, t[k, i : i + take, :]))
            done += take
        return parts

    def norm(pieces, count, stores):
        total = jnp.zeros((1, C), f32)
        for p in pieces:
            for _, _, v in p:
                total = total + jnp.sum(v * v, axis=0, keepdims=True)
        ms = jnp.sum(total, axis=1, keepdims=True) * (1.0 / count)
        scale = lax.rsqrt(ms + 1e-6)
        for p, store in zip(pieces, stores):
            for done, take, v in p:
                store(done, take, v * scale)

    def into(ref, k):
        def f(done, take, v):
            ref[k, done : done + take, :] = v

        return f

    norm([get(C * k, C) for k in range(9)], 9 * C * C, [into(o_mid, k) for k in range(9)])
    norm(
        [get(9 * C + V * k, V) for k in range(9)], 9 * V * C, [into(o_in, k) for k in range(9)]
    )

    def out_store(done, take, v):
        o_out[done : done + take, :] = v

    norm([get(9 * C + 9 * V, V)], V * C, [out_store])

    def noise_store(done, take, v):
        o_noise[done : done + take, :] = v

    norm([[(k, 1, t[k, ROWS : ROWS + 1, :]) for k in range(NB)]], NB * C, [noise_store])
    o_loss[...] = t[0, ROWS + 1 : ROWS + 2, 0:128] * (1.0 / (V * 16 * 720))


def call(kernel, outs, scratch, n_smem, n_in, single=False):
    specs = [pl.BlockSpec(memory_space=pltpu.SMEM)] * n_smem
    specs += [pl.BlockSpec(memory_space=pltpu.VMEM)] * n_in
    out_specs = [pl.BlockSpec(memory_space=pltpu.VMEM)] * len(outs)
    shapes = [jax.ShapeDtypeStruct(s, d) for s, d in outs]
    return pl.pallas_call(
        kernel,
        out_shape=shapes[0] if single else shapes,
        in_specs=specs,
        out_specs=out_specs[0] if single else out_specs,
        scratch_shapes=scratch,
        compiler_params=params(),
    )


def sum_all(g):
    xy = ("xl", "y", "xh")
    core = lax.axis_index("c")

    def other(z, xl, lat, xh):
        return (z, xl, lat ^ 1, xh)

    g = g.reshape(2, 16, BR, C)
    theirs = lax.dynamic_index_in_dim(g, 1 - core, 0, False)
    mine = lax.dynamic_index_in_dim(g, core, 0, False)
    s = mine + send(theirs, other)
    s = lax.all_to_all(s, xy, 0, 0, tiled=True).sum(0)
    r1 = send(s, lambda z, xl, lat, xh: (z ^ 1, xl, lat, xh))
    r2 = send(s, lambda z, xl, lat, xh: (z ^ 2, xl, lat, xh))
    r3 = send(s, lambda z, xl, lat, xh: (z ^ 3, xl, lat, xh))
    s = (s + r1) + (r2 + r3)
    s = s + send(s, lambda z, xl, lat, xh: (z ^ 4, xl, lat, xh))
    half = lax.all_to_all(jnp.broadcast_to(s[None], (16,) + s.shape), xy, 0, 0, tiled=True)
    far = send(half, other)
    first = jnp.where(core == 0, half, far)
    second = jnp.where(core == 0, far, half)
    return jnp.concatenate([first, second], axis=0)


def gather_seeds(seeds):
    z = lax.axis_index("z")
    xl = lax.axis_index("xl")

    def spread(v, moves):
        return [v] + [
            send(v, lambda z, xl, lat, xh, d=d: (z ^ d[0], xl ^ d[1], lat, xh)) for d in moves
        ]

    near = jnp.concatenate(spread(seeds, ((0, 1), (1, 0), (1, 1))), axis=0)
    parts = spread(near, ((2, 0), (4, 0), (6, 0)))
    table = jnp.concatenate(parts, axis=0)
    member = z * 2 + xl
    order = jnp.bitwise_xor(jnp.arange(M, dtype=jnp.int32), member)
    return jnp.take(table, order, axis=0)


def body(state, target, land, seeds, w_in, w_mid, w_out, w_noise):
    z = lax.axis_index("z")
    xl = lax.axis_index("xl")
    lat = lax.axis_index("y") * 2 + lax.axis_index("c")
    member = z * 2 + xl
    info = jnp.stack([member, (45 * member) // 2, member % 2, lat]).astype(jnp.int32)
    x, edge = call(
        prep_kernel, [((2, 384, 256), f32), ((2, 8, 256), f32)],
        [pltpu.VMEM((128, 384), f32)], 0, 3,
    )(state, target, land)
    edge = send(edge, lambda z, xl, lat, xh: (z, xl, lat, xh ^ 1))
    win = call(
        window_kernel, [((2, WP, 256), bf16)], [pltpu.VMEM((2, 376, 256), f32)], 1, 2, True
    )(info, x, edge)
    n2, n1, s1, s2 = (lat_shift(win, d) for d in (2, 1, -1, -2))
    all_seeds = gather_seeds(seeds)
    g = call(
        main_kernel, [((NB, BR, C), f32)],
        [
            pltpu.VMEM((264, 128), f32),
            pltpu.VMEM((264, 128), f32),
            pltpu.VMEM((3, 256, 128), bf16),
            pltpu.VMEM((192, C), f32),
            pltpu.VMEM((164 * M, C), bf16),
            pltpu.VMEM((108 * M, C), bf16),
            pltpu.VMEM((108 * M, C), f32),
            pltpu.VMEM((108 * M, C), f32),
            pltpu.VMEM((108 * M, 128), f32),
            pltpu.VMEM((108 * M, 128), bf16),
            pltpu.VMEM((112 * M, C), bf16),
            pltpu.VMEM((54 * M, C), f32),
            pltpu.VMEM((64, C), f32),
            pltpu.VMEM((264, 128), f32),
            pltpu.VMEM((M, C), f32),
        ],
        1, 10, True,
    )(info, n2, n1, win, s1, s2, all_seeds, w_in, w_mid, w_out, w_noise)
    total = sum_all(g)
    o_in, o_mid, o_out, o_noise, o_loss = call(
        final_kernel,
        [((9, V, C), f32), ((9, C, C), f32), ((V, C), f32), ((NB, C), f32), ((1, 128), f32)],
        [], 0, 1,
    )(total)
    return o_in, o_mid, o_out, o_noise, o_loss[0, 0]


def solution(mesh):
    fine = Mesh(mesh.devices.reshape(8, 2, 4, 2, 2), AX)
    lat = ("y", "c")
    placed = (
        P(None, lat, "xh"), P(None, lat, "xh"), P(lat, "xh"), P(("z", "xl"), None),
        P(), P(), P(), P(),
    )
    return jax.shard_map(
        body, mesh=fine, in_specs=placed, out_specs=(P(), P(), P(), P(), P()), check_vma=False
    )
```

time: 412 us -> 165 us (0.40)
  waiting for transfers between devices: 206 us -> 33.2 us
  Pallas kernels: 0 us -> 26.8 us
  local copies, waits for them, and re-layouts: 30.9 us -> 5.51 us
  blocking collectives: 76.7 us -> 53.2 us
  other arithmetic: 28.4 us -> 7.66 us
  matrix products: 19.7 us -> 0 us
  between operations: 19.6 us -> 0.82 us
  starting transfers between devices: 25.3 us -> 35.6 us
    psum x1 -> x0, waiting for transfers between devices: 181 us -> none  [body(): lax.psum((grad_in, grad_mid, grad_out, grad_noise, loss_term), ('member',...]
    psum x1 -> x0, blocking collectives: 76.7 us -> none  [body(): lax.psum((grad_in, grad_mid, grad_out, grad_noise, loss_term), ('member',...]
    all_to_all x0 -> x2, blocking collectives: none -> 53.2 us  [the longest x1 29.2 us: sum_all(): s = lax.all_to_all(s, xy, 0, 0, tiled=True).sum(0)]
    pallas_call x0 -> x4, Pallas kernels: none -> 26.8 us  [the longest x1 18.3 us: body(): call(main_kernel, [((NB, BR, C), f32)], [pltpu.VMEM((264, 128), f32), plt...]
    ppermute x8 -> x17, starting transfers between devices: 11.2 us -> 35.6 us  [send(): return lax.ppermute(v, AX, perm(f))]
    dot_general x49 -> x0, matrix products: 19.7 us -> none  [the longest x18 9.7 us: conv_forward(): lax.dot_general(weights[offset], window, (((0,), (0,)), ((), ())), prefer...]
    ppermute x8 -> x17, waiting for transfers between devices: 17.5 us -> 33.2 us  [send(): return lax.ppermute(v, AX, perm(f))]
    all_to_all x2 -> x0, starting transfers between devices: 14 us -> none  [the longest x1 8.93 us: body(): lax.all_to_all(output[None], 'member', split_axis=2, concat_axis=0, tiled...]
  transfers between devices with their start and end apart: 11 -> 17, of which waited for: 10 -> 10; matrix products, arithmetic and copies ran while one was open for 4% -> 2% of each run, Pallas kernels for 0% -> 1%
where the time goes in v1:
time: 165 us; the launch traced here: 163 us
  blocking collectives  53.2 us (32%)
  starting transfers between devices  35.6 us (22%)
  waiting for transfers between devices  33.2 us (20%)
  Pallas kernels  26.8 us (16%)
  other arithmetic  7.66 us (5%)
  local copies, waits for them, and re-layouts  5.51 us (3%)
    ppermute x17, starting transfers between devices, send(): return lax.ppermute(v, AX, perm(f))  35.6 us
    ppermute x17, waiting for transfers between devices, send(): return lax.ppermute(v, AX, perm(f))  33.2 us
    all_to_all x1, blocking collectives, sum_all(): s = lax.all_to_all(s, xy, 0, 0, tiled=True).sum(0)  29.2 us
    all_to_all x1, blocking collectives, sum_all(): lax.all_to_all(jnp.broadcast_to(s[None], (16,) + s.shape), xy, 0, 0, tile...  24 us
    pallas_call x1, Pallas kernels, body(): call(main_kernel, [((NB, BR, C), f32)], [pltpu.VMEM((264, 128), f32), plt...  18.3 us
    pallas_call x1, Pallas kernels, body(): call(final_kernel, [((9, V, C), f32), ((9, C, C), f32), ((V, C), f32), ((...  4.35 us
  transfers between devices with their start and end apart: 17, of which 10 were waited for; matrix products, arithmetic and copies ran while one was open for 2% of the time, Pallas kernels for 1%

profile of v1, /device:TPU:33, one launch (start us, length us, event | category | flops | bytes accessed | tf_op | source)
XLA Modules:
  0.0 162.8 jit_solution(2275771311113615087)
XLA Ops:
  0.6 1.3 collective-permute-start.5
  1.9 1.4 collective-permute-start.7
  3.4 2.3 %shard_map.119 = (f32[2,384,256]{2,1,0:T(8,128)}, f32[2,8,256]{2,1,0:T(8,128)}) custom-call(bf16[100,2,360]{2,1,0:T(2,128)(2,1)} %state.1, bf16[100,2,360]{2,1,0:T(2,128)(2,1)} %target.1, s32[2,360]{1,0:T(2,128)} %land.1), custom_call_target="tpu_custom_call" | custom-call | tf_op jit(solution)/shard_map/pallas_call | solution.py:420
  5.7 2.7 %collective-permute-start = (f32[2,8,256]{2,1,0:T(8,128)}, f32[2,8,256]{2,1,0:T(8,128)S(1)}, u32[]{:S(2)}, u32[]{:S(2)}) collective-permute-start(f32[2,8,256]{2,1,0:T(8,128)} %get-tuple-element.13), channel_id=1, source_target_pairs={{0,1},{1,0},{2,3},{3,2},{4,5},{5,4},{6,7},{7,6},{8,9},{9,8},{10,11... | collective-permute-start | bytes 49160 | tf_op jit(solution)/shard_map/ppermute | solution.py:39
  8.5 0.0 collective-permute-done.6
  8.5 0.7 pad_add_fusion
  9.2 5.1 %collective-permute-start.10 = (s32[4,32]{1,0:T(4,128)S(1)}, s32[4,32]{1,0:T(4,128)S(1)}, u32[]{:S(2)}, u32[]{:S(2)}) collective-permute-start(s32[4,32]{1,0:T(4,128)S(1)} %pad_add_fusion), channel_id=1, source_target_pairs={{0,192},{1,193},{2,194},{3,195},{4,196},{5,197},{6,198},{7,199},{8... | collective-permute-start | bytes 1544 | tf_op jit(solution)/shard_map/ppermute | solution.py:39
  14.3 1.2 collective-permute-start.8
  15.5 1.0 collective-permute-start.9
  16.5 0.6 pad_add_fusion.1.info
  17.0 0.6 collective-permute-done.8
  17.6 4.2 %collective-permute-done.9 = s32[4,32]{1,0:T(4,128)S(1)} collective-permute-done((s32[4,32]{1,0:T(4,128)S(1)}, s32[4,32]{1,0:T(4,128)S(1)}, u32[]{:S(2)}, u32[]{:S(2)}) %collective-permute-start.9) | collective-permute-done | bytes 544 | tf_op jit(solution)/shard_map/ppermute | solution.py:39
  21.8 0.7 concatenate.11
  22.5 0.6 gather_fusion
  23.1 0.0 copy-start.4
  23.1 0.6 copy-done.4
  23.7 1.8 %shard_map.120.own = bf16[2,32,256]{2,1,0:T(8,128)(2,1)} custom-call(s32[4]{0:T(128)} %pad_add_fusion.1.info, f32[2,384,256]{2,1,0:T(8,128)} %get-tuple-element.12.x, f32[2,8,256]{2,1,0:T(8,128)} %copy-done.4), custom_call_target="tpu_custom_call" | custom-call | tf_op jit(solution)/shard_map/pallas_call | solution.py:425
  25.5 3.2 %collective-permute-start.1 = (bf16[2,32,256]{2,1,0:T(8,128)(2,1)}, bf16[2,32,256]{2,1,0:T(8,128)(2,1)S(1)}, u32[]{:S(2)}, u32[]{:S(2)}) collective-permute-start(bf16[2,32,256]{2,1,0:T(8,128)(2,1)} %shard_map.120.own), channel_id=1, source_target_pairs={{0,4},{1,5},{2,6},{3,7},{4,8},{5,9},{6,10},{7,11},{8,12},{9,13},{1... | collective-permute-start | bytes 98312 | tf_op jit(solution)/shard_map/ppermute | solution.py:39
  28.7 6.9 %collective-permute-start.2 = (bf16[2,32,256]{2,1,0:T(8,128)(2,1)}, bf16[2,32,256]{2,1,0:T(8,128)(2,1)S(1)}, u32[]{:S(2)}, u32[]{:S(2)}) collective-permute-start(bf16[2,32,256]{2,1,0:T(8,128)(2,1)} %shard_map.120.own), channel_id=1, source_target_pairs={{0,2},{1,3},{2,4},{3,5},{4,6},{5,7},{6,8},{7,9},{8,10},{9,11},{10,... | collective-permute-start | bytes 98312 | tf_op jit(solution)/shard_map/ppermute | solution.py:39
  35.6 1.9 %collective-permute-start.3 = (bf16[2,32,256]{2,1,0:T(8,128)(2,1)}, bf16[2,32,256]{2,1,0:T(8,128)(2,1)S(1)}, u32[]{:S(2)}, u32[]{:S(2)}) collective-permute-start(bf16[2,32,256]{2,1,0:T(8,128)(2,1)} %shard_map.120.own), channel_id=1, source_target_pairs={{2,0},{3,1},{4,2},{5,3},{6,4},{7,5},{8,6},{9,7},{10,8},{11,9},{12,... | collective-permute-start | bytes 98312 | tf_op jit(solution)/shard_map/ppermute | solution.py:39
  37.5 1.3 collective-permute-start.4
  38.8 0.7 broadcast_select_fusion.2.seeds
  39.5 0.0 copy-start.1
  39.5 1.5 collective-permute-done.3.s1
  41.0 1.4 collective-permute-done.4.s2
  42.4 0.6 copy-done.3
  43.0 18.3 %shard_map.121 = f32[32,112,256]{2,1,0:T(8,128)} custom-call(s32[4]{0:T(128)} %pad_add_fusion.1.info, bf16[2,32,256]{2,1,0:T(8,128)(2,1)} %copy-done, bf16[2,32,256]{2,1,0:T(8,128)(2,1)} %copy-done.1, bf16[2,32,256]{2,1,0:T(8,128)(2,1)} %shard_map.120.own, bf16[2,32,256]{2,1,0:T(8,128)(2,1)} %copy-done.2, bf16[2,32,256]{2,1,0:T(8,128)(2,1)} %copy-done.3, ...), custom_call_target="tpu_custom_call" | custom-call | tf_op jit(solution)/shard_map/pallas_call | solution.py:430
  61.3 2.9 %dynamic-slice_bitcast_fusion = f32[16,112,256]{2,1,0:T(8,128)} fusion(f32[2,16,112,256]{3,2,1,0:T(8,128)} %bitcast.13, s32[]{:T(128)S(6)} %select_n.57), kind=kLoop, calls=%fused_computation.3 | loop fusion | bytes 3670020 | tf_op jit(solution)/shard_map/jit(dynamic_index_in_dim)/squeeze | solution.py:381
  64.2 1.3 collective-permute-start.11
  65.5 3.6 %collective-permute-done.11 = f32[16,112,256]{2,1,0:T(8,128)S(1)} collective-permute-done((f32[16,112,256]{2,1,0:T(8,128)}, f32[16,112,256]{2,1,0:T(8,128)S(1)}, u32[]{:S(2)}, u32[]{:S(2)}) %collective-permute-start.11) | collective-permute-done | bytes 1835040 | tf_op jit(solution)/shard_map/ppermute | solution.py:39
  69.1 1.7 %bitcast_add_fusion = f32[16,112,256]{2,1,0:T(8,128)S(1)} fusion(f32[16,112,256]{2,1,0:T(8,128)S(1)} %collective-permute-done.11, f32[2,16,112,256]{3,2,1,0:T(8,128)} %bitcast.14, s32[]{:T(128)S(6)} %select_n.56), kind=kLoop, calls=%fused_computation.2 | loop fusion | flops 458752 | bytes 5505028 | tf_op jit(solution)/shard_map/add | solution.py:383
  70.8 29.2 %all_to_all.10 = f32[16,112,256]{2,1,0:T(8,128)S(1)} all-to-all(f32[16,112,256]{2,1,0:T(8,128)S(1)} %bitcast_add_fusion), channel_id=1, replica_groups=mesh['z'=8,'xl'=2,'y'=4,'c'=2,'xh'=2] {'xl','y','xh'}, dimensions={0} | all-to-all | bytes 3670016 | tf_op jit(solution)/shard_map/all_to_all | solution.py:384
  100.1 0.1 reduce_sum.9
  100.2 0.8 collective-permute-start.12
  101.0 1.2 collective-permute-start.13
  102.2 0.7 collective-permute-start.14
  102.9 1.0 collective-permute-done.12
  103.9 1.8 %collective-permute-done.13 = f32[112,256]{1,0:T(8,128)S(1)} collective-permute-done((f32[112,256]{1,0:T(8,128)S(1)}, f32[112,256]{1,0:T(8,128)S(1)}, u32[]{:S(2)}, u32[]{:S(2)}) %collective-permute-start.13) | collective-permute-done | bytes 114720 | tf_op jit(solution)/shard_map/ppermute | solution.py:39
  105.7 8.0 %collective-permute-done.14 = f32[112,256]{1,0:T(8,128)S(1)} collective-permute-done((f32[112,256]{1,0:T(8,128)S(1)}, f32[112,256]{1,0:T(8,128)S(1)}, u32[]{:S(2)}, u32[]{:S(2)}) %collective-permute-start.14) | collective-permute-done | bytes 114720 | tf_op jit(solution)/shard_map/ppermute | solution.py:39
  113.7 0.1 collective-permute-start.15
  113.8 7.5 %collective-permute-done.15 = f32[112,256]{1,0:T(8,128)S(1)} collective-permute-done((f32[112,256]{1,0:T(8,128)S(1)}, f32[112,256]{1,0:T(8,128)S(1)}, u32[]{:S(2)}, u32[]{:S(2)}) %collective-permute-start.15) | collective-permute-done | bytes 114720 | tf_op jit(solution)/shard_map/ppermute | solution.py:39
  121.4 0.2 broadcast_in_dim.18
  121.6 24.0 %all_to_all.11 = f32[16,112,256]{2,1,0:T(8,128)S(1)} all-to-all(f32[16,112,256]{2,1,0:T(8,128)S(1)} %broadcast_in_dim.18), channel_id=1, replica_groups=mesh['z'=8,'xl'=2,'y'=4,'c'=2,'xh'=2] {'xl','y','xh'}, dimensions={0} | all-to-all | bytes 3670016 | tf_op jit(solution)/shard_map/all_to_all | solution.py:390
  145.6 5.5 %collective-permute-start.16 = (f32[16,112,256]{2,1,0:T(8,128)S(1)}, f32[16,112,256]{2,1,0:T(8,128)}, u32[]{:S(2)}, u32[]{:S(2)}) collective-permute-start(f32[16,112,256]{2,1,0:T(8,128)S(1)} %all_to_all.11), channel_id=1, source_target_pairs={{0,2},{1,3},{2,0},{3,1},{4,6},{5,7},{6,4},{7,5},{8,10},{9,11},{10,... | collective-permute-start | bytes 5505032 | tf_op jit(solution)/shard_map/ppermute | solution.py:39
  151.0 3.5 %collective-permute-done.16 = f32[16,112,256]{2,1,0:T(8,128)} collective-permute-done((f32[16,112,256]{2,1,0:T(8,128)S(1)}, f32[16,112,256]{2,1,0:T(8,128)}, u32[]{:S(2)}, u32[]{:S(2)}) %collective-permute-start.16) | collective-permute-done | bytes 1835040 | tf_op jit(solution)/shard_map/ppermute | solution.py:39
  154.6 1.8 %broadcast_select_fusion.1 = (f32[16,112,256]{2,1,0:T(8,128)S(1)}, f32[16,112,256]{2,1,0:T(8,128)S(1)}) fusion(f32[16,112,256]{2,1,0:T(8,128)S(1)} %all_to_all.11, f32[16,112,256]{2,1,0:T(8,128)} %collective-permute-done.16, pred[]{:T(512)S(6)} %eq.6), kind=kLoop, calls=%fused_computation.5 | loop fusion | flops 917504 | bytes 7340033 | tf_op jit(solution)/shard_map/jit(_where)/select_n | solution.py:392
  156.4 2.1 %pad_maximum_fusion.t = f32[32,112,256]{2,1,0:T(8,128)} fusion(f32[16,112,256]{2,1,0:T(8,128)S(1)} %get-tuple-element.20, f32[16,112,256]{2,1,0:T(8,128)S(1)} %get-tuple-element.19), kind=kLoop, calls=%fused_computation.1 | loop fusion | flops 917504 | bytes 7340032 | tf_op jit(solution)/shard_map/concatenate | solution.py:394
  158.4 4.4 %shard_map.122 = (f32[9,100,256]{2,1,0:T(8,128)}, f32[9,256,256]{2,1,0:T(8,128)}, f32[100,256]{1,0:T(8,128)}, f32[32,256]{1,0:T(8,128)}, f32[1,128]{1,0:T(1,128)}) custom-call(f32[32,112,256]{2,1,0:T(8,128)} %pad_maximum_fusion.t), custom_call_target="tpu_custom_call" | custom-call | tf_op jit(solution)/shard_map/pallas_call | solution.py:452
  (18 shorter events, 0.1 us)
Async XLA Ops:
  0.6 7.9 %collective-permute-start.5 = (s32[1,32]{1,0:T(1,128)}, s32[1,32]{1,0:T(1,128)S(1)}, u32[]{:S(2)}, u32[]{:S(2)}) collective-permute-start(s32[1,32]{1,0:T(1,128)} %param.11), channel_id=1, source_target_pairs={{0,16},{1,17},{2,18},{3,19},{4,20},{5,21},{6,22},{7,23},{8,24},{9,... | collective-permute-start | bytes 392 | tf_op jit(solution)/shard_map/ppermute | solution.py:39
  1.9 6.6 %collective-permute-start.6 = (s32[1,32]{1,0:T(1,128)}, s32[1,32]{1,0:T(1,128)S(1)}, u32[]{:S(2)}, u32[]{:S(2)}) collective-permute-start(s32[1,32]{1,0:T(1,128)} %param.11), channel_id=1, source_target_pairs={{0,32},{1,33},{2,34},{3,35},{4,36},{5,37},{6,38},{7,39},{8,40},{9,... | collective-permute-start | bytes 392 | tf_op jit(solution)/shard_map/ppermute | solution.py:39
  1.9 6.6 %collective-permute-start.7 = (s32[1,32]{1,0:T(1,128)}, s32[1,32]{1,0:T(1,128)S(1)}, u32[]{:S(2)}, u32[]{:S(2)}) collective-permute-start(s32[1,32]{1,0:T(1,128)} %param.11), channel_id=1, source_target_pairs={{0,48},{1,49},{2,50},{3,51},{4,52},{5,53},{6,54},{7,55},{8,56},{9,... | collective-permute-start | bytes 392 | tf_op jit(solution)/shard_map/ppermute | solution.py:39
  5.7 17.4 %collective-permute-start = (f32[2,8,256]{2,1,0:T(8,128)}, f32[2,8,256]{2,1,0:T(8,128)S(1)}, u32[]{:S(2)}, u32[]{:S(2)}) collective-permute-start(f32[2,8,256]{2,1,0:T(8,128)} %get-tuple-element.13), channel_id=1, source_target_pairs={{0,1},{1,0},{2,3},{3,2},{4,5},{5,4},{6,7},{7,6},{8,9},{9,8},{10,11... | collective-permute-start | bytes 49160 | tf_op jit(solution)/shard_map/ppermute | solution.py:39
  9.2 7.9 %collective-permute-start.10 = (s32[4,32]{1,0:T(4,128)S(1)}, s32[4,32]{1,0:T(4,128)S(1)}, u32[]{:S(2)}, u32[]{:S(2)}) collective-permute-start(s32[4,32]{1,0:T(4,128)S(1)} %pad_add_fusion), channel_id=1, source_target_pairs={{0,192},{1,193},{2,194},{3,195},{4,196},{5,197},{6,198},{7,199},{8... | collective-permute-start | bytes 1544 | tf_op jit(solution)/shard_map/ppermute | solution.py:39
  14.3 3.3 %collective-permute-start.8 = (s32[4,32]{1,0:T(4,128)S(1)}, s32[4,32]{1,0:T(4,128)S(1)}, u32[]{:S(2)}, u32[]{:S(2)}) collective-permute-start(s32[4,32]{1,0:T(4,128)S(1)} %pad_add_fusion), channel_id=1, source_target_pairs={{0,64},{1,65},{2,66},{3,67},{4,68},{5,69},{6,70},{7,71},{8,72},{9,... | collective-permute-start | bytes 1544 | tf_op jit(solution)/shard_map/ppermute | solution.py:39
  15.5 6.3 %collective-permute-start.9 = (s32[4,32]{1,0:T(4,128)S(1)}, s32[4,32]{1,0:T(4,128)S(1)}, u32[]{:S(2)}, u32[]{:S(2)}) collective-permute-start(s32[4,32]{1,0:T(4,128)S(1)} %pad_add_fusion), channel_id=1, source_target_pairs={{0,128},{1,129},{2,130},{3,131},{4,132},{5,133},{6,134},{7,135},{8... | collective-permute-start | bytes 1544 | tf_op jit(solution)/shard_map/ppermute | solution.py:39
  23.1 0.6 copy-start.4
  25.5 14.0 %collective-permute-start.1 = (bf16[2,32,256]{2,1,0:T(8,128)(2,1)}, bf16[2,32,256]{2,1,0:T(8,128)(2,1)S(1)}, u32[]{:S(2)}, u32[]{:S(2)}) collective-permute-start(bf16[2,32,256]{2,1,0:T(8,128)(2,1)} %shard_map.120.own), channel_id=1, source_target_pairs={{0,4},{1,5},{2,6},{3,7},{4,8},{5,9},{6,10},{7,11},{8,12},{9,13},{1... | collective-permute-start | bytes 98312 | tf_op jit(solution)/shard_map/ppermute | solution.py:39
  28.7 10.8 %collective-permute-start.2 = (bf16[2,32,256]{2,1,0:T(8,128)(2,1)}, bf16[2,32,256]{2,1,0:T(8,128)(2,1)S(1)}, u32[]{:S(2)}, u32[]{:S(2)}) collective-permute-start(bf16[2,32,256]{2,1,0:T(8,128)(2,1)} %shard_map.120.own), channel_id=1, source_target_pairs={{0,2},{1,3},{2,4},{3,5},{4,6},{5,7},{6,8},{7,9},{8,10},{9,11},{10,... | collective-permute-start | bytes 98312 | tf_op jit(solution)/shard_map/ppermute | solution.py:39
  35.6 5.4 %collective-permute-start.3 = (bf16[2,32,256]{2,1,0:T(8,128)(2,1)}, bf16[2,32,256]{2,1,0:T(8,128)(2,1)S(1)}, u32[]{:S(2)}, u32[]{:S(2)}) collective-permute-start(bf16[2,32,256]{2,1,0:T(8,128)(2,1)} %shard_map.120.own), channel_id=1, source_target_pairs={{2,0},{3,1},{4,2},{5,3},{6,4},{7,5},{8,6},{9,7},{10,8},{11,9},{12,... | collective-permute-start | bytes 98312 | tf_op jit(solution)/shard_map/ppermute | solution.py:39
  37.5 4.9 %collective-permute-start.4 = (bf16[2,32,256]{2,1,0:T(8,128)(2,1)}, bf16[2,32,256]{2,1,0:T(8,128)(2,1)S(1)}, u32[]{:S(2)}, u32[]{:S(2)}) collective-permute-start(bf16[2,32,256]{2,1,0:T(8,128)(2,1)} %shard_map.120.own), channel_id=1, source_target_pairs={{4,0},{5,1},{6,2},{7,3},{8,4},{9,5},{10,6},{11,7},{12,8},{13,9},{1... | collective-permute-start | bytes 98312 | tf_op jit(solution)/shard_map/ppermute | solution.py:39
  39.5 2.9 %copy-start = (bf16[2,32,256]{2,1,0:T(8,128)(2,1)}, bf16[2,32,256]{2,1,0:T(8,128)(2,1)S(1)}, u32[]{:S(2)}) copy-start(bf16[2,32,256]{2,1,0:T(8,128)(2,1)S(1)} %collective-permute-done.1.n2) | copy-start | bytes 98308
  39.5 2.9 %copy-start.1 = (bf16[2,32,256]{2,1,0:T(8,128)(2,1)}, bf16[2,32,256]{2,1,0:T(8,128)(2,1)S(1)}, u32[]{:S(2)}) copy-start(bf16[2,32,256]{2,1,0:T(8,128)(2,1)S(1)} %collective-permute-done.2.n1) | copy-start | bytes 98308
  41.0 1.4 copy-start.2
  42.4 0.6 copy-start.3
  64.2 4.9 %collective-permute-start.11 = (f32[16,112,256]{2,1,0:T(8,128)}, f32[16,112,256]{2,1,0:T(8,128)S(1)}, u32[]{:S(2)}, u32[]{:S(2)}) collective-permute-start(f32[16,112,256]{2,1,0:T(8,128)} %dynamic-slice_bitcast_fusion), channel_id=1, source_target_pairs={{0,2},{1,3},{2,0},{3,1},{4,6},{5,7},{6,4},{7,5},{8,10},{9,11},{10,... | collective-permute-start | bytes 5505032 | tf_op jit(solution)/shard_map/ppermute | solution.py:39
  100.2 3.7 %collective-permute-start.12 = (f32[112,256]{1,0:T(8,128)S(1)}, f32[112,256]{1,0:T(8,128)S(1)}, u32[]{:S(2)}, u32[]{:S(2)}) collective-permute-start(f32[112,256]{1,0:T(8,128)S(1)} %reduce_sum.9), channel_id=1, source_target_pairs={{0,32},{1,33},{2,34},{3,35},{4,36},{5,37},{6,38},{7,39},{8,40},{9,... | collective-permute-start | bytes 344072 | tf_op jit(solution)/shard_map/ppermute | solution.py:39
  101.0 4.7 %collective-permute-start.13 = (f32[112,256]{1,0:T(8,128)S(1)}, f32[112,256]{1,0:T(8,128)S(1)}, u32[]{:S(2)}, u32[]{:S(2)}) collective-permute-start(f32[112,256]{1,0:T(8,128)S(1)} %reduce_sum.9), channel_id=1, source_target_pairs={{0,64},{1,65},{2,66},{3,67},{4,68},{5,69},{6,70},{7,71},{8,72},{9,... | collective-permute-start | bytes 344072 | tf_op jit(solution)/shard_map/ppermute | solution.py:39
  102.2 11.5 %collective-permute-start.14 = (f32[112,256]{1,0:T(8,128)S(1)}, f32[112,256]{1,0:T(8,128)S(1)}, u32[]{:S(2)}, u32[]{:S(2)}) collective-permute-start(f32[112,256]{1,0:T(8,128)S(1)} %reduce_sum.9), channel_id=1, source_target_pairs={{0,96},{1,97},{2,98},{3,99},{4,100},{5,101},{6,102},{7,103},{8,104... | collective-permute-start | bytes 344072 | tf_op jit(solution)/shard_map/ppermute | solution.py:39
  113.7 7.6 %collective-permute-start.15 = (f32[112,256]{1,0:T(8,128)S(1)}, f32[112,256]{1,0:T(8,128)S(1)}, u32[]{:S(2)}, u32[]{:S(2)}) collective-permute-start(f32[112,256]{1,0:T(8,128)S(1)} %add_add_fusion), channel_id=1, source_target_pairs={{0,128},{1,129},{2,130},{3,131},{4,132},{5,133},{6,134},{7,135},{8... | collective-permute-start | bytes 344072 | tf_op jit(solution)/shard_map/ppermute | solution.py:39
  145.6 9.0 %collective-permute-start.16 = (f32[16,112,256]{2,1,0:T(8,128)S(1)}, f32[16,112,256]{2,1,0:T(8,128)}, u32[]{:S(2)}, u32[]{:S(2)}) collective-permute-start(f32[16,112,256]{2,1,0:T(8,128)S(1)} %all_to_all.11), channel_id=1, source_target_pairs={{0,2},{1,3},{2,0},{3,1},{4,6},{5,7},{6,4},{7,5},{8,10},{9,11},{10,... | collective-permute-start | bytes 5505032 | tf_op jit(solution)/shard_map/ppermute | solution.py:39

commit v2 on v1

--- a/solution.py
+++ b/solution.py
@@ -23,14 +23,11 @@
 VMEM = 56 * 1024 * 1024
 
 
-def perm(f, keep=None):
+def perm(f):
     out = []
     for i in range(256):
         z, xl, lat, xh = i >> 5, (i >> 4) & 1, (i >> 1) & 7, i & 1
-        t = f(z, xl, lat, xh)
-        if t is None:
-            continue
-        z2, xl2, lat2, xh2 = t
+        z2, xl2, lat2, xh2 = f(z, xl, lat, xh)
         out.append((i, (z2 % 8) * 32 + xl2 * 16 + lat2 * 2 + xh2))
     return out
 
@@ -41,7 +38,7 @@
 
 def lat_shift(v, d):
     def f(z, xl, lat, xh):
-        return (z, xl, lat + d, xh) if 0 <= lat + d < 8 else None
+        return (z, xl, (lat + d) % 8, xh)
 
     return send(v, f)
 
@@ -71,43 +68,63 @@
     sc[...] = jnp.zeros(sc.shape, f32)
     edge_out[...] = jnp.zeros(edge_out.shape, f32)
     for r in range(2):
+        x_out[r, 0:8, :] = jnp.zeros((8, 256), f32)
+        x_out[r, 8 + TC : 384, :] = jnp.zeros((376 - TC, 256), f32)
         sc[0:V, 0:TC] = state[:, r, :].astype(f32)
         sc[104:105, 0:TC] = 1.0 + land[r : r + 1, :].astype(f32)
-        x_out[r, :, 0:128] = sc[...].T
+        x_out[r, 8 : 8 + TC, 0:128] = sc[...].T[0:TC]
         sc[0:V, 0:TC] = target[:, r, :].astype(f32)
-        x_out[r, :, 128:256] = sc[...].T
-        edge_out[r, 0:3, :] = x_out[r, TC - 3 : TC, :]
-        edge_out[r, 3:6, :] = x_out[r, 0:3, :]
-
-
-def window_kernel(info, x, edge, win, ws):
+        x_out[r, 8 : 8 + TC, 128:256] = sc[...].T[0:TC]
+        edge_out[r, 0:3, :] = x_out[r, TC + 5 : TC + 8, :]
+        edge_out[r, 10:13, :] = x_out[r, 8:11, :]
+
+
+def window_kernel(info, x, edge, sd0, sd1, sd2, sd3, win):
+    m = info[0]
     start = info[1]
+    row = lax.broadcasted_iota(jnp.int32, (16, 256), 0)
+    low = (row < 3) & (m == 0)
+    high = (row >= 10) & (row < 13) & (m == M - 1)
     for r in range(2):
-        ws[r, 8 : 8 + TC, :] = x[r, 0:TC, :]
-        ws[r, 5:8, :] = edge[r, 0:3, :]
-        ws[r, 8 + TC : 11 + TC, :] = edge[r, 3:6, :]
-        ws[r, 11 + TC : 16 + TC, :] = jnp.zeros((5, 256), f32)
         base = pl.multiple_of(((start + 5) // 8) * 8, 8)
-        near = ws[r, pl.ds(base, WP + 8), :]
-        win[r, :, :] = pltpu.roll(near, WP + 8 - (start + 5 - base), 0)[0:WP].astype(bf16)
+        near = x[r, pl.ds(base, WP + 8), :]
+        w = pltpu.roll(near, WP + 8 - (start + 5 - base), 0)[0:WP]
+        e = edge[r]
+        win[WP * r : WP * r + 16, :] = jnp.where(low, e, w[0:16]).astype(bf16)
+        win[WP * r + 16 : WP * r + 32, :] = jnp.where(high, e, w[16:32]).astype(bf16)
+    win[2 * WP : 2 * WP + 16, :] = jnp.zeros((16, 256), bf16)
+    pad = jnp.zeros((12, 32), jnp.int32)
+    sd = jnp.concatenate([sd0[...], sd1[...], sd2[...], sd3[...], pad], axis=0)
+    win[2 * WP : 2 * WP + 16, 0:32] = (sd >> 8).astype(f32).astype(bf16)
+    win[2 * WP : 2 * WP + 16, 128:160] = (sd & 255).astype(f32).astype(bf16)
 
 
 def main_kernel(
-    info, n2, n1, own, s1, s2, seeds, w_in, w_mid, w_out, w_noise, g_out,
-    S, T, SB, PB, HID, HO, SL, UP, OUT, DO, DM, INC, DS, QB, BIAS,
+    info, n2, n1, own, s1, s2, w_in, w_mid, w_out, w_noise, mine_out, theirs_out,
+    S, T, SB, PB, HID, HO, SL, UP, OUT, DO, DM, INC, DS, QB, BIAS, SD, LT,
 ):
     own22 = info[2]
     lat = info[3]
-    rows = (n2[1], n1[0], n1[1], own[0], own[1], s1[0], s1[1], s2[0])
-    for k, row in enumerate(rows):
-        S[32 * k : 32 * k + 32, :] = row[:, 0:128].astype(f32)
-        T[32 * k : 32 * k + 32, :] = row[:, 128:256].astype(f32)
+    core = info[4]
+    rows = ((n2, 1, -2), (n1, 0, -1), (n1, 1, -1), (own, 0, 0), (own, 1, 0),
+            (s1, 0, 1), (s1, 1, 1), (s2, 0, 2))
+    for k, (ref, r, d) in enumerate(rows):
+        inside = (lat + d >= 0) & (lat + d < 8)
+        row = ref[WP * r : WP * r + WP, :].astype(f32) * jnp.where(inside, 1.0, 0.0)
+        S[WP * k : WP * k + WP, :] = row[:, 0:128]
+        T[WP * k : WP * k + WP, :] = row[:, 128:256]
     S[256:264, :] = jnp.zeros((8, 128), f32)
     T[256:264, :] = jnp.zeros((8, 128), f32)
     QB[...] = jnp.broadcast_to(S[:, 104:105], QB.shape)
     for b in range(3):
         SB[b] = S[b : b + 256, :].astype(bf16)
-    latents = (seeds[...].astype(f32) - 32767.5) / 18918.0
+    for d, ref in ((-1, n1), (0, own), (1, s1), (2, s2)):
+        sd = ref[2 * WP : 2 * WP + 16, :].astype(f32)
+        group = pl.multiple_of(((lat + d + 8) & 3) * 8, 8)
+        SD[pl.ds(group, 8), :] = (sd[:, 0:128] * 256.0 + sd[:, 128:256])[0:8]
+    for k in range(4):
+        LT[4 * k : 4 * k + 4, :] = SD[8 * k : 8 * k + 4, :]
+    latents = (LT[:, 0:32] - 32767.5) / 18918.0
     BIAS[...] = jnp.dot(
         latents, w_noise[...], precision=lax.Precision.HIGHEST, preferred_element_type=f32
     )
@@ -250,15 +267,27 @@
 
         dsum = lax.fori_loop(0, 23, in_cell, dsum)
 
-    g_out[:, ROWS:BR, :] = jnp.zeros((NB, BR - ROWS, C), f32)
+    def store(k, lo, hi, value):
+        @pl.when(core == k // 16)
+        def _():
+            mine_out[k % 16, lo:hi, :] = value
+
+        @pl.when(core != k // 16)
+        def _():
+            theirs_out[k % 16, lo:hi, :] = value
+
+    mine_out[:, ROWS:BR, :] = jnp.zeros((16, BR - ROWS, C), f32)
+    theirs_out[:, ROWS:BR, :] = jnp.zeros((16, BR - ROWS, C), f32)
+    peaks = []
 
     def put(row, value):
         done = 0
         n = value.shape[0]
+        peaks.append(jnp.max(jnp.abs(value), axis=0, keepdims=True))
         while done < n:
             k, i = divmod(row + done, ROWS)
             take = min(n - done, ROWS - i)
-            g_out[k, i : i + take, :] = value[done : done + take, :]
+            store(k, i, i + take, value[done : done + take, :])
             done += take
 
     cell = lax.broadcasted_iota(jnp.int32, (NR, C), 0) >> 4
@@ -305,19 +334,35 @@
         latents, dsum, (((0,), (0,)), ((), ())),
         precision=lax.Precision.HIGHEST, preferred_element_type=f32,
     )
+    peaks.append(jnp.max(jnp.abs(gn), axis=0, keepdims=True))
     for k in range(NB):
-        g_out[k, ROWS : ROWS + 1, :] = gn[k : k + 1, :]
-    g_out[0, ROWS + 1 : ROWS + 2, :] = jnp.broadcast_to(loss, (1, C))
-
-
-def final_kernel(t, o_in, o_mid, o_out, o_noise, o_loss):
+        store(k, ROWS, ROWS + 1, gn[k : k + 1, :])
+    store(0, ROWS + 1, ROWS + 2, jnp.broadcast_to(loss, (1, C)))
+    peak = peaks[0]
+    for p in peaks[1:]:
+        peak = jnp.maximum(peak, p)
+    peak = jnp.max(peak, axis=1, keepdims=True)
+    lane = lax.broadcasted_iota(jnp.int32, (1, C), 1)
+    top = jnp.where(lane < 128, peak, jnp.abs(loss))
+    top = jnp.ceil(jnp.log(jnp.maximum(top, 1e-30)) * 1.4426950408889634)
+    for k in range(16):
+        mine_out[k, BR - 1 : BR, :] = top
+        theirs_out[k, BR - 1 : BR, :] = top
+
+
+def final_kernel(info, t, o_in, o_mid, o_out, o_noise, o_loss):
+    core = info[4]
+
+    def block(k):
+        return ((k // 16) ^ core) * 16 + k % 16
+
     def get(row, n):
         parts = []
         done = 0
         while done < n:
             k, i = divmod(row + done, ROWS)
             take = min(n - done, ROWS - i)
-            parts.append((done, take, t[k, i : i + take, :]))
+            parts.append((done, take, t[block(k), i : i + take, :]))
             done += take
         return parts
 
@@ -351,8 +396,8 @@
     def noise_store(done, take, v):
         o_noise[done : done + take, :] = v
 
-    norm([[(k, 1, t[k, ROWS : ROWS + 1, :]) for k in range(NB)]], NB * C, [noise_store])
-    o_loss[...] = t[0, ROWS + 1 : ROWS + 2, 0:128] * (1.0 / (V * 16 * 720))
+    norm([[(k, 1, t[block(k), ROWS : ROWS + 1, :]) for k in range(NB)]], NB * C, [noise_store])
+    o_loss[...] = t[block(0), ROWS + 1 : ROWS + 2, 0:128] * (1.0 / (V * 16 * 720))
 
 
 def call(kernel, outs, scratch, n_smem, n_in, single=False):
@@ -370,65 +415,85 @@
     )
 
 
-def sum_all(g):
+f16 = jnp.float16
+
+
+def decode(msg):
+    v = msg.astype(f32)
+    e = v[..., BR - 1 : BR, 0:1]
+    el = v[..., BR - 1 : BR, 128:129]
+    row = lax.broadcasted_iota(jnp.int32, v.shape, v.ndim - 2)
+    tail = lax.slice_in_dim(v, ROWS + 2, ROWS + 3, axis=v.ndim - 2) * (2.0**-11)
+    power = jnp.where(row == ROWS + 1, el, e) - 14.0
+    v = jnp.where(row == ROWS + 1, v + tail, v)
+    return jnp.where(row > ROWS + 1, 0.0, v * jnp.exp2(power)), e, el
+
+
+def encode(v, e, el):
+    row = lax.broadcasted_iota(jnp.int32, v.shape, v.ndim - 2)
+    lane = lax.broadcasted_iota(jnp.int32, v.shape, v.ndim - 1)
+    big = v * jnp.exp2(14.0 - jnp.where(row == ROWS + 1, el, e))
+    loss = lax.slice_in_dim(v, ROWS + 1, ROWS + 2, axis=v.ndim - 2) * jnp.exp2(14.0 - el)
+    rest = (loss - lax.reduce_precision(loss, 5, 10)) * (2.0**11)
+    big = jnp.where(row == ROWS + 2, rest, big)
+    big = jnp.where(row == BR - 1, jnp.where(lane < 128, e, el), big)
+    return big.astype(f16)
+
+
+def sum_all(mine, theirs):
     xy = ("xl", "y", "xh")
-    core = lax.axis_index("c")
 
     def other(z, xl, lat, xh):
         return (z, xl, lat ^ 1, xh)
 
-    g = g.reshape(2, 16, BR, C)
-    theirs = lax.dynamic_index_in_dim(g, 1 - core, 0, False)
-    mine = lax.dynamic_index_in_dim(g, core, 0, False)
-    s = mine + send(theirs, other)
-    s = lax.all_to_all(s, xy, 0, 0, tiled=True).sum(0)
-    r1 = send(s, lambda z, xl, lat, xh: (z ^ 1, xl, lat, xh))
-    r2 = send(s, lambda z, xl, lat, xh: (z ^ 2, xl, lat, xh))
-    r3 = send(s, lambda z, xl, lat, xh: (z ^ 3, xl, lat, xh))
-    s = (s + r1) + (r2 + r3)
-    s = s + send(s, lambda z, xl, lat, xh: (z ^ 4, xl, lat, xh))
-    half = lax.all_to_all(jnp.broadcast_to(s[None], (16,) + s.shape), xy, 0, 0, tiled=True)
+    e = mine[0:1, BR - 1 : BR, 0:1]
+    el = mine[0:1, BR - 1 : BR, 128:129]
+    got, e1, el1 = decode(send(encode(theirs, e, el), other))
+    s = jnp.where(lax.broadcasted_iota(jnp.int32, mine.shape, 1) > ROWS + 1, 0.0, mine) + got
+    e, el = jnp.maximum(e, e1[0:1]) + 1.0, jnp.maximum(el, el1[0:1]) + 1.0
+    got, e1, el1 = decode(lax.all_to_all(encode(s, e, el), xy, 0, 0, tiled=True))
+    s = got.sum(0)
+    e, el = jnp.max(e1, axis=0) + 4.0, jnp.max(el1, axis=0) + 4.0
+    msg = encode(s, e, el)
+    sets = [decode(msg)]
+    for k in (1, 2, 3):
+        sets.append(decode(send(msg, lambda z, xl, lat, xh, k=k: (z ^ k, xl, lat, xh))))
+    s = (sets[0][0] + sets[1][0]) + (sets[2][0] + sets[3][0])
+    e = jnp.maximum(jnp.maximum(sets[0][1], sets[1][1]), jnp.maximum(sets[2][1], sets[3][1])) + 2.0
+    el = jnp.maximum(jnp.maximum(sets[0][2], sets[1][2]), jnp.maximum(sets[2][2], sets[3][2])) + 2.0
+    msg = encode(s, e, el)
+    v0, e0, el0 = decode(msg)
+    v1, e1, el1 = decode(send(msg, lambda z, xl, lat, xh: (z ^ 4, xl, lat, xh)))
+    msg = encode(v0 + v1, jnp.maximum(e0, e1) + 1.0, jnp.maximum(el0, el1) + 1.0)
+    half = lax.all_to_all(jnp.broadcast_to(msg[None], (16,) + msg.shape), xy, 0, 0, tiled=True)
     far = send(half, other)
-    first = jnp.where(core == 0, half, far)
-    second = jnp.where(core == 0, far, half)
-    return jnp.concatenate([first, second], axis=0)
-
-
-def gather_seeds(seeds):
-    z = lax.axis_index("z")
-    xl = lax.axis_index("xl")
-
-    def spread(v, moves):
-        return [v] + [
-            send(v, lambda z, xl, lat, xh, d=d: (z ^ d[0], xl ^ d[1], lat, xh)) for d in moves
-        ]
-
-    near = jnp.concatenate(spread(seeds, ((0, 1), (1, 0), (1, 1))), axis=0)
-    parts = spread(near, ((2, 0), (4, 0), (6, 0)))
-    table = jnp.concatenate(parts, axis=0)
-    member = z * 2 + xl
-    order = jnp.bitwise_xor(jnp.arange(M, dtype=jnp.int32), member)
-    return jnp.take(table, order, axis=0)
+    return decode(jnp.concatenate([half, far], axis=0))[0]
 
 
 def body(state, target, land, seeds, w_in, w_mid, w_out, w_noise):
     z = lax.axis_index("z")
     xl = lax.axis_index("xl")
-    lat = lax.axis_index("y") * 2 + lax.axis_index("c")
+    core = lax.axis_index("c")
+    lat = lax.axis_index("y") * 2 + core
     member = z * 2 + xl
-    info = jnp.stack([member, (45 * member) // 2, member % 2, lat]).astype(jnp.int32)
+    info = jnp.stack([member, (45 * member) // 2, member % 2, lat, core]).astype(jnp.int32)
     x, edge = call(
-        prep_kernel, [((2, 384, 256), f32), ((2, 8, 256), f32)],
+        prep_kernel, [((2, 384, 256), f32), ((2, 16, 256), f32)],
         [pltpu.VMEM((128, 384), f32)], 0, 3,
     )(state, target, land)
+    edge, seeds = lax.optimization_barrier((edge, seeds))
     edge = send(edge, lambda z, xl, lat, xh: (z, xl, lat, xh ^ 1))
-    win = call(
-        window_kernel, [((2, WP, 256), bf16)], [pltpu.VMEM((2, 376, 256), f32)], 1, 2, True
-    )(info, x, edge)
+    near = [
+        send(
+            seeds,
+            lambda z, xl, lat, xh, k=k: (z ^ (2 * (lat % 4) + (k >> 1)), xl ^ (k & 1), lat, xh),
+        )
+        for k in range(4)
+    ]
+    win = call(window_kernel, [((80, 256), bf16)], [], 1, 6, True)(info, x, edge, *near)
     n2, n1, s1, s2 = (lat_shift(win, d) for d in (2, 1, -1, -2))
-    all_seeds = gather_seeds(seeds)
-    g = call(
-        main_kernel, [((NB, BR, C), f32)],
+    mine, theirs = call(
+        main_kernel, [((16, BR, C), f32), ((16, BR, C), f32)],
         [
             pltpu.VMEM((264, 128), f32),
             pltpu.VMEM((264, 128), f32),
@@ -445,15 +510,17 @@
             pltpu.VMEM((64, C), f32),
             pltpu.VMEM((264, 128), f32),
             pltpu.VMEM((M, C), f32),
+            pltpu.VMEM((32, 128), f32),
+            pltpu.VMEM((M, 128), f32),
         ],
-        1, 10, True,
-    )(info, n2, n1, win, s1, s2, all_seeds, w_in, w_mid, w_out, w_noise)
-    total = sum_all(g)
+        1, 9,
+    )(info, n2, n1, win, s1, s2, w_in, w_mid, w_out, w_noise)
+    total = sum_all(mine, theirs)
     o_in, o_mid, o_out, o_noise, o_loss = call(
         final_kernel,
         [((9, V, C), f32), ((9, C, C), f32), ((V, C), f32), ((NB, C), f32), ((1, 128), f32)],
-        [], 0, 1,
-    )(total)
+        [], 1, 1,
+    )(info, total)
     return o_in, o_mid, o_out, o_noise, o_loss[0, 0]
 
 

time: 165 us -> 165 us (level)
  blocking collectives: 53.2 us -> 31.9 us
  other arithmetic: 7.66 us -> 21.6 us
  waiting for transfers between devices: 33.2 us -> 19.6 us
  between operations: 0.82 us -> 13.5 us
  Pallas kernels: 26.8 us -> 32.8 us
  local copies, waits for them, and re-layouts: 5.51 us -> 7.4 us
    all_to_all x2, blocking collectives: 53.2 us -> 31.9 us  [the longest x1 17.1 us: sum_all(): lax.all_to_all(encode(s, e, el), xy, 0, 0, tiled=True)]
    ppermute x17 -> x15, waiting for transfers between devices: 33.2 us -> 19.6 us  [send(): return lax.ppermute(v, AX, perm(f))]
    exp2 x0 -> x11, other arithmetic: none -> 9 us  [the longest x6 7.66 us: decode(): return (jnp.where(row > ROWS + 1, 0.0, v * jnp.exp2(power)), e, el)]
    pallas_call x3, Pallas kernels: 22.4 us -> 28.5 us  [the longest x1 24.3 us: body(): call(main_kernel, [((16, BR, C), f32), ((16, BR, C), f32)], [pltpu.VMEM((...]
    slice x0 -> x10, local copies, waits for them, and re-layouts: none -> 5.46 us  [the longest x8 3.72 us: decode(): el = v[..., BR - 1:BR, 128:129]]
    convert_element_type x0 -> x12, other arithmetic: none -> 3.43 us  [the longest x3 2.37 us: encode(): return big.astype(f16)]
    squeeze x1 -> x0, local copies, waits for them, and re-layouts: 2.87 us -> none  [sum_all(): theirs = lax.dynamic_index_in_dim(g, 1 - core, 0, False)]
    concatenate x2 -> x0, other arithmetic: 2.73 us -> none  [the longest x1 2.06 us: sum_all(): return jnp.concatenate([first, second], axis=0)]
  transfers between devices with their start and end apart: 17 -> 15, of which waited for: 10 -> 8; matrix products, arithmetic and copies ran while one was open for 2% -> 3% of each run, Pallas kernels for 1% -> 0%
where the time goes in v2:
time: 165 us; the launch traced here: 162 us
  starting transfers between devices  34.9 us (21%)
  Pallas kernels  32.8 us (20%)
  blocking collectives  31.9 us (19%)
  other arithmetic  21.6 us (13%)
  waiting for transfers between devices  19.6 us (12%)
  between operations  13.5 us (8%)
  local copies, waits for them, and re-layouts  7.4 us (4%)
    ppermute x15, starting transfers between devices, send(): return lax.ppermute(v, AX, perm(f))  34.9 us
    pallas_call x1, Pallas kernels, body(): call(main_kernel, [((16, BR, C), f32), ((16, BR, C), f32)], [pltpu.VMEM((...  24.3 us
    ppermute x15, waiting for transfers between devices, send(): return lax.ppermute(v, AX, perm(f))  19.6 us
    all_to_all x1, blocking collectives, sum_all(): lax.all_to_all(encode(s, e, el), xy, 0, 0, tiled=True)  17.1 us
    all_to_all x1, blocking collectives, sum_all(): lax.all_to_all(jnp.broadcast_to(msg[None], (16,) + msg.shape), xy, 0, 0,...  14.7 us
    exp2 x6, other arithmetic, decode(): return (jnp.where(row > ROWS + 1, 0.0, v * jnp.exp2(power)), e, el)  7.66 us
    pallas_call x1, Pallas kernels, body(): call(final_kernel, [((9, V, C), f32), ((9, C, C), f32), ((V, C), f32), ((...  4.37 us
    select_n x1, other arithmetic, decode(): return (jnp.where(row > ROWS + 1, 0.0, v * jnp.exp2(power)), e, el)  3.86 us
  transfers between devices with their start and end apart: 15, of which 8 were waited for; matrix products, arithmetic and copies ran while one was open for 3% of the time, Pallas kernels for 0%

profile of v2, /device:TPU:33, one launch (start us, length us, event | category | flops | bytes accessed | tf_op | source)
XLA Modules:
  0.0 161.6 jit_solution(3890408471399577847)
XLA Ops:
  0.6 2.3 %shard_map.119 = (f32[2,384,256]{2,1,0:T(8,128)}, f32[2,16,256]{2,1,0:T(8,128)}) custom-call(bf16[100,2,360]{2,1,0:T(2,128)(2,1)} %state.1, bf16[100,2,360]{2,1,0:T(2,128)(2,1)} %target.1, s32[2,360]{1,0:T(2,128)} %land.1), custom_call_target="tpu_custom_call" | custom-call | tf_op jit(solution)/shard_map/pallas_call | solution.py:480
  2.9 2.7 %collective-permute-start = (f32[2,16,256]{2,1,0:T(8,128)}, f32[2,16,256]{2,1,0:T(8,128)S(1)}, u32[]{:S(2)}, u32[]{:S(2)}) collective-permute-start(f32[2,16,256]{2,1,0:T(8,128)} %get-tuple-element.18), channel_id=1, source_target_pairs={{0,1},{1,0},{2,3},{3,2},{4,5},{5,4},{6,7},{7,6},{8,9},{9,8},{10,11... | collective-permute-start | bytes 98312 | tf_op jit(solution)/shard_map/ppermute | solution.py:36
  5.7 1.7 %collective-permute-start.4 = (s32[1,32]{1,0:T(1,128)}, s32[1,32]{1,0:T(1,128)S(1)}, u32[]{:S(2)}, u32[]{:S(2)}) collective-permute-start(s32[1,32]{1,0:T(1,128)} %param.11), channel_id=1, source_target_pairs={{0,48},{1,49},{2,114},{3,115},{4,180},{5,181},{6,246},{7,247},{8,5... | collective-permute-start | bytes 392 | tf_op jit(solution)/shard_map/ppermute | solution.py:36
  7.3 5.5 %collective-permute-start.2 = (s32[1,32]{1,0:T(1,128)}, s32[1,32]{1,0:T(1,128)S(1)}, u32[]{:S(2)}, u32[]{:S(2)}) collective-permute-start(s32[1,32]{1,0:T(1,128)} %param.11), channel_id=1, source_target_pairs={{0,16},{1,17},{2,82},{3,83},{4,148},{5,149},{6,214},{7,215},{8,24}... | collective-permute-start | bytes 392 | tf_op jit(solution)/shard_map/ppermute | solution.py:36
  12.8 1.9 %collective-permute-start.1 = (s32[1,32]{1,0:T(1,128)}, s32[1,32]{1,0:T(1,128)S(1)}, u32[]{:S(2)}, u32[]{:S(2)}) collective-permute-start(s32[1,32]{1,0:T(1,128)} %param.11), channel_id=1, source_target_pairs={{0,0},{1,1},{2,66},{3,67},{4,132},{5,133},{6,198},{7,199},{8,8},{9... | collective-permute-start | bytes 392 | tf_op jit(solution)/shard_map/ppermute | solution.py:36
  14.8 0.6 stack.23.info
  15.4 2.7 %collective-permute-done.1.sd0 = s32[1,32]{1,0:T(1,128)S(1)} collective-permute-done((s32[1,32]{1,0:T(1,128)}, s32[1,32]{1,0:T(1,128)S(1)}, u32[]{:S(2)}, u32[]{:S(2)}) %collective-permute-start.1) | collective-permute-done | bytes 160 | tf_op jit(solution)/shard_map/ppermute | solution.py:36
  18.2 0.5 copy-done.9
  18.8 1.8 %shard_map.120.own = bf16[80,256]{1,0:T(8,128)(2,1)} custom-call(s32[5]{0:T(128)} %stack.23.info, f32[2,384,256]{2,1,0:T(8,128)} %get-tuple-element.16.x, f32[2,16,256]{2,1,0:T(8,128)} %copy-done.5, s32[1,32]{1,0:T(1,128)} %copy-done.9, s32[1,32]{1,0:T(1,128)} %copy-done.8, s32[1,32]{1,0:T(1,128)} %copy-done.7, s32[1,32]{1,0:T(1,128)} %copy-done.6), custom_call_target="tpu_custom_call" | custom-call | tf_op jit(solution)/shard_map/pallas_call | solution.py:493
  20.6 5.5 %collective-permute-start.8 = (bf16[80,256]{1,0:T(8,128)(2,1)}, bf16[80,256]{1,0:T(8,128)(2,1)S(1)}, u32[]{:S(2)}, u32[]{:S(2)}) collective-permute-start(bf16[80,256]{1,0:T(8,128)(2,1)} %shard_map.120.own), channel_id=1, source_target_pairs={{0,12},{1,13},{2,14},{3,15},{4,0},{5,1},{6,2},{7,3},{8,4},{9,5},{1... | collective-permute-start | bytes 122888 | tf_op jit(solution)/shard_map/ppermute | solution.py:36
  26.1 7.7 %collective-permute-start.7 = (bf16[80,256]{1,0:T(8,128)(2,1)}, bf16[80,256]{1,0:T(8,128)(2,1)S(1)}, u32[]{:S(2)}, u32[]{:S(2)}) collective-permute-start(bf16[80,256]{1,0:T(8,128)(2,1)} %shard_map.120.own), channel_id=1, source_target_pairs={{0,14},{1,15},{2,0},{3,1},{4,2},{5,3},{6,4},{7,5},{8,6},{9,7},{10,... | collective-permute-start | bytes 122888 | tf_op jit(solution)/shard_map/ppermute | solution.py:36
  33.8 1.0 collective-permute-done.7.s1
  35.2 3.2 %collective-permute-done.5.n2 = bf16[80,256]{1,0:T(8,128)(2,1)S(1)} collective-permute-done((bf16[80,256]{1,0:T(8,128)(2,1)}, bf16[80,256]{1,0:T(8,128)(2,1)S(1)}, u32[]{:S(2)}, u32[]{:S(2)}) %collective-permute-start.5) | collective-permute-done | bytes 40992 | tf_op jit(solution)/shard_map/ppermute | solution.py:36
  38.4 0.6 copy-done.4
  39.0 24.3 %shard_map.121 = (f32[16,112,256]{2,1,0:T(8,128)}, f32[16,112,256]{2,1,0:T(8,128)}) custom-call(s32[5]{0:T(128)} %stack.23.info, bf16[80,256]{1,0:T(8,128)(2,1)} %copy-done.4, bf16[80,256]{1,0:T(8,128)(2,1)} %copy-done.3, bf16[80,256]{1,0:T(8,128)(2,1)} %shard_map.120.own, bf16[80,256]{1,0:T(8,128)(2,1)} %copy-done.2, bf16[80,256]{1,0:T(8,128)(2,1)} %copy-done.1, ...), custom_call_target="tpu_custom_call" | custom-call | tf_op jit(solution)/shard_map/pallas_call | solution.py:495
  63.4 1.2 fusion.37
  64.6 1.3 multiply_exponential_fusion.10
  65.9 1.3 fusion.33
  67.9 1.0 fusion.24
  68.9 1.9 %select_convert_fusion.1 = f16[16,112,256]{2,1,0:T(8,128)(2,1)S(1)} fusion(f32[16,112,256]{2,1,0:T(8,128)} %get-tuple-element.21, f32[112]{0:T(128)S(1)} %multiply_exponential_fusion.10, f32[16,256]{1,0:T(8,128)S(1)} %bitcast.57, f32[256]{0:T(256)S(1)} %fusion.33, pred[112]{0:T(512)(128)(4,1)S(1)} %get-tuple-element.55, pred[112]{0:T(512)(128)(4,1)S(1)} %get-tuple-element.56), kind=kLoop, calls=%fused_computation.13 | loop fusion | flops 1835008 | bytes 2770592 | tf_op jit(solution)/shard_map/convert_element_type | solution.py:440
  70.8 1.6 %collective-permute-start.9 = (f16[16,112,256]{2,1,0:T(8,128)(2,1)S(1)}, f16[16,112,256]{2,1,0:T(8,128)(2,1)S(1)}, u32[]{:S(2)}, u32[]{:S(2)}) collective-permute-start(f16[16,112,256]{2,1,0:T(8,128)(2,1)S(1)} %select_convert_fusion.1), channel_id=1, source_target_pairs={{0,2},{1,3},{2,0},{3,1},{4,6},{5,7},{6,4},{7,5},{8,10},{9,11},{10,... | collective-permute-start | bytes 2752520 | tf_op jit(solution)/shard_map/ppermute | solution.py:36
  72.4 2.1 %collective-permute-done.9 = f16[16,112,256]{2,1,0:T(8,128)(2,1)S(1)} collective-permute-done((f16[16,112,256]{2,1,0:T(8,128)(2,1)S(1)}, f16[16,112,256]{2,1,0:T(8,128)(2,1)S(1)}, u32[]{:S(2)}, u32[]{:S(2)}) %collective-permute-start.9) | collective-permute-done | bytes 917536 | tf_op jit(solution)/shard_map/ppermute | solution.py:36
  74.7 0.5 fusion.36
  78.1 1.0 fusion.4
  79.6 17.1 %all_to_all.10 = f16[16,112,256]{2,1,0:T(8,128)(2,1)S(1)} all-to-all(f16[16,112,256]{2,1,0:T(8,128)(2,1)S(1)} %select_convert_fusion), channel_id=1, replica_groups=mesh['z'=8,'xl'=2,'y'=4,'c'=2,'xh'=2] {'xl','y','xh'}, dimensions={0} | all-to-all | bytes 1835008 | tf_op jit(solution)/shard_map/all_to_all | solution.py:454
  96.9 0.7 slice_reduce_fusion.5
  99.0 0.7 fusion.7
  99.9 0.5 fusion.40
  100.4 0.7 collective-permute-start.12
  101.2 2.1 %collective-permute-start.11 = (f16[112,256]{1,0:T(8,128)(2,1)S(1)}, f16[112,256]{1,0:T(8,128)(2,1)S(1)}, u32[]{:S(2)}, u32[]{:S(2)}) collective-permute-start(f16[112,256]{1,0:T(8,128)(2,1)S(1)} %get-tuple-element.38), channel_id=1, source_target_pairs={{0,64},{1,65},{2,66},{3,67},{4,68},{5,69},{6,70},{7,71},{8,72},{9,... | collective-permute-start | bytes 172040 | tf_op jit(solution)/shard_map/ppermute | solution.py:36
  103.2 1.2 multiply_exponential_fusion.7
  104.4 2.4 %collective-permute-done.10 = f16[112,256]{1,0:T(8,128)(2,1)S(1)} collective-permute-done((f16[112,256]{1,0:T(8,128)(2,1)S(1)}, f16[112,256]{1,0:T(8,128)(2,1)S(1)}, u32[]{:S(2)}, u32[]{:S(2)}) %collective-permute-start.10) | collective-permute-done | bytes 57376 | tf_op jit(solution)/shard_map/ppermute | solution.py:36
  106.8 0.6 fusion.41
  107.4 0.5 fusion.42
  108.0 0.5 fusion.43
  113.6 1.3 multiply_exponential_fusion.6
  114.9 1.3 multiply_exponential_fusion.5
  116.2 1.3 multiply_exponential_fusion.4
  117.9 0.5 fusion.38
  118.4 1.3 multiply_exponential_fusion.2
  119.7 5.7 %collective-permute-done.13 = f16[112,256]{1,0:T(8,128)(2,1)S(1)} collective-permute-done((f16[112,256]{1,0:T(8,128)(2,1)S(1)}, f16[112,256]{1,0:T(8,128)(2,1)S(1)}, u32[]{:S(2)}, u32[]{:S(2)}) %collective-permute-start.13) | collective-permute-done | bytes 57376 | tf_op jit(solution)/shard_map/ppermute | solution.py:36
  125.5 0.5 fusion.39
  128.6 1.3 multiply_exponential_fusion.1
  130.3 14.7 %all_to_all.11 = f16[16,112,256]{2,1,0:T(8,128)(2,1)S(1)} all-to-all(f16[16,112,256]{2,1,0:T(8,128)(2,1)S(1)} %broadcast_in_dim.405), channel_id=1, replica_groups=mesh['z'=8,'xl'=2,'y'=4,'c'=2,'xh'=2] {'xl','y','xh'}, dimensions={0} | all-to-all | bytes 1835008 | tf_op jit(solution)/shard_map/all_to_all | solution.py:468
  145.1 5.4 %collective-permute-start.14 = (f16[16,112,256]{2,1,0:T(8,128)(2,1)S(1)}, f16[16,112,256]{2,1,0:T(8,128)(2,1)S(1)}, u32[]{:S(2)}, u32[]{:S(2)}) collective-permute-start(f16[16,112,256]{2,1,0:T(8,128)(2,1)S(1)} %all_to_all.11), channel_id=1, source_target_pairs={{0,2},{1,3},{2,0},{3,1},{4,6},{5,7},{6,4},{7,5},{8,10},{9,11},{10,... | collective-permute-start | bytes 2752520 | tf_op jit(solution)/shard_map/ppermute | solution.py:36
  150.5 2.1 %collective-permute-done.14 = f16[16,112,256]{2,1,0:T(8,128)(2,1)S(1)} collective-permute-done((f16[16,112,256]{2,1,0:T(8,128)(2,1)S(1)}, f16[16,112,256]{2,1,0:T(8,128)(2,1)S(1)}, u32[]{:S(2)}, u32[]{:S(2)}) %collective-permute-start.14) | collective-permute-done | bytes 917536 | tf_op jit(solution)/shard_map/ppermute | solution.py:36
  153.4 3.9 %fusion.1.t = f32[32,112,256]{2,1,0:T(8,128)} fusion(f32[32]{0:T(128)S(1)} %get-tuple-element.28, f32[32]{0:T(128)S(1)} %get-tuple-element.27, f32[32,256]{1,0:T(8,128)S(1)} %bitcast.55, pred[112]{0:T(512)(128)(4,1)S(1)} %iota_compare_fusion.3, pred[112]{0:T(512)(128)(4,1)S(1)} %iota_compare_fusion.4, f16[16,112,256]{2,1,0:T(8,128)(2,1)S(1)} %collective-permute-done.14, ...), kind=kLoop, calls=%fused_computation.2 | loop fusion | flops 8257536 | bytes 5538272 | tf_op jit(solution)/shard_map/jit(_where)/select_n | solution.py:429
  157.3 4.4 %shard_map.122 = (f32[9,100,256]{2,1,0:T(8,128)}, f32[9,256,256]{2,1,0:T(8,128)}, f32[100,256]{1,0:T(8,128)}, f32[32,256]{1,0:T(8,128)}, f32[1,128]{1,0:T(1,128)}) custom-call(s32[5]{0:T(128)} %stack.23.info, f32[32,112,256]{2,1,0:T(8,128)} %fusion.1.t), custom_call_target="tpu_custom_call" | custom-call | tf_op jit(solution)/shard_map/pallas_call | solution.py:519
  (76 shorter events, 3.4 us)
Async XLA Ops:
  2.9 15.2 %collective-permute-start = (f32[2,16,256]{2,1,0:T(8,128)}, f32[2,16,256]{2,1,0:T(8,128)S(1)}, u32[]{:S(2)}, u32[]{:S(2)}) collective-permute-start(f32[2,16,256]{2,1,0:T(8,128)} %get-tuple-element.18), channel_id=1, source_target_pairs={{0,1},{1,0},{2,3},{3,2},{4,5},{5,4},{6,7},{7,6},{8,9},{9,8},{10,11... | collective-permute-start | bytes 98312 | tf_op jit(solution)/shard_map/ppermute | solution.py:36
  5.7 9.7 %collective-permute-start.4 = (s32[1,32]{1,0:T(1,128)}, s32[1,32]{1,0:T(1,128)S(1)}, u32[]{:S(2)}, u32[]{:S(2)}) collective-permute-start(s32[1,32]{1,0:T(1,128)} %param.11), channel_id=1, source_target_pairs={{0,48},{1,49},{2,114},{3,115},{4,180},{5,181},{6,246},{7,247},{8,5... | collective-permute-start | bytes 392 | tf_op jit(solution)/shard_map/ppermute | solution.py:36
  7.3 8.1 %collective-permute-start.3 = (s32[1,32]{1,0:T(1,128)}, s32[1,32]{1,0:T(1,128)S(1)}, u32[]{:S(2)}, u32[]{:S(2)}) collective-permute-start(s32[1,32]{1,0:T(1,128)} %param.11), channel_id=1, source_target_pairs={{0,32},{1,33},{2,98},{3,99},{4,164},{5,165},{6,230},{7,231},{8,40}... | collective-permute-start | bytes 392 | tf_op jit(solution)/shard_map/ppermute | solution.py:36
  7.3 8.1 %collective-permute-start.2 = (s32[1,32]{1,0:T(1,128)}, s32[1,32]{1,0:T(1,128)S(1)}, u32[]{:S(2)}, u32[]{:S(2)}) collective-permute-start(s32[1,32]{1,0:T(1,128)} %param.11), channel_id=1, source_target_pairs={{0,16},{1,17},{2,82},{3,83},{4,148},{5,149},{6,214},{7,215},{8,24}... | collective-permute-start | bytes 392 | tf_op jit(solution)/shard_map/ppermute | solution.py:36
  12.8 5.3 %collective-permute-start.1 = (s32[1,32]{1,0:T(1,128)}, s32[1,32]{1,0:T(1,128)S(1)}, u32[]{:S(2)}, u32[]{:S(2)}) collective-permute-start(s32[1,32]{1,0:T(1,128)} %param.11), channel_id=1, source_target_pairs={{0,0},{1,1},{2,66},{3,67},{4,132},{5,133},{6,198},{7,199},{8,8},{9... | collective-permute-start | bytes 392 | tf_op jit(solution)/shard_map/ppermute | solution.py:36
  15.4 2.7 %copy-start.6 = (s32[1,32]{1,0:T(1,128)}, s32[1,32]{1,0:T(1,128)S(1)}, u32[]{:S(2)}) copy-start(s32[1,32]{1,0:T(1,128)S(1)} %collective-permute-done.4.sd3) | copy-start | bytes 388
  15.4 2.7 %copy-start.7 = (s32[1,32]{1,0:T(1,128)}, s32[1,32]{1,0:T(1,128)S(1)}, u32[]{:S(2)}) copy-start(s32[1,32]{1,0:T(1,128)S(1)} %collective-permute-done.3.sd2) | copy-start | bytes 388
  15.4 2.7 %copy-start.8 = (s32[1,32]{1,0:T(1,128)}, s32[1,32]{1,0:T(1,128)S(1)}, u32[]{:S(2)}) copy-start(s32[1,32]{1,0:T(1,128)S(1)} %collective-permute-done.2.sd1) | copy-start | bytes 388
  18.1 0.5 copy-start.9
  18.1 0.6 copy-start.5
  20.6 13.2 %collective-permute-start.8 = (bf16[80,256]{1,0:T(8,128)(2,1)}, bf16[80,256]{1,0:T(8,128)(2,1)S(1)}, u32[]{:S(2)}, u32[]{:S(2)}) collective-permute-start(bf16[80,256]{1,0:T(8,128)(2,1)} %shard_map.120.own), channel_id=1, source_target_pairs={{0,12},{1,13},{2,14},{3,15},{4,0},{5,1},{6,2},{7,3},{8,4},{9,5},{1... | collective-permute-start | bytes 122888 | tf_op jit(solution)/shard_map/ppermute | solution.py:36
  26.1 8.8 %collective-permute-start.7 = (bf16[80,256]{1,0:T(8,128)(2,1)}, bf16[80,256]{1,0:T(8,128)(2,1)S(1)}, u32[]{:S(2)}, u32[]{:S(2)}) collective-permute-start(bf16[80,256]{1,0:T(8,128)(2,1)} %shard_map.120.own), channel_id=1, source_target_pairs={{0,14},{1,15},{2,0},{3,1},{4,2},{5,3},{6,4},{7,5},{8,6},{9,7},{10,... | collective-permute-start | bytes 122888 | tf_op jit(solution)/shard_map/ppermute | solution.py:36
  33.8 1.4 collective-permute-start.6
  33.8 4.6 %collective-permute-start.5 = (bf16[80,256]{1,0:T(8,128)(2,1)}, bf16[80,256]{1,0:T(8,128)(2,1)S(1)}, u32[]{:S(2)}, u32[]{:S(2)}) collective-permute-start(bf16[80,256]{1,0:T(8,128)(2,1)} %shard_map.120.own), channel_id=1, source_target_pairs={{0,4},{1,5},{2,6},{3,7},{4,8},{5,9},{6,10},{7,11},{8,12},{9,13},{1... | collective-permute-start | bytes 122888 | tf_op jit(solution)/shard_map/ppermute | solution.py:36
  33.8 4.6 %copy-start.1 = (bf16[80,256]{1,0:T(8,128)(2,1)}, bf16[80,256]{1,0:T(8,128)(2,1)S(1)}, u32[]{:S(2)}) copy-start(bf16[80,256]{1,0:T(8,128)(2,1)S(1)} %collective-permute-done.8.s2) | copy-start | bytes 122884
  34.9 3.5 %copy-start.2 = (bf16[80,256]{1,0:T(8,128)(2,1)}, bf16[80,256]{1,0:T(8,128)(2,1)S(1)}, u32[]{:S(2)}) copy-start(bf16[80,256]{1,0:T(8,128)(2,1)S(1)} %collective-permute-done.7.s1) | copy-start | bytes 122884
  35.2 3.2 %copy-start.3 = (bf16[80,256]{1,0:T(8,128)(2,1)}, bf16[80,256]{1,0:T(8,128)(2,1)S(1)}, u32[]{:S(2)}) copy-start(bf16[80,256]{1,0:T(8,128)(2,1)S(1)} %collective-permute-done.6.n1) | copy-start | bytes 122884
  38.4 0.6 copy-start.4
  70.8 7.4 %copy-start = (f32[16,112,256]{2,1,0:T(8,128)S(1)}, f32[16,112,256]{2,1,0:T(8,128)}, u32[]{:S(2)}) copy-start(f32[16,112,256]{2,1,0:T(8,128)} %get-tuple-element.20) | copy-start | bytes 5505028
  70.8 3.7 %collective-permute-start.9 = (f16[16,112,256]{2,1,0:T(8,128)(2,1)S(1)}, f16[16,112,256]{2,1,0:T(8,128)(2,1)S(1)}, u32[]{:S(2)}, u32[]{:S(2)}) collective-permute-start(f16[16,112,256]{2,1,0:T(8,128)(2,1)S(1)} %select_convert_fusion.1), channel_id=1, source_target_pairs={{0,2},{1,3},{2,0},{3,1},{4,6},{5,7},{6,4},{7,5},{8,10},{9,11},{10,... | collective-permute-start | bytes 2752520 | tf_op jit(solution)/shard_map/ppermute | solution.py:36
  100.4 7.5 %collective-permute-start.12 = (f16[112,256]{1,0:T(8,128)(2,1)S(1)}, f16[112,256]{1,0:T(8,128)(2,1)S(1)}, u32[]{:S(2)}, u32[]{:S(2)}) collective-permute-start(f16[112,256]{1,0:T(8,128)(2,1)S(1)} %get-tuple-element.38), channel_id=1, source_target_pairs={{0,96},{1,97},{2,98},{3,99},{4,100},{5,101},{6,102},{7,103},{8,104... | collective-permute-start | bytes 172040 | tf_op jit(solution)/shard_map/ppermute | solution.py:36
  101.2 6.2 %collective-permute-start.11 = (f16[112,256]{1,0:T(8,128)(2,1)S(1)}, f16[112,256]{1,0:T(8,128)(2,1)S(1)}, u32[]{:S(2)}, u32[]{:S(2)}) collective-permute-start(f16[112,256]{1,0:T(8,128)(2,1)S(1)} %get-tuple-element.38), channel_id=1, source_target_pairs={{0,64},{1,65},{2,66},{3,67},{4,68},{5,69},{6,70},{7,71},{8,72},{9,... | collective-permute-start | bytes 172040 | tf_op jit(solution)/shard_map/ppermute | solution.py:36
  103.2 3.6 %collective-permute-start.10 = (f16[112,256]{1,0:T(8,128)(2,1)S(1)}, f16[112,256]{1,0:T(8,128)(2,1)S(1)}, u32[]{:S(2)}, u32[]{:S(2)}) collective-permute-start(f16[112,256]{1,0:T(8,128)(2,1)S(1)} %get-tuple-element.38), channel_id=1, source_target_pairs={{0,32},{1,33},{2,34},{3,35},{4,36},{5,37},{6,38},{7,39},{8,40},{9,... | collective-permute-start | bytes 172040 | tf_op jit(solution)/shard_map/ppermute | solution.py:36
  118.4 7.0 %collective-permute-start.13 = (f16[112,256]{1,0:T(8,128)(2,1)S(1)}, f16[112,256]{1,0:T(8,128)(2,1)S(1)}, u32[]{:S(2)}, u32[]{:S(2)}) collective-permute-start(f16[112,256]{1,0:T(8,128)(2,1)S(1)} %get-tuple-element.36), channel_id=1, source_target_pairs={{0,128},{1,129},{2,130},{3,131},{4,132},{5,133},{6,134},{7,135},{8... | collective-permute-start | bytes 172040 | tf_op jit(solution)/shard_map/ppermute | solution.py:36
  145.1 7.5 %collective-permute-start.14 = (f16[16,112,256]{2,1,0:T(8,128)(2,1)S(1)}, f16[16,112,256]{2,1,0:T(8,128)(2,1)S(1)}, u32[]{:S(2)}, u32[]{:S(2)}) collective-permute-start(f16[16,112,256]{2,1,0:T(8,128)(2,1)S(1)} %all_to_all.11), channel_id=1, source_target_pairs={{0,2},{1,3},{2,0},{3,1},{4,6},{5,7},{6,4},{7,5},{8,10},{9,11},{10,... | collective-permute-start | bytes 2752520 | tf_op jit(solution)/shard_map/ppermute | solution.py:36

commit v3 on v2

--- a/solution.py
+++ b/solution.py
@@ -79,7 +79,7 @@
         edge_out[r, 10:13, :] = x_out[r, 8:11, :]
 
 
-def window_kernel(info, x, edge, sd0, sd1, sd2, sd3, win):
+def window_kernel(info, x, edge, sd0, sd1, win):
     m = info[0]
     start = info[1]
     row = lax.broadcasted_iota(jnp.int32, (16, 256), 0)
@@ -89,18 +89,19 @@
         base = pl.multiple_of(((start + 5) // 8) * 8, 8)
         near = x[r, pl.ds(base, WP + 8), :]
         w = pltpu.roll(near, WP + 8 - (start + 5 - base), 0)[0:WP]
-        e = edge[r]
+        e = edge[16 * r : 16 * r + 16, :]
         win[WP * r : WP * r + 16, :] = jnp.where(low, e, w[0:16]).astype(bf16)
         win[WP * r + 16 : WP * r + 32, :] = jnp.where(high, e, w[16:32]).astype(bf16)
     win[2 * WP : 2 * WP + 16, :] = jnp.zeros((16, 256), bf16)
     pad = jnp.zeros((12, 32), jnp.int32)
-    sd = jnp.concatenate([sd0[...], sd1[...], sd2[...], sd3[...], pad], axis=0)
+    far = edge[32:34, 0:32].astype(jnp.int32)
+    sd = jnp.concatenate([sd0[...], sd1[...], far, pad], axis=0)
     win[2 * WP : 2 * WP + 16, 0:32] = (sd >> 8).astype(f32).astype(bf16)
     win[2 * WP : 2 * WP + 16, 128:160] = (sd & 255).astype(f32).astype(bf16)
 
 
 def main_kernel(
-    info, n2, n1, own, s1, s2, w_in, w_mid, w_out, w_noise, mine_out, theirs_out,
+    info, n2, n1, own, s1, s2, w_in, w_mid, w_out, w_noise, g_out, e_out,
     S, T, SB, PB, HID, HO, SL, UP, OUT, DO, DM, INC, DS, QB, BIAS, SD, LT,
 ):
     own22 = info[2]
@@ -268,16 +269,9 @@
         dsum = lax.fori_loop(0, 23, in_cell, dsum)
 
     def store(k, lo, hi, value):
-        @pl.when(core == k // 16)
-        def _():
-            mine_out[k % 16, lo:hi, :] = value
-
-        @pl.when(core != k // 16)
-        def _():
-            theirs_out[k % 16, lo:hi, :] = value
-
-    mine_out[:, ROWS:BR, :] = jnp.zeros((16, BR - ROWS, C), f32)
-    theirs_out[:, ROWS:BR, :] = jnp.zeros((16, BR - ROWS, C), f32)
+        g_out[(k // 16) ^ core, k % 16, lo:hi, :] = value
+
+    g_out[:, :, ROWS:BR, :] = jnp.zeros((2, 16, BR - ROWS, C), f32)
     peaks = []
 
     def put(row, value):
@@ -337,24 +331,60 @@
     peaks.append(jnp.max(jnp.abs(gn), axis=0, keepdims=True))
     for k in range(NB):
         store(k, ROWS, ROWS + 1, gn[k : k + 1, :])
-    store(0, ROWS + 1, ROWS + 2, jnp.broadcast_to(loss, (1, C)))
+    store(0, ROWS + 1, ROWS + 3, jnp.broadcast_to(loss, (2, C)))
     peak = peaks[0]
     for p in peaks[1:]:
         peak = jnp.maximum(peak, p)
     peak = jnp.max(peak, axis=1, keepdims=True)
-    lane = lax.broadcasted_iota(jnp.int32, (1, C), 1)
-    top = jnp.where(lane < 128, peak, jnp.abs(loss))
-    top = jnp.ceil(jnp.log(jnp.maximum(top, 1e-30)) * 1.4426950408889634)
-    for k in range(16):
-        mine_out[k, BR - 1 : BR, :] = top
-        theirs_out[k, BR - 1 : BR, :] = top
-
-
-def final_kernel(info, t, o_in, o_mid, o_out, o_noise, o_loss):
+    lane = lax.broadcasted_iota(jnp.int32, (8, 256), 1)
+    e_out[...] = exponent(jnp.where(lane < 128, peak, jnp.abs(loss)))
+
+
+def exponent(bound):
+    return jnp.ceil(jnp.log(jnp.maximum(bound, 1e-30)) * 1.4426950408889634)
+
+
+def power(e):
+    return jnp.exp2(e)
+
+
+def plane_kernel(msg, out):
+    total = None
+    bound = None
+    row = lax.broadcasted_iota(jnp.int32, (BR, C), 0)
+    for j in range(16):
+        v = msg[j]
+        e = v[BR - 1 : BR, :]
+        grad = power(e[:, 0:1] - 14.0)
+        loss = power(e[:, 128:129] - 14.0)
+        f = jnp.where(row == ROWS + 1, loss, jnp.where(row == ROWS + 2, loss * 2.0**-11, grad))
+        v = v * f
+        total = v if total is None else total + v
+        b = power(e)
+        bound = b if bound is None else bound + b
+    out[...] = total
+    out[BR - 1 : BR, :] = bound
+
+
+def scale_kernel(a, b, out):
+    s = a[...] + b[...]
+    e = exponent(s[BR - 1 : BR, :])
+    grad = power(14.0 - e[:, 0:1])
+    loss = power(14.0 - e[:, 128:129])
+    row = lax.broadcasted_iota(jnp.int32, (BR, C), 0)
+    f = jnp.where((row == ROWS + 1) | (row == ROWS + 2), loss, grad)
+    out[...] = jnp.where(row == BR - 1, e, s * f)
+
+
+def final_kernel(info, half, far, o_in, o_mid, o_out, o_noise, o_loss, t):
     core = info[4]
-
-    def block(k):
-        return ((k // 16) ^ core) * 16 + k % 16
+    row = lax.broadcasted_iota(jnp.int32, (BR, C), 0)
+    is_loss = (row == ROWS + 1) | (row == ROWS + 2)
+    for slot, ref in ((core, half), (1 - core, far)):
+        for k in range(16):
+            e = ref[k, BR - 1 : BR, :]
+            f = jnp.where(is_loss, power(e[:, 128:129] - 14.0), power(e[:, 0:1] - 14.0))
+            t[slot * 16 + k] = ref[k] * f
 
     def get(row, n):
         parts = []
@@ -362,7 +392,7 @@
         while done < n:
             k, i = divmod(row + done, ROWS)
             take = min(n - done, ROWS - i)
-            parts.append((done, take, t[block(k), i : i + take, :]))
+            parts.append((done, take, t[k, i : i + take, :]))
             done += take
         return parts
 
@@ -396,8 +426,8 @@
     def noise_store(done, take, v):
         o_noise[done : done + take, :] = v
 
-    norm([[(k, 1, t[block(k), ROWS : ROWS + 1, :]) for k in range(NB)]], NB * C, [noise_store])
-    o_loss[...] = t[block(0), ROWS + 1 : ROWS + 2, 0:128] * (1.0 / (V * 16 * 720))
+    norm([[(k, 1, t[k, ROWS : ROWS + 1, :]) for k in range(NB)]], NB * C, [noise_store])
+    o_loss[...] = (t[0, ROWS + 1 : ROWS + 2, 0:128] + t[0, ROWS + 2 : ROWS + 3, 0:128]) * (1.0 / (V * 16 * 720))
 
 
 def call(kernel, outs, scratch, n_smem, n_in, single=False):
@@ -418,56 +448,31 @@
 f16 = jnp.float16
 
 
-def decode(msg):
-    v = msg.astype(f32)
-    e = v[..., BR - 1 : BR, 0:1]
-    el = v[..., BR - 1 : BR, 128:129]
-    row = lax.broadcasted_iota(jnp.int32, v.shape, v.ndim - 2)
-    tail = lax.slice_in_dim(v, ROWS + 2, ROWS + 3, axis=v.ndim - 2) * (2.0**-11)
-    power = jnp.where(row == ROWS + 1, el, e) - 14.0
-    v = jnp.where(row == ROWS + 1, v + tail, v)
-    return jnp.where(row > ROWS + 1, 0.0, v * jnp.exp2(power)), e, el
-
-
-def encode(v, e, el):
-    row = lax.broadcasted_iota(jnp.int32, v.shape, v.ndim - 2)
-    lane = lax.broadcasted_iota(jnp.int32, v.shape, v.ndim - 1)
-    big = v * jnp.exp2(14.0 - jnp.where(row == ROWS + 1, el, e))
-    loss = lax.slice_in_dim(v, ROWS + 1, ROWS + 2, axis=v.ndim - 2) * jnp.exp2(14.0 - el)
-    rest = (loss - lax.reduce_precision(loss, 5, 10)) * (2.0**11)
-    big = jnp.where(row == ROWS + 2, rest, big)
-    big = jnp.where(row == BR - 1, jnp.where(lane < 128, e, el), big)
-    return big.astype(f16)
-
-
-def sum_all(mine, theirs):
+def sum_all(g, e):
     xy = ("xl", "y", "xh")
 
     def other(z, xl, lat, xh):
         return (z, xl, lat ^ 1, xh)
 
-    e = mine[0:1, BR - 1 : BR, 0:1]
-    el = mine[0:1, BR - 1 : BR, 128:129]
-    got, e1, el1 = decode(send(encode(theirs, e, el), other))
-    s = jnp.where(lax.broadcasted_iota(jnp.int32, mine.shape, 1) > ROWS + 1, 0.0, mine) + got
-    e, el = jnp.maximum(e, e1[0:1]) + 1.0, jnp.maximum(el, el1[0:1]) + 1.0
-    got, e1, el1 = decode(lax.all_to_all(encode(s, e, el), xy, 0, 0, tiled=True))
-    s = got.sum(0)
-    e, el = jnp.max(e1, axis=0) + 4.0, jnp.max(el1, axis=0) + 4.0
-    msg = encode(s, e, el)
-    sets = [decode(msg)]
-    for k in (1, 2, 3):
-        sets.append(decode(send(msg, lambda z, xl, lat, xh, k=k: (z ^ k, xl, lat, xh))))
-    s = (sets[0][0] + sets[1][0]) + (sets[2][0] + sets[3][0])
-    e = jnp.maximum(jnp.maximum(sets[0][1], sets[1][1]), jnp.maximum(sets[2][1], sets[3][1])) + 2.0
-    el = jnp.maximum(jnp.maximum(sets[0][2], sets[1][2]), jnp.maximum(sets[2][2], sets[3][2])) + 2.0
-    msg = encode(s, e, el)
-    v0, e0, el0 = decode(msg)
-    v1, e1, el1 = decode(send(msg, lambda z, xl, lat, xh: (z ^ 4, xl, lat, xh)))
-    msg = encode(v0 + v1, jnp.maximum(e0, e1) + 1.0, jnp.maximum(el0, el1) + 1.0)
-    half = lax.all_to_all(jnp.broadcast_to(msg[None], (16,) + msg.shape), xy, 0, 0, tiled=True)
+    e = jnp.maximum(e, send(e, other)) + 1.0
+    grow = jnp.exp2(14.0 - e)
+    s = g[0] + send(g[1], other)
+    row = lax.broadcasted_iota(jnp.int32, s.shape, 1)
+    lane = lax.broadcasted_iota(jnp.int32, s.shape, 2)
+    s = s * jnp.where((row == ROWS + 1) | (row == ROWS + 2), grow[0, 128], grow[0, 0])
+    s = jnp.where(row == ROWS + 2, (s - lax.reduce_precision(s, 5, 10)) * 2.0**11, s)
+    s = jnp.where(row == BR - 1, jnp.where(lane < 128, e[0, 0], e[0, 128]), s)
+    got = lax.all_to_all(s.astype(f16), xy, 0, 0, tiled=True)
+    s = call(plane_kernel, [((BR, C), f32)], [], 0, 1, True)(got.astype(f32))
+    r1, r2, r3 = (
+        send(s, lambda z, xl, lat, xh, k=k: (z ^ k, xl, lat, xh)) for k in (1, 2, 3)
+    )
+    s = (s + r1) + (r2 + r3)
+    far = send(s, lambda z, xl, lat, xh: (7 - z, xl, lat, xh))
+    s = call(scale_kernel, [((BR, C), f32)], [], 0, 2, True)(s, far).astype(f16)
+    half = lax.all_to_all(jnp.broadcast_to(s[None], (16,) + s.shape), xy, 0, 0, tiled=True)
     far = send(half, other)
-    return decode(jnp.concatenate([half, far], axis=0))[0]
+    return half.astype(f32), far.astype(f32)
 
 
 def body(state, target, land, seeds, w_in, w_mid, w_out, w_noise):
@@ -477,23 +482,24 @@
     lat = lax.axis_index("y") * 2 + core
     member = z * 2 + xl
     info = jnp.stack([member, (45 * member) // 2, member % 2, lat, core]).astype(jnp.int32)
+    near = [
+        send(
+            seeds,
+            lambda z, xl, lat, xh, k=k: (z ^ (2 * (lat % 4) + xh), xl ^ k, lat, xh),
+        )
+        for k in range(2)
+    ]
     x, edge = call(
         prep_kernel, [((2, 384, 256), f32), ((2, 16, 256), f32)],
         [pltpu.VMEM((128, 384), f32)], 0, 3,
     )(state, target, land)
-    edge, seeds = lax.optimization_barrier((edge, seeds))
+    edge = jnp.concatenate([edge.reshape(32, 256), jnp.pad(
+        jnp.concatenate(near, axis=0).astype(f32), ((0, 6), (0, 224)))], axis=0)
     edge = send(edge, lambda z, xl, lat, xh: (z, xl, lat, xh ^ 1))
-    near = [
-        send(
-            seeds,
-            lambda z, xl, lat, xh, k=k: (z ^ (2 * (lat % 4) + (k >> 1)), xl ^ (k & 1), lat, xh),
-        )
-        for k in range(4)
-    ]
-    win = call(window_kernel, [((80, 256), bf16)], [], 1, 6, True)(info, x, edge, *near)
+    win = call(window_kernel, [((80, 256), bf16)], [], 1, 4, True)(info, x, edge, *near)
     n2, n1, s1, s2 = (lat_shift(win, d) for d in (2, 1, -1, -2))
-    mine, theirs = call(
-        main_kernel, [((16, BR, C), f32), ((16, BR, C), f32)],
+    g, e = call(
+        main_kernel, [((2, 16, BR, C), f32), ((8, 256), f32)],
         [
             pltpu.VMEM((264, 128), f32),
             pltpu.VMEM((264, 128), f32),
@@ -515,12 +521,12 @@
         ],
         1, 9,
     )(info, n2, n1, win, s1, s2, w_in, w_mid, w_out, w_noise)
-    total = sum_all(mine, theirs)
+    half, far = sum_all(g, e)
     o_in, o_mid, o_out, o_noise, o_loss = call(
         final_kernel,
         [((9, V, C), f32), ((9, C, C), f32), ((V, C), f32), ((NB, C), f32), ((1, 128), f32)],
-        [], 1, 1,
-    )(info, total)
+        [pltpu.VMEM((NB, BR, C), f32)], 1, 2,
+    )(info, half, far)
     return o_in, o_mid, o_out, o_noise, o_loss[0, 0]
 
 

time: 165 us -> 139 us (0.84); the launches traced: 162 us -> 139 us
  between operations: 13.5 us -> 0.75 us
  other arithmetic: 21.6 us -> 11.5 us
  waiting for transfers between devices: 19.6 us -> 24.7 us
  starting transfers between devices: 34.9 us -> 31.3 us
  local copies, waits for them, and re-layouts: 7.4 us -> 4.87 us
  blocking collectives: 31.9 us -> 34.2 us
    exp2 x11 -> x1, other arithmetic: 9 us -> 0.71 us  [sum_all(): grow = jnp.exp2(14.0 - e)]
    ppermute x15 -> x14, waiting for transfers between devices: 19.6 us -> 24.7 us  [send(): return lax.ppermute(v, AX, perm(f))]
    slice x10 -> x1, local copies, waits for them, and re-layouts: 5.46 us -> 0.53 us  [sum_all(): s = jnp.where(row == BR - 1, jnp.where(lane < 128, e[0, 0], e[0, 128]), s)]
    ppermute x15 -> x14, starting transfers between devices: 34.9 us -> 31.3 us  [send(): return lax.ppermute(v, AX, perm(f))]
    convert_element_type x12 -> x6, other arithmetic: 3.43 us -> 6.53 us  [the longest x2 2.84 us: sum_all(): return (half.astype(f32), far.astype(f32))]
    select_n x6 -> x2, other arithmetic: 5.18 us -> 2.59 us  [the longest x1 1.3 us: sum_all(): s = jnp.where(row == BR - 1, jnp.where(lane < 128, e[0, 0], e[0, 128]), s)]
    all_to_all x2, blocking collectives: 31.9 us -> 34.2 us  [the longest x1 18.2 us: sum_all(): got = lax.all_to_all(s.astype(f16), xy, 0, 0, tiled=True)]
    pallas_call x2 -> x4, Pallas kernels: 26.2 us -> 24.2 us  [the longest x1 18.4 us: body(): call(main_kernel, [((2, 16, BR, C), f32), ((8, 256), f32)], [pltpu.VMEM((...]
  transfers between devices with their start and end apart: 15 -> 14, of which waited for: 8 -> 9; matrix products, arithmetic and copies ran while one was open for 3% -> 4% of each run, Pallas kernels for 0% -> 2%
where the time goes in v3:
time: 139 us
  blocking collectives  34.2 us (25%)
  Pallas kernels  31.4 us (23%)
  starting transfers between devices  31.3 us (23%)
  waiting for transfers between devices  24.7 us (18%)
  other arithmetic  11.5 us (8%)
  local copies, waits for them, and re-layouts  4.87 us (4%)
    ppermute x14, starting transfers between devices, send(): return lax.ppermute(v, AX, perm(f))  31.3 us
    ppermute x14, waiting for transfers between devices, send(): return lax.ppermute(v, AX, perm(f))  24.7 us
    pallas_call x1, Pallas kernels, body(): call(main_kernel, [((2, 16, BR, C), f32), ((8, 256), f32)], [pltpu.VMEM((...  18.4 us
    all_to_all x1, blocking collectives, sum_all(): got = lax.all_to_all(s.astype(f16), xy, 0, 0, tiled=True)  18.2 us
    all_to_all x1, blocking collectives, sum_all(): lax.all_to_all(jnp.broadcast_to(s[None], (16,) + s.shape), xy, 0, 0, tile...  16 us
    pallas_call x1, Pallas kernels, body(): call(final_kernel, [((9, V, C), f32), ((9, C, C), f32), ((V, C), f32), ((...  4.82 us
    convert_element_type x2, other arithmetic, sum_all(): return (half.astype(f32), far.astype(f32))  2.84 us
  transfers between devices with their start and end apart: 14, of which 9 were waited for; matrix products, arithmetic and copies ran while one was open for 4% of the time, Pallas kernels for 2%

profile of v3, /device:TPU:33, one launch (start us, length us, event | category | flops | bytes accessed | tf_op | source)
XLA Modules:
  0.0 138.7 jit_solution(17435303166387565302)
XLA Ops:
  0.6 4.9 %collective-permute-start = (s32[1,32]{1,0:T(1,128)}, s32[1,32]{1,0:T(1,128)S(1)}, u32[]{:S(2)}, u32[]{:S(2)}) collective-permute-start(s32[1,32]{1,0:T(1,128)} %param.11), channel_id=1, source_target_pairs={{0,0},{1,33},{2,66},{3,99},{4,132},{5,165},{6,198},{7,231},{8,8},{... | collective-permute-start | bytes 392 | tf_op jit(solution)/shard_map/ppermute | solution.py:36
  5.5 1.0 collective-permute-start.1
  6.6 2.3 %shard_map.119 = (f32[2,384,256]{2,1,0:T(8,128)}, f32[2,16,256]{2,1,0:T(8,128)}) custom-call(bf16[100,2,360]{2,1,0:T(2,128)(2,1)} %state.1, bf16[100,2,360]{2,1,0:T(2,128)(2,1)} %target.1, s32[2,360]{1,0:T(2,128)} %land.1), custom_call_target="tpu_custom_call" | custom-call | tf_op jit(solution)/shard_map/pallas_call | solution.py:492
  8.9 1.1 collective-permute-done.1.sd1
  10.0 0.8 select_maximum_fusion
  10.7 0.5 collective-permute-start.2
  11.2 0.6 stack.23.info
  11.8 3.3 %collective-permute-done.2.edge = f32[40,256]{1,0:T(8,128)S(1)} collective-permute-done((f32[40,256]{1,0:T(8,128)S(1)}, f32[40,256]{1,0:T(8,128)S(1)}, u32[]{:S(2)}, u32[]{:S(2)}) %collective-permute-start.2) | collective-permute-done | bytes 40992 | tf_op jit(solution)/shard_map/ppermute | solution.py:36
  15.1 0.6 copy-done.3
  15.7 1.8 %shard_map.120.own = bf16[80,256]{1,0:T(8,128)(2,1)} custom-call(s32[5]{0:T(128)} %stack.23.info, f32[2,384,256]{2,1,0:T(8,128)} %get-tuple-element.14.x, f32[40,256]{1,0:T(8,128)} %copy-done.3, s32[1,32]{1,0:T(1,128)} %copy-done.8, s32[1,32]{1,0:T(1,128)} %copy-done.9), custom_call_target="tpu_custom_call" | custom-call | tf_op jit(solution)/shard_map/pallas_call | solution.py:499
  17.5 5.8 %collective-permute-start.3 = (bf16[80,256]{1,0:T(8,128)(2,1)}, bf16[80,256]{1,0:T(8,128)(2,1)S(1)}, u32[]{:S(2)}, u32[]{:S(2)}) collective-permute-start(bf16[80,256]{1,0:T(8,128)(2,1)} %shard_map.120.own), channel_id=1, source_target_pairs={{0,4},{1,5},{2,6},{3,7},{4,8},{5,9},{6,10},{7,11},{8,12},{9,13},{1... | collective-permute-start | bytes 122888 | tf_op jit(solution)/shard_map/ppermute | solution.py:36
  23.3 4.7 %collective-permute-start.4 = (bf16[80,256]{1,0:T(8,128)(2,1)}, bf16[80,256]{1,0:T(8,128)(2,1)S(1)}, u32[]{:S(2)}, u32[]{:S(2)}) collective-permute-start(bf16[80,256]{1,0:T(8,128)(2,1)} %shard_map.120.own), channel_id=1, source_target_pairs={{0,2},{1,3},{2,4},{3,5},{4,6},{5,7},{6,8},{7,9},{8,10},{9,11},{10,... | collective-permute-start | bytes 122888 | tf_op jit(solution)/shard_map/ppermute | solution.py:36
  28.0 0.4 collective-permute-start.5
  28.4 2.6 %collective-permute-start.6 = (bf16[80,256]{1,0:T(8,128)(2,1)}, bf16[80,256]{1,0:T(8,128)(2,1)S(1)}, u32[]{:S(2)}, u32[]{:S(2)}) collective-permute-start(bf16[80,256]{1,0:T(8,128)(2,1)} %shard_map.120.own), channel_id=1, source_target_pairs={{0,12},{1,13},{2,14},{3,15},{4,0},{5,1},{6,2},{7,3},{8,4},{9,5},{1... | collective-permute-start | bytes 122888 | tf_op jit(solution)/shard_map/ppermute | solution.py:36
  31.0 0.7 collective-permute-done.5.s1
  31.7 0.8 collective-permute-done.6.s2
  32.5 0.6 copy-done.7
  33.1 18.4 %shard_map.121 = (f32[2,16,112,256]{3,2,1,0:T(8,128)}, f32[8,256]{1,0:T(8,128)}) custom-call(s32[5]{0:T(128)} %stack.23.info, bf16[80,256]{1,0:T(8,128)(2,1)} %copy-done.4, bf16[80,256]{1,0:T(8,128)(2,1)} %copy-done.5, bf16[80,256]{1,0:T(8,128)(2,1)} %shard_map.120.own, bf16[80,256]{1,0:T(8,128)(2,1)} %copy-done.6, bf16[80,256]{1,0:T(8,128)(2,1)} %copy-done.7, ...), custom_call_target="tpu_custom_call" | custom-call | tf_op jit(solution)/shard_map/pallas_call | solution.py:501
  51.6 1.8 %slice_bitcast_fusion = f32[16,112,256]{2,1,0:T(8,128)S(1)} fusion(f32[2,16,112,256]{3,2,1,0:T(8,128)} %get-tuple-element.17), kind=kLoop, calls=%fused_computation.7 | loop fusion | bytes 3670016 | tf_op jit(solution)/shard_map/squeeze | solution.py:459
  53.4 3.1 %collective-permute-start.8 = (f32[16,112,256]{2,1,0:T(8,128)S(1)}, f32[16,112,256]{2,1,0:T(8,128)S(1)}, u32[]{:S(2)}, u32[]{:S(2)}) collective-permute-start(f32[16,112,256]{2,1,0:T(8,128)S(1)} %slice_bitcast_fusion), channel_id=1, source_target_pairs={{0,2},{1,3},{2,0},{3,1},{4,6},{5,7},{6,4},{7,5},{8,10},{9,11},{10,... | collective-permute-start | bytes 5505032 | tf_op jit(solution)/shard_map/ppermute | solution.py:36
  56.5 0.1 collective-permute-start.7
  56.6 3.4 %collective-permute-done.7 = f32[8,256]{1,0:T(8,128)S(1)} collective-permute-done((f32[8,256]{1,0:T(8,128)}, f32[8,256]{1,0:T(8,128)S(1)}, u32[]{:S(2)}, u32[]{:S(2)}) %collective-permute-start.7) | collective-permute-done | bytes 8224 | tf_op jit(solution)/shard_map/ppermute | solution.py:36
  60.0 0.7 multiply_exponential_fusion
  60.7 0.5 fusion.5
  61.2 1.3 or_select_fusion
  62.5 1.3 compare_select_fusion
  63.9 1.4 fusion.3
  65.2 18.2 %all_to_all.10 = f16[16,112,256]{2,1,0:T(8,128)(2,1)S(1)} all-to-all(f16[16,112,256]{2,1,0:T(8,128)(2,1)S(1)} %fusion.3), channel_id=1, replica_groups=mesh['z'=8,'xl'=2,'y'=4,'c'=2,'xh'=2] {'xl','y','xh'}, dimensions={0} | all-to-all | bytes 1835008 | tf_op jit(solution)/shard_map/all_to_all | solution.py:465
  83.4 1.4 %convert_element_type.22.msg = f32[16,112,256]{2,1,0:T(8,128)} convert(f16[16,112,256]{2,1,0:T(8,128)(2,1)S(1)} %all_to_all.10) | non-fusion elementwise | flops 458752 | bytes 2752512 | tf_op jit(solution)/shard_map/convert_element_type | solution.py:466
  84.8 2.3 %shard_map.122 = f32[112,256]{1,0:T(8,128)} custom-call(f32[16,112,256]{2,1,0:T(8,128)} %convert_element_type.22.msg), custom_call_target="tpu_custom_call" | custom-call | tf_op jit(solution)/shard_map/pallas_call | solution.py:466
  87.2 1.2 collective-permute-start.10
  88.4 0.7 collective-permute-start.11
  89.1 1.6 %collective-permute-start.9 = (f32[112,256]{1,0:T(8,128)}, f32[112,256]{1,0:T(8,128)S(1)}, u32[]{:S(2)}, u32[]{:S(2)}) collective-permute-start(f32[112,256]{1,0:T(8,128)} %shard_map.122), channel_id=1, source_target_pairs={{0,32},{1,33},{2,34},{3,35},{4,36},{5,37},{6,38},{7,39},{8,40},{9,... | collective-permute-start | bytes 344072 | tf_op jit(solution)/shard_map/ppermute | solution.py:36
  90.7 3.1 %collective-permute-done.10 = f32[112,256]{1,0:T(8,128)S(1)} collective-permute-done((f32[112,256]{1,0:T(8,128)}, f32[112,256]{1,0:T(8,128)S(1)}, u32[]{:S(2)}, u32[]{:S(2)}) %collective-permute-start.10) | collective-permute-done | bytes 114720 | tf_op jit(solution)/shard_map/ppermute | solution.py:36
  93.8 5.6 %collective-permute-done.11 = f32[112,256]{1,0:T(8,128)S(1)} collective-permute-done((f32[112,256]{1,0:T(8,128)}, f32[112,256]{1,0:T(8,128)S(1)}, u32[]{:S(2)}, u32[]{:S(2)}) %collective-permute-start.11) | collective-permute-done | bytes 114720 | tf_op jit(solution)/shard_map/ppermute | solution.py:36
  99.4 0.9 add_add_fusion.a
  100.4 0.7 collective-permute-start.12
  101.1 6.1 %collective-permute-done.12.b = f32[112,256]{1,0:T(8,128)S(1)} collective-permute-done((f32[112,256]{1,0:T(8,128)S(1)}, f32[112,256]{1,0:T(8,128)S(1)}, u32[]{:S(2)}, u32[]{:S(2)}) %collective-permute-start.12) | collective-permute-done | bytes 114720 | tf_op jit(solution)/shard_map/ppermute | solution.py:36
  107.2 0.6 copy-done.2
  107.9 1.7 %shard_map.123 = f32[112,256]{1,0:T(8,128)} custom-call(f32[112,256]{1,0:T(8,128)} %copy-done.1, f32[112,256]{1,0:T(8,128)} %copy-done.2), custom_call_target="tpu_custom_call" | custom-call | tf_op jit(solution)/shard_map/pallas_call | solution.py:472
  109.5 0.9 convert_element_type.23
  110.5 0.1 broadcast_in_dim.24
  110.5 16.0 %all_to_all.11 = f16[16,112,256]{2,1,0:T(8,128)(2,1)S(1)} all-to-all(f16[16,112,256]{2,1,0:T(8,128)(2,1)S(1)} %broadcast_in_dim.24), channel_id=1, replica_groups=mesh['z'=8,'xl'=2,'y'=4,'c'=2,'xh'=2] {'xl','y','xh'}, dimensions={0} | all-to-all | bytes 1835008 | tf_op jit(solution)/shard_map/all_to_all | solution.py:473
  126.5 3.9 %collective-permute-start.13 = (f16[16,112,256]{2,1,0:T(8,128)(2,1)S(1)}, f16[16,112,256]{2,1,0:T(8,128)(2,1)S(1)}, u32[]{:S(2)}, u32[]{:S(2)}) collective-permute-start(f16[16,112,256]{2,1,0:T(8,128)(2,1)S(1)} %all_to_all.11), channel_id=1, source_target_pairs={{0,2},{1,3},{2,0},{3,1},{4,6},{5,7},{6,4},{7,5},{8,10},{9,11},{10,... | collective-permute-start | bytes 2752520 | tf_op jit(solution)/shard_map/ppermute | solution.py:36
  130.4 1.4 %convert_element_type.24.half = f32[16,112,256]{2,1,0:T(8,128)} convert(f16[16,112,256]{2,1,0:T(8,128)(2,1)S(1)} %all_to_all.11) | non-fusion elementwise | flops 458752 | bytes 2752512 | tf_op jit(solution)/shard_map/convert_element_type | solution.py:475
  131.8 0.7 collective-permute-done.13
  132.5 1.4 %convert_element_type.25.far = f32[16,112,256]{2,1,0:T(8,128)} convert(f16[16,112,256]{2,1,0:T(8,128)(2,1)S(1)} %collective-permute-done.13) | non-fusion elementwise | flops 458752 | bytes 2752512 | tf_op jit(solution)/shard_map/convert_element_type | solution.py:475
  133.9 4.8 %shard_map.124 = (f32[9,100,256]{2,1,0:T(8,128)}, f32[9,256,256]{2,1,0:T(8,128)}, f32[100,256]{1,0:T(8,128)}, f32[32,256]{1,0:T(8,128)}, f32[1,128]{1,0:T(1,128)}) custom-call(s32[5]{0:T(128)} %stack.23.info, f32[16,112,256]{2,1,0:T(8,128)} %convert_element_type.24.half, f32[16,112,256]{2,1,0:T(8,128)} %convert_element_type.25.far), custom_call_target="tpu_custom_call" | custom-call | tf_op jit(solution)/shard_map/pallas_call | solution.py:525
  (24 shorter events, 0.1 us)
Async XLA Ops:
  0.6 8.2 %collective-permute-start = (s32[1,32]{1,0:T(1,128)}, s32[1,32]{1,0:T(1,128)S(1)}, u32[]{:S(2)}, u32[]{:S(2)}) collective-permute-start(s32[1,32]{1,0:T(1,128)} %param.11), channel_id=1, source_target_pairs={{0,0},{1,33},{2,66},{3,99},{4,132},{5,165},{6,198},{7,231},{8,8},{... | collective-permute-start | bytes 392 | tf_op jit(solution)/shard_map/ppermute | solution.py:36
  5.5 4.4 %collective-permute-start.1 = (s32[1,32]{1,0:T(1,128)}, s32[1,32]{1,0:T(1,128)S(1)}, u32[]{:S(2)}, u32[]{:S(2)}) collective-permute-start(s32[1,32]{1,0:T(1,128)} %param.11), channel_id=1, source_target_pairs={{0,16},{1,49},{2,82},{3,115},{4,148},{5,181},{6,214},{7,247},{8,24... | collective-permute-start | bytes 392 | tf_op jit(solution)/shard_map/ppermute | solution.py:36
  8.9 6.2 %copy-start.8 = (s32[1,32]{1,0:T(1,128)}, s32[1,32]{1,0:T(1,128)S(1)}, u32[]{:S(2)}) copy-start(s32[1,32]{1,0:T(1,128)S(1)} %collective-permute-done.sd0) | copy-start | bytes 388
  9.9 5.1 %copy-start.9 = (s32[1,32]{1,0:T(1,128)}, s32[1,32]{1,0:T(1,128)S(1)}, u32[]{:S(2)}) copy-start(s32[1,32]{1,0:T(1,128)S(1)} %collective-permute-done.1.sd1) | copy-start | bytes 388
  10.7 4.4 %collective-permute-start.2 = (f32[40,256]{1,0:T(8,128)S(1)}, f32[40,256]{1,0:T(8,128)S(1)}, u32[]{:S(2)}, u32[]{:S(2)}) collective-permute-start(f32[40,256]{1,0:T(8,128)S(1)} %select_maximum_fusion), channel_id=1, source_target_pairs={{0,1},{1,0},{2,3},{3,2},{4,5},{5,4},{6,7},{7,6},{8,9},{9,8},{10,11... | collective-permute-start | bytes 122888 | tf_op jit(solution)/shard_map/ppermute | solution.py:36
  15.1 0.6 copy-start.3
  17.5 13.5 %collective-permute-start.3 = (bf16[80,256]{1,0:T(8,128)(2,1)}, bf16[80,256]{1,0:T(8,128)(2,1)S(1)}, u32[]{:S(2)}, u32[]{:S(2)}) collective-permute-start(bf16[80,256]{1,0:T(8,128)(2,1)} %shard_map.120.own), channel_id=1, source_target_pairs={{0,4},{1,5},{2,6},{3,7},{4,8},{5,9},{6,10},{7,11},{8,12},{9,13},{1... | collective-permute-start | bytes 122888 | tf_op jit(solution)/shard_map/ppermute | solution.py:36
  23.3 7.7 %collective-permute-start.4 = (bf16[80,256]{1,0:T(8,128)(2,1)}, bf16[80,256]{1,0:T(8,128)(2,1)S(1)}, u32[]{:S(2)}, u32[]{:S(2)}) collective-permute-start(bf16[80,256]{1,0:T(8,128)(2,1)} %shard_map.120.own), channel_id=1, source_target_pairs={{0,2},{1,3},{2,4},{3,5},{4,6},{5,7},{6,8},{7,9},{8,10},{9,11},{10,... | collective-permute-start | bytes 122888 | tf_op jit(solution)/shard_map/ppermute | solution.py:36
  28.0 3.6 %collective-permute-start.5 = (bf16[80,256]{1,0:T(8,128)(2,1)}, bf16[80,256]{1,0:T(8,128)(2,1)S(1)}, u32[]{:S(2)}, u32[]{:S(2)}) collective-permute-start(bf16[80,256]{1,0:T(8,128)(2,1)} %shard_map.120.own), channel_id=1, source_target_pairs={{0,14},{1,15},{2,0},{3,1},{4,2},{5,3},{6,4},{7,5},{8,6},{9,7},{10,... | collective-permute-start | bytes 122888 | tf_op jit(solution)/shard_map/ppermute | solution.py:36
  28.4 4.1 %collective-permute-start.6 = (bf16[80,256]{1,0:T(8,128)(2,1)}, bf16[80,256]{1,0:T(8,128)(2,1)S(1)}, u32[]{:S(2)}, u32[]{:S(2)}) collective-permute-start(bf16[80,256]{1,0:T(8,128)(2,1)} %shard_map.120.own), channel_id=1, source_target_pairs={{0,12},{1,13},{2,14},{3,15},{4,0},{5,1},{6,2},{7,3},{8,4},{9,5},{1... | collective-permute-start | bytes 122888 | tf_op jit(solution)/shard_map/ppermute | solution.py:36
  31.0 1.5 %copy-start.4 = (bf16[80,256]{1,0:T(8,128)(2,1)}, bf16[80,256]{1,0:T(8,128)(2,1)S(1)}, u32[]{:S(2)}) copy-start(bf16[80,256]{1,0:T(8,128)(2,1)S(1)} %collective-permute-done.3.n2) | copy-start | bytes 122884
  31.0 1.5 %copy-start.5 = (bf16[80,256]{1,0:T(8,128)(2,1)}, bf16[80,256]{1,0:T(8,128)(2,1)S(1)}, u32[]{:S(2)}) copy-start(bf16[80,256]{1,0:T(8,128)(2,1)S(1)} %collective-permute-done.4.n1) | copy-start | bytes 122884
  31.7 0.8 copy-start.6
  32.5 0.6 copy-start.7
  51.6 12.3 %copy-start = (f32[2,16,112,256]{3,2,1,0:T(8,128)S(1)}, f32[2,16,112,256]{3,2,1,0:T(8,128)}, u32[]{:S(2)}) copy-start(f32[2,16,112,256]{3,2,1,0:T(8,128)} %get-tuple-element.17) | copy-start | bytes 11010052
  53.4 10.5 %collective-permute-start.8 = (f32[16,112,256]{2,1,0:T(8,128)S(1)}, f32[16,112,256]{2,1,0:T(8,128)S(1)}, u32[]{:S(2)}, u32[]{:S(2)}) collective-permute-start(f32[16,112,256]{2,1,0:T(8,128)S(1)} %slice_bitcast_fusion), channel_id=1, source_target_pairs={{0,2},{1,3},{2,0},{3,1},{4,6},{5,7},{6,4},{7,5},{8,10},{9,11},{10,... | collective-permute-start | bytes 5505032 | tf_op jit(solution)/shard_map/ppermute | solution.py:36
  56.5 3.5 %collective-permute-start.7 = (f32[8,256]{1,0:T(8,128)}, f32[8,256]{1,0:T(8,128)S(1)}, u32[]{:S(2)}, u32[]{:S(2)}) collective-permute-start(f32[8,256]{1,0:T(8,128)} %get-tuple-element.16), channel_id=1, source_target_pairs={{0,2},{1,3},{2,0},{3,1},{4,6},{5,7},{6,4},{7,5},{8,10},{9,11},{10,... | collective-permute-start | bytes 24584 | tf_op jit(solution)/shard_map/ppermute | solution.py:36
  87.2 6.7 %collective-permute-start.10 = (f32[112,256]{1,0:T(8,128)}, f32[112,256]{1,0:T(8,128)S(1)}, u32[]{:S(2)}, u32[]{:S(2)}) collective-permute-start(f32[112,256]{1,0:T(8,128)} %shard_map.122), channel_id=1, source_target_pairs={{0,64},{1,65},{2,66},{3,67},{4,68},{5,69},{6,70},{7,71},{8,72},{9,... | collective-permute-start | bytes 344072 | tf_op jit(solution)/shard_map/ppermute | solution.py:36
  88.4 11.1 %collective-permute-start.11 = (f32[112,256]{1,0:T(8,128)}, f32[112,256]{1,0:T(8,128)S(1)}, u32[]{:S(2)}, u32[]{:S(2)}) collective-permute-start(f32[112,256]{1,0:T(8,128)} %shard_map.122), channel_id=1, source_target_pairs={{0,96},{1,97},{2,98},{3,99},{4,100},{5,101},{6,102},{7,103},{8,104... | collective-permute-start | bytes 344072 | tf_op jit(solution)/shard_map/ppermute | solution.py:36
  89.1 10.4 %collective-permute-start.9 = (f32[112,256]{1,0:T(8,128)}, f32[112,256]{1,0:T(8,128)S(1)}, u32[]{:S(2)}, u32[]{:S(2)}) collective-permute-start(f32[112,256]{1,0:T(8,128)} %shard_map.122), channel_id=1, source_target_pairs={{0,32},{1,33},{2,34},{3,35},{4,36},{5,37},{6,38},{7,39},{8,40},{9,... | collective-permute-start | bytes 344072 | tf_op jit(solution)/shard_map/ppermute | solution.py:36
  100.4 6.9 %copy-start.1 = (f32[112,256]{1,0:T(8,128)}, f32[112,256]{1,0:T(8,128)S(1)}, u32[]{:S(2)}) copy-start(f32[112,256]{1,0:T(8,128)S(1)} %add_add_fusion.a) | copy-start | bytes 344068
  100.4 6.8 %collective-permute-start.12 = (f32[112,256]{1,0:T(8,128)S(1)}, f32[112,256]{1,0:T(8,128)S(1)}, u32[]{:S(2)}, u32[]{:S(2)}) collective-permute-start(f32[112,256]{1,0:T(8,128)S(1)} %add_add_fusion.a), channel_id=1, source_target_pairs={{0,224},{1,225},{2,226},{3,227},{4,228},{5,229},{6,230},{7,231},{8... | collective-permute-start | bytes 344072 | tf_op jit(solution)/shard_map/ppermute | solution.py:36
  107.2 0.6 copy-start.2
  126.5 6.0 %collective-permute-start.13 = (f16[16,112,256]{2,1,0:T(8,128)(2,1)S(1)}, f16[16,112,256]{2,1,0:T(8,128)(2,1)S(1)}, u32[]{:S(2)}, u32[]{:S(2)}) collective-permute-start(f16[16,112,256]{2,1,0:T(8,128)(2,1)S(1)} %all_to_all.11), channel_id=1, source_target_pairs={{0,2},{1,3},{2,0},{3,1},{4,6},{5,7},{6,4},{7,5},{8,10},{9,11},{10,... | collective-permute-start | bytes 2752520 | tf_op jit(solution)/shard_map/ppermute | solution.py:36

commit v4 on v3

--- a/solution.py
+++ b/solution.py
@@ -43,6 +43,14 @@
     return send(v, f)
 
 
+def member_index():
+    return lax.axis_index("z") * 2 + lax.axis_index("xl")
+
+
+def lat_index():
+    return lax.axis_index("y") * 2 + lax.axis_index("c")
+
+
 def params():
     return pltpu.CompilerParams(vmem_limit_bytes=VMEM)
 
@@ -64,9 +72,10 @@
     return gelu_both(x)[1]
 
 
-def prep_kernel(state, target, land, x_out, edge_out, sc):
+def prep_kernel(state, target, land, seeds, x_out, edge_out, seeds_out, sc):
     sc[...] = jnp.zeros(sc.shape, f32)
     edge_out[...] = jnp.zeros(edge_out.shape, f32)
+    seeds_out[...] = jnp.broadcast_to(seeds[...], seeds_out.shape)
     for r in range(2):
         x_out[r, 0:8, :] = jnp.zeros((8, 256), f32)
         x_out[r, 8 + TC : 384, :] = jnp.zeros((376 - TC, 256), f32)
@@ -75,13 +84,13 @@
         x_out[r, 8 : 8 + TC, 0:128] = sc[...].T[0:TC]
         sc[0:V, 0:TC] = target[:, r, :].astype(f32)
         x_out[r, 8 : 8 + TC, 128:256] = sc[...].T[0:TC]
-        edge_out[r, 0:3, :] = x_out[r, TC + 5 : TC + 8, :]
-        edge_out[r, 10:13, :] = x_out[r, 8:11, :]
-
-
-def window_kernel(info, x, edge, sd0, sd1, win):
-    m = info[0]
-    start = info[1]
+        edge_out[16 * r : 16 * r + 3, :] = x_out[r, TC + 5 : TC + 8, :]
+        edge_out[16 * r + 10 : 16 * r + 13, :] = x_out[r, 8:11, :]
+
+
+def window_kernel(x, edge, win):
+    m = member_index()
+    start = (45 * m) // 2
     row = lax.broadcasted_iota(jnp.int32, (16, 256), 0)
     low = (row < 3) & (m == 0)
     high = (row >= 10) & (row < 13) & (m == M - 1)
@@ -92,21 +101,15 @@
         e = edge[16 * r : 16 * r + 16, :]
         win[WP * r : WP * r + 16, :] = jnp.where(low, e, w[0:16]).astype(bf16)
         win[WP * r + 16 : WP * r + 32, :] = jnp.where(high, e, w[16:32]).astype(bf16)
-    win[2 * WP : 2 * WP + 16, :] = jnp.zeros((16, 256), bf16)
-    pad = jnp.zeros((12, 32), jnp.int32)
-    far = edge[32:34, 0:32].astype(jnp.int32)
-    sd = jnp.concatenate([sd0[...], sd1[...], far, pad], axis=0)
-    win[2 * WP : 2 * WP + 16, 0:32] = (sd >> 8).astype(f32).astype(bf16)
-    win[2 * WP : 2 * WP + 16, 128:160] = (sd & 255).astype(f32).astype(bf16)
 
 
 def main_kernel(
-    info, n2, n1, own, s1, s2, w_in, w_mid, w_out, w_noise, g_out, e_out,
-    S, T, SB, PB, HID, HO, SL, UP, OUT, DO, DM, INC, DS, QB, BIAS, SD, LT,
+    n2, n1, own, s1, s2, seeds, w_in, w_mid, w_out, w_noise, mine_out, theirs_out, e_out,
+    S, T, SB, PB, HID, HO, SL, UP, OUT, DO, DM, INC, DS, QB, BIAS, g_out, sems,
 ):
-    own22 = info[2]
-    lat = info[3]
-    core = info[4]
+    own22 = member_index() % 2
+    lat = lat_index()
+    core = lax.axis_index("c")
     rows = ((n2, 1, -2), (n1, 0, -1), (n1, 1, -1), (own, 0, 0), (own, 1, 0),
             (s1, 0, 1), (s1, 1, 1), (s2, 0, 2))
     for k, (ref, r, d) in enumerate(rows):
@@ -119,13 +122,7 @@
     QB[...] = jnp.broadcast_to(S[:, 104:105], QB.shape)
     for b in range(3):
         SB[b] = S[b : b + 256, :].astype(bf16)
-    for d, ref in ((-1, n1), (0, own), (1, s1), (2, s2)):
-        sd = ref[2 * WP : 2 * WP + 16, :].astype(f32)
-        group = pl.multiple_of(((lat + d + 8) & 3) * 8, 8)
-        SD[pl.ds(group, 8), :] = (sd[:, 0:128] * 256.0 + sd[:, 128:256])[0:8]
-    for k in range(4):
-        LT[4 * k : 4 * k + 4, :] = SD[8 * k : 8 * k + 4, :]
-    latents = (LT[:, 0:32] - 32767.5) / 18918.0
+    latents = (seeds[...].astype(f32) - 32767.5) / 18918.0
     BIAS[...] = jnp.dot(
         latents, w_noise[...], precision=lax.Precision.HIGHEST, preferred_element_type=f32
     )
@@ -331,60 +328,46 @@
     peaks.append(jnp.max(jnp.abs(gn), axis=0, keepdims=True))
     for k in range(NB):
         store(k, ROWS, ROWS + 1, gn[k : k + 1, :])
-    store(0, ROWS + 1, ROWS + 3, jnp.broadcast_to(loss, (2, C)))
+    loss = jnp.broadcast_to(loss * (1.0 / (V * 16 * 720)), (1, C))
+    first = loss.astype(bf16).astype(f32)
+    store(0, ROWS + 1, ROWS + 2, first)
+    store(0, ROWS + 2, ROWS + 3, loss - first)
+    peaks.append(jnp.abs(loss))
     peak = peaks[0]
     for p in peaks[1:]:
         peak = jnp.maximum(peak, p)
-    peak = jnp.max(peak, axis=1, keepdims=True)
-    lane = lax.broadcasted_iota(jnp.int32, (8, 256), 1)
-    e_out[...] = exponent(jnp.where(lane < 128, peak, jnp.abs(loss)))
+    peak = jnp.broadcast_to(jnp.max(peak, axis=1, keepdims=True), (8, C))
+    e_out[...] = exponent(peak)
+    moves = [
+        pltpu.make_async_copy(g_out.at[i], ref, sems.at[i])
+        for i, ref in enumerate((mine_out, theirs_out))
+    ]
+    for move in moves:
+        move.start()
+    for move in moves:
+        move.wait()
 
 
 def exponent(bound):
-    return jnp.ceil(jnp.log(jnp.maximum(bound, 1e-30)) * 1.4426950408889634)
-
-
-def power(e):
-    return jnp.exp2(e)
-
-
-def plane_kernel(msg, out):
-    total = None
-    bound = None
-    row = lax.broadcasted_iota(jnp.int32, (BR, C), 0)
-    for j in range(16):
-        v = msg[j]
-        e = v[BR - 1 : BR, :]
-        grad = power(e[:, 0:1] - 14.0)
-        loss = power(e[:, 128:129] - 14.0)
-        f = jnp.where(row == ROWS + 1, loss, jnp.where(row == ROWS + 2, loss * 2.0**-11, grad))
-        v = v * f
-        total = v if total is None else total + v
-        b = power(e)
-        bound = b if bound is None else bound + b
-    out[...] = total
-    out[BR - 1 : BR, :] = bound
-
-
-def scale_kernel(a, b, out):
-    s = a[...] + b[...]
-    e = exponent(s[BR - 1 : BR, :])
-    grad = power(14.0 - e[:, 0:1])
-    loss = power(14.0 - e[:, 128:129])
-    row = lax.broadcasted_iota(jnp.int32, (BR, C), 0)
-    f = jnp.where((row == ROWS + 1) | (row == ROWS + 2), loss, grad)
-    out[...] = jnp.where(row == BR - 1, e, s * f)
-
-
-def final_kernel(info, half, far, o_in, o_mid, o_out, o_noise, o_loss, t):
-    core = info[4]
-    row = lax.broadcasted_iota(jnp.int32, (BR, C), 0)
-    is_loss = (row == ROWS + 1) | (row == ROWS + 2)
-    for slot, ref in ((core, half), (1 - core, far)):
-        for k in range(16):
-            e = ref[k, BR - 1 : BR, :]
-            f = jnp.where(is_loss, power(e[:, 128:129] - 14.0), power(e[:, 0:1] - 14.0))
-            t[slot * 16 + k] = ref[k] * f
+    return jnp.ceil(jnp.log2(jnp.maximum(bound, 1e-30)))
+
+
+def final_kernel(half, far, o_in, o_mid, o_out, o_noise, o_loss, t, u, in_sems, out_sems):
+    core = lax.axis_index("c")
+    steps = []
+    for i, (slot, ref) in enumerate(((core, half), (1 - core, far))):
+        for j in range(4):
+            first = slot * 16 + 4 * j
+            move = pltpu.make_async_copy(
+                ref.at[pl.ds(4 * j, 4)], t.at[pl.ds(first, 4)], in_sems.at[4 * i + j]
+            )
+            move.start()
+            steps.append((first, move))
+    for first, move in steps:
+        move.wait()
+        for k in range(4):
+            f = jnp.exp2(t[first + k, BR - 1 : BR, :] - 14.0)
+            t[first + k] = t[first + k] * f
 
     def get(row, n):
         parts = []
@@ -392,114 +375,106 @@
         while done < n:
             k, i = divmod(row + done, ROWS)
             take = min(n - done, ROWS - i)
-            parts.append((done, take, t[k, i : i + take, :]))
+            parts.append((done, take, k, i))
             done += take
         return parts
 
-    def norm(pieces, count, stores):
-        total = jnp.zeros((1, C), f32)
+    def scale_of(pieces, count):
+        total = jnp.zeros((8, C), f32)
+        ragged = jnp.zeros((1, C), f32)
         for p in pieces:
-            for _, _, v in p:
-                total = total + jnp.sum(v * v, axis=0, keepdims=True)
+            for _, take, k, i in p:
+                v = t[k, i : i + take, :]
+                v = v * v
+                if take % 8 == 0:
+                    total = total + jnp.sum(v.reshape(take // 8, 8, C), axis=0)
+                else:
+                    ragged = ragged + jnp.sum(v, axis=0, keepdims=True)
+        total = jnp.sum(total, axis=0, keepdims=True) + ragged
         ms = jnp.sum(total, axis=1, keepdims=True) * (1.0 / count)
-        scale = lax.rsqrt(ms + 1e-6)
-        for p, store in zip(pieces, stores):
-            for done, take, v in p:
-                store(done, take, v * scale)
-
-    def into(ref, k):
-        def f(done, take, v):
-            ref[k, done : done + take, :] = v
-
-        return f
-
-    norm([get(C * k, C) for k in range(9)], 9 * C * C, [into(o_mid, k) for k in range(9)])
-    norm(
-        [get(9 * C + V * k, V) for k in range(9)], 9 * V * C, [into(o_in, k) for k in range(9)]
-    )
-
-    def out_store(done, take, v):
-        o_out[done : done + take, :] = v
-
-    norm([get(9 * C + 9 * V, V)], V * C, [out_store])
-
-    def noise_store(done, take, v):
-        o_noise[done : done + take, :] = v
-
-    norm([[(k, 1, t[k, ROWS : ROWS + 1, :]) for k in range(NB)]], NB * C, [noise_store])
-    o_loss[...] = (t[0, ROWS + 1 : ROWS + 2, 0:128] + t[0, ROWS + 2 : ROWS + 3, 0:128]) * (1.0 / (V * 16 * 720))
-
-
-def call(kernel, outs, scratch, n_smem, n_in, single=False):
-    specs = [pl.BlockSpec(memory_space=pltpu.SMEM)] * n_smem
-    specs += [pl.BlockSpec(memory_space=pltpu.VMEM)] * n_in
-    out_specs = [pl.BlockSpec(memory_space=pltpu.VMEM)] * len(outs)
-    shapes = [jax.ShapeDtypeStruct(s, d) for s, d in outs]
+        return lax.rsqrt(ms + 1e-6)
+
+    moves = []
+
+    def emit(pieces, scale, buf, out, k):
+        for done, take, b, i in pieces:
+            buf[done : done + take, :] = t[b, i : i + take, :] * scale
+        if out is not None:
+            move = pltpu.make_async_copy(buf, out, out_sems.at[k])
+            move.start()
+            moves.append(move)
+
+    pieces = [get(C * k, C) for k in range(9)]
+    scale = scale_of(pieces, 9 * C * C)
+    for k in range(9):
+        emit(pieces[k], scale, u.at[k], o_mid.at[k], k)
+    pieces = [get(9 * C + V * k, V) for k in range(9)]
+    scale = scale_of(pieces, 9 * V * C)
+    for k in range(9):
+        emit(pieces[k], scale, o_in.at[k], None, 0)
+    pieces = get(9 * C + 9 * V, V)
+    emit(pieces, scale_of([pieces], V * C), o_out, None, 0)
+    pieces = [(k, 1, k, ROWS) for k in range(NB)]
+    emit(pieces, scale_of([pieces], NB * C), o_noise, None, 0)
+    o_loss[...] = t[0, ROWS + 1 : ROWS + 2, 0:128] + t[0, ROWS + 2 : ROWS + 3, 0:128]
+    for move in moves:
+        move.wait()
+
+
+def call(kernel, outs, scratch, ins, place=None):
+    place = place or {}
+    vmem = pl.BlockSpec(memory_space=pltpu.VMEM)
+    left = pl.BlockSpec(memory_space=pl.ANY)
     return pl.pallas_call(
         kernel,
-        out_shape=shapes[0] if single else shapes,
-        in_specs=specs,
-        out_specs=out_specs[0] if single else out_specs,
+        out_shape=[jax.ShapeDtypeStruct(s, d) for s, d in outs],
+        in_specs=[left if ("in", i) in place else vmem for i in range(len(ins))],
+        out_specs=[left if ("out", i) in place else vmem for i in range(len(outs))],
         scratch_shapes=scratch,
         compiler_params=params(),
-    )
+    )(*ins)
 
 
 f16 = jnp.float16
 
 
-def sum_all(g, e):
+def sum_all(mine, theirs, e):
     xy = ("xl", "y", "xh")
 
     def other(z, xl, lat, xh):
         return (z, xl, lat ^ 1, xh)
 
-    e = jnp.maximum(e, send(e, other)) + 1.0
-    grow = jnp.exp2(14.0 - e)
-    s = g[0] + send(g[1], other)
-    row = lax.broadcasted_iota(jnp.int32, s.shape, 1)
-    lane = lax.broadcasted_iota(jnp.int32, s.shape, 2)
-    s = s * jnp.where((row == ROWS + 1) | (row == ROWS + 2), grow[0, 128], grow[0, 0])
-    s = jnp.where(row == ROWS + 2, (s - lax.reduce_precision(s, 5, 10)) * 2.0**11, s)
-    s = jnp.where(row == BR - 1, jnp.where(lane < 128, e[0, 0], e[0, 128]), s)
+    e = (jnp.maximum(e, send(e, other)) + 1.0)[0:1]
+    last = (jnp.arange(BR, dtype=jnp.int32) == BR - 1)[:, None]
+    tag = jnp.where(last, e, 0.0)
+    s = (mine + send(theirs, other)) * jnp.exp2(14.0 - e)[None] + tag[None]
     got = lax.all_to_all(s.astype(f16), xy, 0, 0, tiled=True)
-    s = call(plane_kernel, [((BR, C), f32)], [], 0, 1, True)(got.astype(f32))
+    q = jnp.exp2(got[:, BR - 1 : BR, :].astype(f32) - 14.0)
+    s = jnp.sum(jnp.where(last[None], 2.0**14, got.astype(f32)) * q, axis=0)
     r1, r2, r3 = (
         send(s, lambda z, xl, lat, xh, k=k: (z ^ k, xl, lat, xh)) for k in (1, 2, 3)
     )
     s = (s + r1) + (r2 + r3)
-    far = send(s, lambda z, xl, lat, xh: (7 - z, xl, lat, xh))
-    s = call(scale_kernel, [((BR, C), f32)], [], 0, 2, True)(s, far).astype(f16)
+    s = s + send(s, lambda z, xl, lat, xh: (7 - z, xl, lat, xh))
+    e = exponent(s[BR - 1 : BR, :])
+    s = jnp.where(last, e, s * jnp.exp2(14.0 - e)).astype(f16)
     half = lax.all_to_all(jnp.broadcast_to(s[None], (16,) + s.shape), xy, 0, 0, tiled=True)
     far = send(half, other)
     return half.astype(f32), far.astype(f32)
 
 
 def body(state, target, land, seeds, w_in, w_mid, w_out, w_noise):
-    z = lax.axis_index("z")
-    xl = lax.axis_index("xl")
-    core = lax.axis_index("c")
-    lat = lax.axis_index("y") * 2 + core
-    member = z * 2 + xl
-    info = jnp.stack([member, (45 * member) // 2, member % 2, lat, core]).astype(jnp.int32)
-    near = [
-        send(
-            seeds,
-            lambda z, xl, lat, xh, k=k: (z ^ (2 * (lat % 4) + xh), xl ^ k, lat, xh),
-        )
-        for k in range(2)
-    ]
-    x, edge = call(
-        prep_kernel, [((2, 384, 256), f32), ((2, 16, 256), f32)],
-        [pltpu.VMEM((128, 384), f32)], 0, 3,
-    )(state, target, land)
-    edge = jnp.concatenate([edge.reshape(32, 256), jnp.pad(
-        jnp.concatenate(near, axis=0).astype(f32), ((0, 6), (0, 224)))], axis=0)
+    x, edge, seeds = call(
+        prep_kernel, [((2, 384, 256), f32), ((32, 256), f32), ((M, 32), jnp.int32)],
+        [pltpu.VMEM((128, 384), f32)], (state, target, land, seeds),
+    )
     edge = send(edge, lambda z, xl, lat, xh: (z, xl, lat, xh ^ 1))
-    win = call(window_kernel, [((80, 256), bf16)], [], 1, 4, True)(info, x, edge, *near)
+    seeds = lax.all_to_all(seeds, ("z", "xl"), 0, 0, tiled=True)
+    (win,) = call(window_kernel, [((2 * WP, 256), bf16)], [], (x, edge))
+    win, seeds = lax.optimization_barrier((win, seeds))
     n2, n1, s1, s2 = (lat_shift(win, d) for d in (2, 1, -1, -2))
-    g, e = call(
-        main_kernel, [((2, 16, BR, C), f32), ((8, 256), f32)],
+    mine, theirs, e = call(
+        main_kernel, [((16, BR, C), f32), ((16, BR, C), f32), ((8, C), f32)],
         [
             pltpu.VMEM((264, 128), f32),
             pltpu.VMEM((264, 128), f32),
@@ -516,17 +491,25 @@
             pltpu.VMEM((64, C), f32),
             pltpu.VMEM((264, 128), f32),
             pltpu.VMEM((M, C), f32),
-            pltpu.VMEM((32, 128), f32),
-            pltpu.VMEM((M, 128), f32),
+            pltpu.VMEM((2, 16, BR, C), f32),
+            pltpu.SemaphoreType.DMA((2,)),
         ],
-        1, 9,
-    )(info, n2, n1, win, s1, s2, w_in, w_mid, w_out, w_noise)
-    half, far = sum_all(g, e)
+        (n2, n1, win, s1, s2, seeds, w_in, w_mid, w_out, w_noise),
+        {("out", 0), ("out", 1)},
+    )
+    half, far = sum_all(mine, theirs, e)
     o_in, o_mid, o_out, o_noise, o_loss = call(
         final_kernel,
         [((9, V, C), f32), ((9, C, C), f32), ((V, C), f32), ((NB, C), f32), ((1, 128), f32)],
-        [pltpu.VMEM((NB, BR, C), f32)], 1, 2,
-    )(info, half, far)
+        [
+            pltpu.VMEM((NB, BR, C), f32),
+            pltpu.VMEM((9, C, C), f32),
+            pltpu.SemaphoreType.DMA((8,)),
+            pltpu.SemaphoreType.DMA((9,)),
+        ],
+        (half, far),
+        {("in", 0), ("in", 1), ("out", 1)},
+    )
     return o_in, o_mid, o_out, o_noise, o_loss[0, 0]
 
 

time: 139 us -> 121 us (0.87)
  other arithmetic: 11.5 us -> 6.12 us
  starting transfers between devices: 31.3 us -> 27.5 us
  local copies, waits for them, and re-layouts: 4.87 us -> 1.3 us
  Pallas kernels: 31.4 us -> 27.9 us
  blocking collectives: 34.2 us -> 31.6 us
    ppermute x14 -> x12, starting transfers between devices: 31.3 us -> 19.5 us  [send(): return lax.ppermute(v, AX, perm(f))]
    all_to_all x0 -> x1, starting transfers between devices: none -> 8.05 us  [body(): seeds = lax.all_to_all(seeds, ('z', 'xl'), 0, 0, tiled=True)]
    ppermute x14 -> x12, waiting for transfers between devices: 24.7 us -> 20.3 us  [send(): return lax.ppermute(v, AX, perm(f))]
    all_to_all x0 -> x1, waiting for transfers between devices: none -> 3.81 us  [body(): seeds = lax.all_to_all(seeds, ('z', 'xl'), 0, 0, tiled=True)]
    pallas_call x6 -> x4, Pallas kernels: 31.4 us -> 27.9 us  [call(): pl.pallas_call(kernel, out_shape=[jax.ShapeDtypeStruct(s, d) for s, d in...]
    select_n x2 -> x1, other arithmetic: 2.59 us -> 0.08 us  [sum_all(): tag = jnp.where(last, e, 0.0)]
    convert_element_type x3 -> x1, other arithmetic: 2.33 us -> 0.09 us  [sum_all(): s = jnp.where(last, e, s * jnp.exp2(14.0 - e)).astype(f16)]
    squeeze x1 -> x0, local copies, waits for them, and re-layouts: 1.77 us -> none  [sum_all(): s = g[0] + send(g[1], other)]
  transfers between devices with their start and end apart: 14 -> 13, of which waited for: 9 -> 9; matrix products, arithmetic and copies ran while one was open for 4% -> 2% of each run, Pallas kernels for 2% -> 1%
where the time goes in v4:
time: 121 us; the launch traced here: 119 us
  blocking collectives  31.6 us (26%)
  Pallas kernels  27.9 us (23%)
  starting transfers between devices  27.5 us (23%)
  waiting for transfers between devices  24.2 us (20%)
  other arithmetic  6.12 us (5%)
  local copies, waits for them, and re-layouts  1.3 us (1%)
    pallas_call x4, Pallas kernels, call(): pl.pallas_call(kernel, out_shape=[jax.ShapeDtypeStruct(s, d) for s, d in...  27.9 us
    ppermute x12, waiting for transfers between devices, send(): return lax.ppermute(v, AX, perm(f))  20.3 us
    ppermute x12, starting transfers between devices, send(): return lax.ppermute(v, AX, perm(f))  19.5 us
    all_to_all x1, blocking collectives, sum_all(): got = lax.all_to_all(s.astype(f16), xy, 0, 0, tiled=True)  17 us
    all_to_all x1, blocking collectives, sum_all(): lax.all_to_all(jnp.broadcast_to(s[None], (16,) + s.shape), xy, 0, 0, tile...  14.6 us
    all_to_all x1, starting transfers between devices, body(): seeds = lax.all_to_all(seeds, ('z', 'xl'), 0, 0, tiled=True)  8.05 us
    all_to_all x1, waiting for transfers between devices, body(): seeds = lax.all_to_all(seeds, ('z', 'xl'), 0, 0, tiled=True)  3.81 us
    convert_element_type x2, other arithmetic, sum_all(): return (half.astype(f32), far.astype(f32))  2.87 us
  transfers between devices with their start and end apart: 13, of which 9 were waited for; matrix products, arithmetic and copies ran while one was open for 2% of the time, Pallas kernels for 1%

profile of v4, /device:TPU:33, one launch (start us, length us, event | category | flops | bytes accessed | tf_op | source)
XLA Modules:
  0.0 119.5 jit_solution(7182865536444611600)
XLA Ops:
  0.6 2.3 %shard_map.119 = (f32[2,384,256]{2,1,0:T(8,128)}, f32[32,256]{1,0:T(8,128)}, s32[16,32]{1,0:T(8,128)}) custom-call(bf16[100,2,360]{2,1,0:T(2,128)(2,1)} %state.1, bf16[100,2,360]{2,1,0:T(2,128)(2,1)} %target.1, s32[2,360]{1,0:T(2,128)} %land.1, s32[1,32]{1,0:T(1,128)} %seeds.1), custom_call_target="tpu_custom_call" | custom-call | tf_op jit(solution)/shard_map/pallas_call | solution.py:428
  2.9 2.7 %collective-permute-start = (f32[32,256]{1,0:T(8,128)}, f32[32,256]{1,0:T(8,128)S(1)}, u32[]{:S(2)}, u32[]{:S(2)}) collective-permute-start(f32[32,256]{1,0:T(8,128)} %get-tuple-element.19), channel_id=1, source_target_pairs={{0,1},{1,0},{2,3},{3,2},{4,5},{5,4},{6,7},{7,6},{8,9},{9,8},{10,11... | collective-permute-start | bytes 98312 | tf_op jit(solution)/shard_map/ppermute | solution.py:36
  5.7 8.1 %all-to-all-start = ((s32[16,1,32]{2,1,0:T(1,128)}), s32[16,1,32]{2,1,0:T(1,128)S(1)}, u32[]{:S(2)}, u32[]{:S(2)}) async-start(s32[16,1,32]{2,1,0:T(1,128)} %bitcast.15), calls=%async_computation | async-start | bytes 16384 | tf_op jit(solution)/shard_map/all_to_all | solution.py:472
  13.7 0.0 collective-permute-done.edge
  13.7 0.0 copy-start.1
  13.8 0.6 copy-done.1
  14.4 1.8 %shard_map.120.own = bf16[64,256]{1,0:T(8,128)(2,1)} custom-call(f32[2,384,256]{2,1,0:T(8,128)} %get-tuple-element.18.x, f32[32,256]{1,0:T(8,128)} %copy-done.1), custom_call_target="tpu_custom_call" | custom-call | tf_op jit(solution)/shard_map/pallas_call | solution.py:428
  16.1 3.8 %all-to-all-done = s32[16,1,32]{2,1,0:T(1,128)S(1)} async-done(((s32[16,1,32]{2,1,0:T(1,128)}), s32[16,1,32]{2,1,0:T(1,128)S(1)}, u32[]{:S(2)}, u32[]{:S(2)}) %all-to-all-start) | async-done | bytes 2080 | tf_op jit(solution)/shard_map/all_to_all | solution.py:472
  19.9 2.7 %collective-permute-start.4 = (bf16[64,256]{1,0:T(8,128)(2,1)}, bf16[64,256]{1,0:T(8,128)(2,1)S(1)}, u32[]{:S(2)}, u32[]{:S(2)}) collective-permute-start(bf16[64,256]{1,0:T(8,128)(2,1)} %shard_map.120.own), channel_id=1, source_target_pairs={{0,12},{1,13},{2,14},{3,15},{4,0},{5,1},{6,2},{7,3},{8,4},{9,5},{1... | collective-permute-start | bytes 98312 | tf_op jit(solution)/shard_map/ppermute | solution.py:36
  22.7 2.7 %collective-permute-start.3 = (bf16[64,256]{1,0:T(8,128)(2,1)}, bf16[64,256]{1,0:T(8,128)(2,1)S(1)}, u32[]{:S(2)}, u32[]{:S(2)}) collective-permute-start(bf16[64,256]{1,0:T(8,128)(2,1)} %shard_map.120.own), channel_id=1, source_target_pairs={{0,14},{1,15},{2,0},{3,1},{4,2},{5,3},{6,4},{7,5},{8,6},{9,7},{10,... | collective-permute-start | bytes 98312 | tf_op jit(solution)/shard_map/ppermute | solution.py:36
  25.3 0.0 collective-permute-start.2
  25.4 0.0 collective-permute-start.1
  25.4 0.0 collective-permute-done.4.s2
  25.4 0.0 copy-start.2
  25.4 1.0 collective-permute-done.3.s1
  26.4 0.3 collective-permute-done.2.n1
  26.8 3.0 %collective-permute-done.1.n2 = bf16[64,256]{1,0:T(8,128)(2,1)S(1)} collective-permute-done((bf16[64,256]{1,0:T(8,128)(2,1)}, bf16[64,256]{1,0:T(8,128)(2,1)S(1)}, u32[]{:S(2)}, u32[]{:S(2)}) %collective-permute-start.1) | collective-permute-done | bytes 32800 | tf_op jit(solution)/shard_map/ppermute | solution.py:36
  29.8 0.0 copy-done
  29.8 0.0 copy-done.2
  29.8 0.0 copy-done.3
  29.8 0.0 copy-start.5
  29.8 0.6 copy-done.5
  30.4 19.0 %shard_map.121 = (f32[16,112,256]{2,1,0:T(8,128)}, f32[16,112,256]{2,1,0:T(8,128)}, f32[8,256]{1,0:T(8,128)}) custom-call(bf16[64,256]{1,0:T(8,128)(2,1)} %copy-done.5, bf16[64,256]{1,0:T(8,128)(2,1)} %copy-done.4, bf16[64,256]{1,0:T(8,128)(2,1)} %shard_map.120.own, bf16[64,256]{1,0:T(8,128)(2,1)} %copy-done.3, bf16[64,256]{1,0:T(8,128)(2,1)} %copy-done.2, ...), custom_call_target="tpu_custom_call" | custom-call | tf_op jit(solution)/shard_map/pallas_call | solution.py:428
  49.4 1.5 %collective-permute-start.5 = (f32[16,112,256]{2,1,0:T(8,128)}, f32[16,112,256]{2,1,0:T(8,128)S(1)}, u32[]{:S(2)}, u32[]{:S(2)}) collective-permute-start(f32[16,112,256]{2,1,0:T(8,128)} %get-tuple-element.24), channel_id=1, source_target_pairs={{0,2},{1,3},{2,0},{3,1},{4,6},{5,7},{6,4},{7,5},{8,10},{9,11},{10,... | collective-permute-start | bytes 5505032 | tf_op jit(solution)/shard_map/ppermute | solution.py:36
  50.9 0.1 collective-permute-start.6
  51.1 3.5 %collective-permute-done.6 = f32[8,256]{1,0:T(8,128)S(1)} collective-permute-done((f32[8,256]{1,0:T(8,128)}, f32[8,256]{1,0:T(8,128)S(1)}, u32[]{:S(2)}, u32[]{:S(2)}) %collective-permute-start.6) | collective-permute-done | bytes 8224 | tf_op jit(solution)/shard_map/ppermute | solution.py:36
  54.6 0.7 multiply_exponential_fusion.1
  55.3 0.1 broadcast_select_fusion
  55.4 0.0 collective-permute-done.5
  55.4 2.0 %add_convert_fusion = f16[16,112,256]{2,1,0:T(8,128)(2,1)S(1)} fusion(f32[16,112,256]{2,1,0:T(8,128)} %get-tuple-element.23, f32[16,112,256]{2,1,0:T(8,128)S(1)} %collective-permute-done.5, f32[112,256]{1,0:T(8,128)S(1)} %broadcast_select_fusion, f32[256]{0:T(256)S(1)} %bitcast.18), kind=kLoop, calls=%fused_computation.1 | loop fusion | flops 1835008 | bytes 4703232 | tf_op jit(solution)/shard_map/convert_element_type | solution.py:451
  57.3 17.0 %all_to_all.22 = f16[16,112,256]{2,1,0:T(8,128)(2,1)S(1)} all-to-all(f16[16,112,256]{2,1,0:T(8,128)(2,1)S(1)} %add_convert_fusion), channel_id=1, replica_groups=mesh['z'=8,'xl'=2,'y'=4,'c'=2,'xh'=2] {'xl','y','xh'}, dimensions={0} | all-to-all | bytes 1835008 | tf_op jit(solution)/shard_map/all_to_all | solution.py:451
  74.4 0.3 multiply_reduce_fusion
  74.7 0.4 collective-permute-start.9
  75.1 3.0 %collective-permute-start.8 = (f32[112,256]{1,0:T(8,128)S(1)}, f32[112,256]{1,0:T(8,128)S(1)}, u32[]{:S(2)}, u32[]{:S(2)}) collective-permute-start(f32[112,256]{1,0:T(8,128)S(1)} %multiply_reduce_fusion), channel_id=1, source_target_pairs={{0,64},{1,65},{2,66},{3,67},{4,68},{5,69},{6,70},{7,71},{8,72},{9,... | collective-permute-start | bytes 344072 | tf_op jit(solution)/shard_map/ppermute | solution.py:36
  78.0 0.0 collective-permute-start.7
  78.0 1.2 %collective-permute-done.9 = f32[112,256]{1,0:T(8,128)S(1)} collective-permute-done((f32[112,256]{1,0:T(8,128)S(1)}, f32[112,256]{1,0:T(8,128)S(1)}, u32[]{:S(2)}, u32[]{:S(2)}) %collective-permute-start.9) | collective-permute-done | bytes 114720 | tf_op jit(solution)/shard_map/ppermute | solution.py:36
  79.3 5.1 %collective-permute-done.8 = f32[112,256]{1,0:T(8,128)S(1)} collective-permute-done((f32[112,256]{1,0:T(8,128)S(1)}, f32[112,256]{1,0:T(8,128)S(1)}, u32[]{:S(2)}, u32[]{:S(2)}) %collective-permute-start.8) | collective-permute-done | bytes 114720 | tf_op jit(solution)/shard_map/ppermute | solution.py:36
  84.4 0.0 collective-permute-done.7
  84.4 1.3 %collective-permute-start.10 = (f32[112,256]{1,0:T(8,128)S(1)}, f32[112,256]{1,0:T(8,128)S(1)}, u32[]{:S(2)}, u32[]{:S(2)}) collective-permute-start(f32[112,256]{1,0:T(8,128)S(1)} %add_add_fusion), channel_id=1, source_target_pairs={{0,224},{1,225},{2,226},{3,227},{4,228},{5,229},{6,230},{7,231},{8... | collective-permute-start | bytes 344072 | tf_op jit(solution)/shard_map/ppermute | solution.py:36
  85.7 5.5 %collective-permute-done.10 = f32[112,256]{1,0:T(8,128)S(1)} collective-permute-done((f32[112,256]{1,0:T(8,128)S(1)}, f32[112,256]{1,0:T(8,128)S(1)}, u32[]{:S(2)}, u32[]{:S(2)}) %collective-permute-start.10) | collective-permute-done | bytes 114720 | tf_op jit(solution)/shard_map/ppermute | solution.py:36
  91.2 0.1 select_convert_fusion
  91.3 0.1 broadcast_in_dim.66
  91.3 14.6 %all_to_all.23 = f16[16,112,256]{2,1,0:T(8,128)(2,1)S(1)} all-to-all(f16[16,112,256]{2,1,0:T(8,128)(2,1)S(1)} %broadcast_in_dim.66), channel_id=1, replica_groups=mesh['z'=8,'xl'=2,'y'=4,'c'=2,'xh'=2] {'xl','y','xh'}, dimensions={0} | all-to-all | bytes 1835008 | tf_op jit(solution)/shard_map/all_to_all | solution.py:461
  106.0 5.1 %collective-permute-start.11 = (f16[16,112,256]{2,1,0:T(8,128)(2,1)S(1)}, f16[16,112,256]{2,1,0:T(8,128)(2,1)S(1)}, u32[]{:S(2)}, u32[]{:S(2)}) collective-permute-start(f16[16,112,256]{2,1,0:T(8,128)(2,1)S(1)} %all_to_all.23), channel_id=1, source_target_pairs={{0,2},{1,3},{2,0},{3,1},{4,6},{5,7},{6,4},{7,5},{8,10},{9,11},{10,... | collective-permute-start | bytes 2752520 | tf_op jit(solution)/shard_map/ppermute | solution.py:36
  111.1 1.5 %convert_element_type.22.half = f32[16,112,256]{2,1,0:T(8,128)} convert(f16[16,112,256]{2,1,0:T(8,128)(2,1)S(1)} %all_to_all.23) | non-fusion elementwise | flops 458752 | bytes 2752512 | tf_op jit(solution)/shard_map/convert_element_type | solution.py:463
  112.6 0.6 collective-permute-done.11
  113.2 1.4 %convert_element_type.23.far = f32[16,112,256]{2,1,0:T(8,128)} convert(f16[16,112,256]{2,1,0:T(8,128)(2,1)S(1)} %collective-permute-done.11) | non-fusion elementwise | flops 458752 | bytes 2752512 | tf_op jit(solution)/shard_map/convert_element_type | solution.py:463
  114.6 4.8 %shard_map.122 = (f32[9,100,256]{2,1,0:T(8,128)}, f32[9,256,256]{2,1,0:T(8,128)}, f32[100,256]{1,0:T(8,128)}, f32[32,256]{1,0:T(8,128)}, f32[1,128]{1,0:T(1,128)}) custom-call(f32[16,112,256]{2,1,0:T(8,128)} %convert_element_type.22.half, f32[16,112,256]{2,1,0:T(8,128)} %convert_element_type.23.far), custom_call_target="tpu_custom_call" | custom-call | tf_op jit(solution)/shard_map/pallas_call | solution.py:428
  (10 shorter events, 0.1 us)
Async XLA Ops:
  2.9 10.8 %collective-permute-start = (f32[32,256]{1,0:T(8,128)}, f32[32,256]{1,0:T(8,128)S(1)}, u32[]{:S(2)}, u32[]{:S(2)}) collective-permute-start(f32[32,256]{1,0:T(8,128)} %get-tuple-element.19), channel_id=1, source_target_pairs={{0,1},{1,0},{2,3},{3,2},{4,5},{5,4},{6,7},{7,6},{8,9},{9,8},{10,11... | collective-permute-start | bytes 98312 | tf_op jit(solution)/shard_map/ppermute | solution.py:36
  5.7 14.3 %all-to-all-start = ((s32[16,1,32]{2,1,0:T(1,128)}), s32[16,1,32]{2,1,0:T(1,128)S(1)}, u32[]{:S(2)}, u32[]{:S(2)}) async-start(s32[16,1,32]{2,1,0:T(1,128)} %bitcast.15), calls=%async_computation | async-start | bytes 16384 | tf_op jit(solution)/shard_map/all_to_all | solution.py:472
  13.7 0.6 copy-start.1
  19.9 9.8 %copy-start = (s32[16,1,32]{2,1,0:T(1,128)}, s32[16,1,32]{2,1,0:T(1,128)S(1)}, u32[]{:S(2)}) copy-start(s32[16,1,32]{2,1,0:T(1,128)S(1)} %all-to-all-done) | copy-start | bytes 6148
  19.9 5.4 %collective-permute-start.4 = (bf16[64,256]{1,0:T(8,128)(2,1)}, bf16[64,256]{1,0:T(8,128)(2,1)S(1)}, u32[]{:S(2)}, u32[]{:S(2)}) collective-permute-start(bf16[64,256]{1,0:T(8,128)(2,1)} %shard_map.120.own), channel_id=1, source_target_pairs={{0,12},{1,13},{2,14},{3,15},{4,0},{5,1},{6,2},{7,3},{8,4},{9,5},{1... | collective-permute-start | bytes 98312 | tf_op jit(solution)/shard_map/ppermute | solution.py:36
  22.7 3.7 %collective-permute-start.3 = (bf16[64,256]{1,0:T(8,128)(2,1)}, bf16[64,256]{1,0:T(8,128)(2,1)S(1)}, u32[]{:S(2)}, u32[]{:S(2)}) collective-permute-start(bf16[64,256]{1,0:T(8,128)(2,1)} %shard_map.120.own), channel_id=1, source_target_pairs={{0,14},{1,15},{2,0},{3,1},{4,2},{5,3},{6,4},{7,5},{8,6},{9,7},{10,... | collective-permute-start | bytes 98312 | tf_op jit(solution)/shard_map/ppermute | solution.py:36
  25.3 1.4 %collective-permute-start.2 = (bf16[64,256]{1,0:T(8,128)(2,1)}, bf16[64,256]{1,0:T(8,128)(2,1)S(1)}, u32[]{:S(2)}, u32[]{:S(2)}) collective-permute-start(bf16[64,256]{1,0:T(8,128)(2,1)} %shard_map.120.own), channel_id=1, source_target_pairs={{0,2},{1,3},{2,4},{3,5},{4,6},{5,7},{6,8},{7,9},{8,10},{9,11},{10,... | collective-permute-start | bytes 98312 | tf_op jit(solution)/shard_map/ppermute | solution.py:36
  25.4 4.4 %collective-permute-start.1 = (bf16[64,256]{1,0:T(8,128)(2,1)}, bf16[64,256]{1,0:T(8,128)(2,1)S(1)}, u32[]{:S(2)}, u32[]{:S(2)}) collective-permute-start(bf16[64,256]{1,0:T(8,128)(2,1)} %shard_map.120.own), channel_id=1, source_target_pairs={{0,4},{1,5},{2,6},{3,7},{4,8},{5,9},{6,10},{7,11},{8,12},{9,13},{1... | collective-permute-start | bytes 98312 | tf_op jit(solution)/shard_map/ppermute | solution.py:36
  25.4 4.4 %copy-start.2 = (bf16[64,256]{1,0:T(8,128)(2,1)}, bf16[64,256]{1,0:T(8,128)(2,1)S(1)}, u32[]{:S(2)}) copy-start(bf16[64,256]{1,0:T(8,128)(2,1)S(1)} %collective-permute-done.4.s2) | copy-start | bytes 98308
  26.4 3.4 %copy-start.3 = (bf16[64,256]{1,0:T(8,128)(2,1)}, bf16[64,256]{1,0:T(8,128)(2,1)S(1)}, u32[]{:S(2)}) copy-start(bf16[64,256]{1,0:T(8,128)(2,1)S(1)} %collective-permute-done.3.s1) | copy-start | bytes 98308
  26.8 3.0 %copy-start.4 = (bf16[64,256]{1,0:T(8,128)(2,1)}, bf16[64,256]{1,0:T(8,128)(2,1)S(1)}, u32[]{:S(2)}) copy-start(bf16[64,256]{1,0:T(8,128)(2,1)S(1)} %collective-permute-done.2.n1) | copy-start | bytes 98308
  29.8 0.6 copy-start.5
  49.4 5.9 %collective-permute-start.5 = (f32[16,112,256]{2,1,0:T(8,128)}, f32[16,112,256]{2,1,0:T(8,128)S(1)}, u32[]{:S(2)}, u32[]{:S(2)}) collective-permute-start(f32[16,112,256]{2,1,0:T(8,128)} %get-tuple-element.24), channel_id=1, source_target_pairs={{0,2},{1,3},{2,0},{3,1},{4,6},{5,7},{6,4},{7,5},{8,10},{9,11},{10,... | collective-permute-start | bytes 5505032 | tf_op jit(solution)/shard_map/ppermute | solution.py:36
  50.9 3.6 %collective-permute-start.6 = (f32[8,256]{1,0:T(8,128)}, f32[8,256]{1,0:T(8,128)S(1)}, u32[]{:S(2)}, u32[]{:S(2)}) collective-permute-start(f32[8,256]{1,0:T(8,128)} %get-tuple-element.25), channel_id=1, source_target_pairs={{0,2},{1,3},{2,0},{3,1},{4,6},{5,7},{6,4},{7,5},{8,10},{9,11},{10,... | collective-permute-start | bytes 24584 | tf_op jit(solution)/shard_map/ppermute | solution.py:36
  74.7 4.6 %collective-permute-start.9 = (f32[112,256]{1,0:T(8,128)S(1)}, f32[112,256]{1,0:T(8,128)S(1)}, u32[]{:S(2)}, u32[]{:S(2)}) collective-permute-start(f32[112,256]{1,0:T(8,128)S(1)} %multiply_reduce_fusion), channel_id=1, source_target_pairs={{0,96},{1,97},{2,98},{3,99},{4,100},{5,101},{6,102},{7,103},{8,104... | collective-permute-start | bytes 344072 | tf_op jit(solution)/shard_map/ppermute | solution.py:36
  75.1 9.3 %collective-permute-start.8 = (f32[112,256]{1,0:T(8,128)S(1)}, f32[112,256]{1,0:T(8,128)S(1)}, u32[]{:S(2)}, u32[]{:S(2)}) collective-permute-start(f32[112,256]{1,0:T(8,128)S(1)} %multiply_reduce_fusion), channel_id=1, source_target_pairs={{0,64},{1,65},{2,66},{3,67},{4,68},{5,69},{6,70},{7,71},{8,72},{9,... | collective-permute-start | bytes 344072 | tf_op jit(solution)/shard_map/ppermute | solution.py:36
  78.0 6.3 %collective-permute-start.7 = (f32[112,256]{1,0:T(8,128)S(1)}, f32[112,256]{1,0:T(8,128)S(1)}, u32[]{:S(2)}, u32[]{:S(2)}) collective-permute-start(f32[112,256]{1,0:T(8,128)S(1)} %multiply_reduce_fusion), channel_id=1, source_target_pairs={{0,32},{1,33},{2,34},{3,35},{4,36},{5,37},{6,38},{7,39},{8,40},{9,... | collective-permute-start | bytes 344072 | tf_op jit(solution)/shard_map/ppermute | solution.py:36
  84.4 6.7 %collective-permute-start.10 = (f32[112,256]{1,0:T(8,128)S(1)}, f32[112,256]{1,0:T(8,128)S(1)}, u32[]{:S(2)}, u32[]{:S(2)}) collective-permute-start(f32[112,256]{1,0:T(8,128)S(1)} %add_add_fusion), channel_id=1, source_target_pairs={{0,224},{1,225},{2,226},{3,227},{4,228},{5,229},{6,230},{7,231},{8... | collective-permute-start | bytes 344072 | tf_op jit(solution)/shard_map/ppermute | solution.py:36
  106.0 7.2 %collective-permute-start.11 = (f16[16,112,256]{2,1,0:T(8,128)(2,1)S(1)}, f16[16,112,256]{2,1,0:T(8,128)(2,1)S(1)}, u32[]{:S(2)}, u32[]{:S(2)}) collective-permute-start(f16[16,112,256]{2,1,0:T(8,128)(2,1)S(1)} %all_to_all.23), channel_id=1, source_target_pairs={{0,2},{1,3},{2,0},{3,1},{4,6},{5,7},{6,4},{7,5},{8,10},{9,11},{10,... | collective-permute-start | bytes 2752520 | tf_op jit(solution)/shard_map/ppermute | solution.py:36

commit v5 on v4

--- a/solution.py
+++ b/solution.py
@@ -20,7 +20,6 @@
 BR = 112
 NB = 32
 AX = ("z", "xl", "y", "c", "xh")
-VMEM = 56 * 1024 * 1024
 
 
 def perm(f):
@@ -51,8 +50,8 @@
     return lax.axis_index("y") * 2 + lax.axis_index("c")
 
 
-def params():
-    return pltpu.CompilerParams(vmem_limit_bytes=VMEM)
+def params(limit=None):
+    return pltpu.CompilerParams(vmem_limit_bytes=(limit or 16) * 1024 * 1024)
 
 
 def gelu(x):
@@ -72,7 +71,16 @@
     return gelu_both(x)[1]
 
 
-def prep_kernel(state, target, land, seeds, x_out, edge_out, seeds_out, sc):
+def prep_kernel(
+    state, target, land, seeds, w_in, w_out, w_noise,
+    x_out, edge_out, seeds_out, w_in_out, w_out_out, w_noise_out, sc, sems,
+):
+    moves = [
+        pltpu.make_async_copy(w, out, sems.at[i])
+        for i, (w, out) in enumerate(((w_in, w_in_out), (w_out, w_out_out), (w_noise, w_noise_out)))
+    ]
+    for move in moves:
+        move.start()
     sc[...] = jnp.zeros(sc.shape, f32)
     edge_out[...] = jnp.zeros(edge_out.shape, f32)
     seeds_out[...] = jnp.broadcast_to(seeds[...], seeds_out.shape)
@@ -86,6 +94,8 @@
         x_out[r, 8 : 8 + TC, 128:256] = sc[...].T[0:TC]
         edge_out[16 * r : 16 * r + 3, :] = x_out[r, TC + 5 : TC + 8, :]
         edge_out[16 * r + 10 : 16 * r + 13, :] = x_out[r, 8:11, :]
+    for move in moves:
+        move.wait()
 
 
 def window_kernel(x, edge, win):
@@ -104,8 +114,8 @@
 
 
 def main_kernel(
-    n2, n1, own, s1, s2, seeds, w_in, w_mid, w_out, w_noise, mine_out, theirs_out, e_out,
-    S, T, SB, PB, HID, HO, SL, UP, OUT, DO, DM, INC, DS, QB, BIAS, g_out, sems,
+    n2, n1, own, s1, s2, seeds, w_in, w_mid, w_out, w_noise, g_out, e_out,
+    S, T, SB, PB, HID, HO, SL, UP, OUT, DO, DM, INC, DS, QB, BIAS,
 ):
     own22 = member_index() % 2
     lat = lat_index()
@@ -338,36 +348,18 @@
         peak = jnp.maximum(peak, p)
     peak = jnp.broadcast_to(jnp.max(peak, axis=1, keepdims=True), (8, C))
     e_out[...] = exponent(peak)
-    moves = [
-        pltpu.make_async_copy(g_out.at[i], ref, sems.at[i])
-        for i, ref in enumerate((mine_out, theirs_out))
-    ]
-    for move in moves:
-        move.start()
-    for move in moves:
-        move.wait()
 
 
 def exponent(bound):
     return jnp.ceil(jnp.log2(jnp.maximum(bound, 1e-30)))
 
 
-def final_kernel(half, far, o_in, o_mid, o_out, o_noise, o_loss, t, u, in_sems, out_sems):
+def final_kernel(half, far, o_in, o_mid, o_out, o_noise, o_loss, t, u, out_sems):
     core = lax.axis_index("c")
-    steps = []
-    for i, (slot, ref) in enumerate(((core, half), (1 - core, far))):
-        for j in range(4):
-            first = slot * 16 + 4 * j
-            move = pltpu.make_async_copy(
-                ref.at[pl.ds(4 * j, 4)], t.at[pl.ds(first, 4)], in_sems.at[4 * i + j]
-            )
-            move.start()
-            steps.append((first, move))
-    for first, move in steps:
-        move.wait()
-        for k in range(4):
-            f = jnp.exp2(t[first + k, BR - 1 : BR, :] - 14.0)
-            t[first + k] = t[first + k] * f
+    for slot, ref in ((core, half), (1 - core, far)):
+        for k in range(16):
+            f = jnp.exp2(ref[k, BR - 1 : BR, :] - 14.0)
+            t[slot * 16 + k] = ref[k] * f
 
     def get(row, n):
         parts = []
@@ -421,17 +413,23 @@
         move.wait()
 
 
-def call(kernel, outs, scratch, ins, place=None):
+def call(kernel, outs, scratch, ins, place=None, kept=(), limit=None):
     place = place or {}
     vmem = pl.BlockSpec(memory_space=pltpu.VMEM)
     left = pl.BlockSpec(memory_space=pl.ANY)
+    ins = [
+        pltpu.with_memory_space_constraint(v, pltpu.VMEM) if i in kept else v
+        for i, v in enumerate(ins)
+    ]
     return pl.pallas_call(
         kernel,
-        out_shape=[jax.ShapeDtypeStruct(s, d) for s, d in outs],
+        out_shape=[
+            pltpu.VMEM(o[0], o[1]) if len(o) > 2 else jax.ShapeDtypeStruct(*o) for o in outs
+        ],
         in_specs=[left if ("in", i) in place else vmem for i in range(len(ins))],
         out_specs=[left if ("out", i) in place else vmem for i in range(len(outs))],
         scratch_shapes=scratch,
-        compiler_params=params(),
+        compiler_params=params(limit),
     )(*ins)
 
 
@@ -464,17 +462,23 @@
 
 
 def body(state, target, land, seeds, w_in, w_mid, w_out, w_noise):
-    x, edge, seeds = call(
-        prep_kernel, [((2, 384, 256), f32), ((32, 256), f32), ((M, 32), jnp.int32)],
-        [pltpu.VMEM((128, 384), f32)], (state, target, land, seeds),
+    x, edge, seeds, w_in, w_out, w_noise = call(
+        prep_kernel,
+        [
+            ((2, 384, 256), f32, 1), ((32, 256), f32, 1), ((M, 32), jnp.int32, 1),
+            ((9, V, C), bf16, 1), ((V, C), bf16, 1), ((NB, C), f32, 1),
+        ],
+        [pltpu.VMEM((128, 384), f32), pltpu.SemaphoreType.DMA((3,))],
+        (state, target, land, seeds, w_in, w_out, w_noise),
+        {("in", 4), ("in", 5), ("in", 6)},
     )
     edge = send(edge, lambda z, xl, lat, xh: (z, xl, lat, xh ^ 1))
     seeds = lax.all_to_all(seeds, ("z", "xl"), 0, 0, tiled=True)
-    (win,) = call(window_kernel, [((2 * WP, 256), bf16)], [], (x, edge))
+    (win,) = call(window_kernel, [((2 * WP, 256), bf16, 1)], [], (x, edge), kept=(0, 1))
     win, seeds = lax.optimization_barrier((win, seeds))
     n2, n1, s1, s2 = (lat_shift(win, d) for d in (2, 1, -1, -2))
-    mine, theirs, e = call(
-        main_kernel, [((16, BR, C), f32), ((16, BR, C), f32), ((8, C), f32)],
+    g, e = call(
+        main_kernel, [((2, 16, BR, C), f32, 1), ((8, C), f32, 1)],
         [
             pltpu.VMEM((264, 128), f32),
             pltpu.VMEM((264, 128), f32),
@@ -491,24 +495,23 @@
             pltpu.VMEM((64, C), f32),
             pltpu.VMEM((264, 128), f32),
             pltpu.VMEM((M, C), f32),
-            pltpu.VMEM((2, 16, BR, C), f32),
-            pltpu.SemaphoreType.DMA((2,)),
         ],
         (n2, n1, win, s1, s2, seeds, w_in, w_mid, w_out, w_noise),
-        {("out", 0), ("out", 1)},
-    )
-    half, far = sum_all(mine, theirs, e)
+        kept=(0, 1, 2, 3, 4, 5, 6, 8, 9),
+        limit=32,
+    )
+    half, far = sum_all(g[0], g[1], e)
     o_in, o_mid, o_out, o_noise, o_loss = call(
         final_kernel,
         [((9, V, C), f32), ((9, C, C), f32), ((V, C), f32), ((NB, C), f32), ((1, 128), f32)],
         [
             pltpu.VMEM((NB, BR, C), f32),
             pltpu.VMEM((9, C, C), f32),
-            pltpu.SemaphoreType.DMA((8,)),
             pltpu.SemaphoreType.DMA((9,)),
         ],
         (half, far),
-        {("in", 0), ("in", 1), ("out", 1)},
+        {("out", 1)},
+        kept=(0, 1),
     )
     return o_in, o_mid, o_out, o_noise, o_loss[0, 0]
 

time: 121 us -> 120 us (level); the launches traced: 119 us -> 120 us
  Pallas kernels: 27.9 us -> 19.7 us
  other arithmetic: 6.12 us -> 1.39 us
  local copies, waits for them, and re-layouts: 1.3 us -> 5.95 us
  waiting for transfers between devices: 24.2 us -> 28.7 us
  blocking collectives: 31.6 us -> 35.2 us
    pallas_call x4, Pallas kernels: 27.9 us -> 19.7 us  [call(): pl.pallas_call(kernel, out_shape=[pltpu.VMEM(o[0], o[1]) if len(o) > 2 el...]
    unnamed x13 -> x17, local copies, waits for them, and re-layouts: 1.24 us -> 5.75 us
    convert_element_type x2, other arithmetic: 2.87 us -> 0.35 us  [sum_all(): return (half.astype(f32), far.astype(f32))]
    all_to_all x1, blocking collectives: 14.6 us -> 17.1 us  [sum_all(): lax.all_to_all(jnp.broadcast_to(s[None], (16,) + s.shape), xy, 0, 0, tile...]
    all_to_all x1, waiting for transfers between devices: 3.81 us -> 6.14 us  [body(): seeds = lax.all_to_all(seeds, ('z', 'xl'), 0, 0, tiled=True)]
    ppermute x12, waiting for transfers between devices: 20.3 us -> 22.6 us  [send(): return lax.ppermute(v, AX, perm(f))]
    convert_element_type x1, other arithmetic: 1.95 us -> 0.44 us  [sum_all(): got = lax.all_to_all(s.astype(f16), xy, 0, 0, tiled=True)]
  transfers between devices with their start and end apart: 13 -> 13, of which waited for: 9 -> 7; matrix products, arithmetic and copies ran while one was open for 2% -> 0% of each run, Pallas kernels for 1% -> 0%
where the time goes in v5:
time: 120 us
  blocking collectives  35.2 us (29%)
  waiting for transfers between devices  28.7 us (24%)
  starting transfers between devices  28 us (23%)
  Pallas kernels  19.7 us (16%)
  local copies, waits for them, and re-layouts  5.95 us (5%)
  other arithmetic  1.39 us (1%)
    ppermute x12, waiting for transfers between devices, send(): return lax.ppermute(v, AX, perm(f))  22.6 us
    ppermute x12, starting transfers between devices, send(): return lax.ppermute(v, AX, perm(f))  19.9 us
    pallas_call x4, Pallas kernels, call(): pl.pallas_call(kernel, out_shape=[pltpu.VMEM(o[0], o[1]) if len(o) > 2 el...  19.7 us
    all_to_all x1, blocking collectives, sum_all(): got = lax.all_to_all(s.astype(f16), xy, 0, 0, tiled=True)  18.1 us
    all_to_all x1, blocking collectives, sum_all(): lax.all_to_all(jnp.broadcast_to(s[None], (16,) + s.shape), xy, 0, 0, tile...  17.1 us
    all_to_all x1, starting transfers between devices, body(): seeds = lax.all_to_all(seeds, ('z', 'xl'), 0, 0, tiled=True)  8.05 us
    all_to_all x1, waiting for transfers between devices, body(): seeds = lax.all_to_all(seeds, ('z', 'xl'), 0, 0, tiled=True)  6.14 us
    unnamed x17, local copies, waits for them, and re-layouts  5.75 us
  transfers between devices with their start and end apart: 13, of which 7 were waited for; matrix products, arithmetic and copies ran while one was open for 0% of the time, Pallas kernels for 0%

profile of v5, /device:TPU:33, one launch (start us, length us, event | category | flops | bytes accessed | tf_op | source)
XLA Modules:
  0.0 119.7 jit_solution(6496679038770937302)
XLA Ops:
  0.6 0.0 copy-start.1
  0.6 1.0 copy-done.1
  1.7 0.9 copy-done.2
  2.6 0.9 copy-done.3
  3.5 0.8 copy-done.4
  4.3 0.8 copy-done.5
  5.1 0.7 copy-done.6
  5.7 0.7 copy-done.7
  6.4 1.5 %shard_map.119 = (f32[2,384,256]{2,1,0:T(8,128)S(1)}, f32[32,256]{1,0:T(8,128)S(1)}, s32[16,32]{1,0:T(8,128)}, bf16[9,100,256]{2,1,0:T(8,128)(2,1)S(1)}, bf16[10...) custom-call(bf16[100,2,360]{2,1,0:T(2,128)(2,1)S(1)} %copy-done.2, bf16[100,2,360]{2,1,0:T(2,128)(2,1)S(1)} %copy-done.3, ...), custom_call_target="tpu_custom_call" | custom-call | tf_op jit(solution)/shard_map/pallas_call | solution.py:424
  7.9 2.8 %collective-permute-start = (f32[32,256]{1,0:T(8,128)S(1)}, f32[32,256]{1,0:T(8,128)S(1)}, u32[]{:S(2)}, u32[]{:S(2)}) collective-permute-start(f32[32,256]{1,0:T(8,128)S(1)} %get-tuple-element.21), channel_id=1, source_target_pairs={{0,1},{1,0},{2,3},{3,2},{4,5},{5,4},{6,7},{7,6},{8,9},{9,8},{10,11... | collective-permute-start | bytes 98312 | tf_op jit(solution)/shard_map/ppermute | solution.py:35
  10.7 8.1 %all-to-all-start = ((s32[16,1,32]{2,1,0:T(1,128)}), s32[16,1,32]{2,1,0:T(1,128)S(1)}, u32[]{:S(2)}, u32[]{:S(2)}) async-start(s32[16,1,32]{2,1,0:T(1,128)} %bitcast.1), calls=%async_computation | async-start | bytes 16384 | tf_op jit(solution)/shard_map/all_to_all | solution.py:476
  18.8 0.0 collective-permute-done.edge
  18.8 0.1 shard_map.120.own
  18.8 6.1 %all-to-all-done = s32[16,1,32]{2,1,0:T(1,128)S(1)} async-done(((s32[16,1,32]{2,1,0:T(1,128)}), s32[16,1,32]{2,1,0:T(1,128)S(1)}, u32[]{:S(2)}, u32[]{:S(2)}) %all-to-all-start) | async-done | bytes 2080 | tf_op jit(solution)/shard_map/all_to_all | solution.py:476
  25.0 1.3 %collective-permute-start.1 = (bf16[64,256]{1,0:T(8,128)(2,1)S(1)}, bf16[64,256]{1,0:T(8,128)(2,1)S(1)}, u32[]{:S(2)}, u32[]{:S(2)}) collective-permute-start(bf16[64,256]{1,0:T(8,128)(2,1)S(1)} %shard_map.120.own), channel_id=1, source_target_pairs={{0,4},{1,5},{2,6},{3,7},{4,8},{5,9},{6,10},{7,11},{8,12},{9,13},{1... | collective-permute-start | bytes 98312 | tf_op jit(solution)/shard_map/ppermute | solution.py:35
  26.3 3.8 %collective-permute-start.2 = (bf16[64,256]{1,0:T(8,128)(2,1)S(1)}, bf16[64,256]{1,0:T(8,128)(2,1)S(1)}, u32[]{:S(2)}, u32[]{:S(2)}) collective-permute-start(bf16[64,256]{1,0:T(8,128)(2,1)S(1)} %shard_map.120.own), channel_id=1, source_target_pairs={{0,2},{1,3},{2,4},{3,5},{4,6},{5,7},{6,8},{7,9},{8,10},{9,11},{10,... | collective-permute-start | bytes 98312 | tf_op jit(solution)/shard_map/ppermute | solution.py:35
  30.1 0.0 collective-permute-start.3
  30.1 1.4 %collective-permute-start.4 = (bf16[64,256]{1,0:T(8,128)(2,1)S(1)}, bf16[64,256]{1,0:T(8,128)(2,1)S(1)}, u32[]{:S(2)}, u32[]{:S(2)}) collective-permute-start(bf16[64,256]{1,0:T(8,128)(2,1)S(1)} %shard_map.120.own), channel_id=1, source_target_pairs={{0,12},{1,13},{2,14},{3,15},{4,0},{5,1},{6,2},{7,3},{8,4},{9,5},{1... | collective-permute-start | bytes 98312 | tf_op jit(solution)/shard_map/ppermute | solution.py:35
  31.5 0.0 collective-permute-done.1.n2
  31.5 0.0 collective-permute-done.2.n1
  31.5 1.9 %collective-permute-done.3.s1 = bf16[64,256]{1,0:T(8,128)(2,1)S(1)} collective-permute-done((bf16[64,256]{1,0:T(8,128)(2,1)S(1)}, bf16[64,256]{1,0:T(8,128)(2,1)S(1)}, u32[]{:S(2)}, u32[]{:S(2)}) %collective-permute-start.3) | collective-permute-done | bytes 32800 | tf_op jit(solution)/shard_map/ppermute | solution.py:35
  33.5 0.0 collective-permute-done.4.s2
  33.5 15.1 %shard_map.121 = (f32[2,16,112,256]{3,2,1,0:T(8,128)S(1)}, f32[8,256]{1,0:T(8,128)S(1)}) custom-call(bf16[64,256]{1,0:T(8,128)(2,1)S(1)} %collective-permute-done.1.n2, bf16[64,256]{1,0:T(8,128)(2,1)S(1)} %collective-permute-done.2.n1, bf16[64,256]{1,0:T(8,128)(2,1)S(1)} %shard_map.120.own, bf16[64,256]{1,0:T(8,128)(2,1)S(1)} %collective-permute-done.3.s1, ...), custom_call_target="tpu_custom_call" | custom-call | tf_op jit(solution)/shard_map/pallas_call | solution.py:424
  48.6 0.1 slice_bitcast_fusion
  48.7 2.4 %collective-permute-start.5 = (f32[16,112,256]{2,1,0:T(8,128)S(1)}, f32[16,112,256]{2,1,0:T(8,128)S(1)}, u32[]{:S(2)}, u32[]{:S(2)}) collective-permute-start(f32[16,112,256]{2,1,0:T(8,128)S(1)} %slice_bitcast_fusion), channel_id=1, source_target_pairs={{0,2},{1,3},{2,0},{3,1},{4,6},{5,7},{6,4},{7,5},{8,10},{9,11},{10,... | collective-permute-start | bytes 5505032 | tf_op jit(solution)/shard_map/ppermute | solution.py:35
  51.2 0.1 collective-permute-start.6
  51.3 3.3 %collective-permute-done.6 = f32[8,256]{1,0:T(8,128)S(1)} collective-permute-done((f32[8,256]{1,0:T(8,128)S(1)}, f32[8,256]{1,0:T(8,128)S(1)}, u32[]{:S(2)}, u32[]{:S(2)}) %collective-permute-start.6) | collective-permute-done | bytes 8224 | tf_op jit(solution)/shard_map/ppermute | solution.py:35
  54.6 0.1 broadcast_select_fusion
  54.7 0.0 collective-permute-done.5
  54.7 0.4 fusion.2
  55.2 18.1 %all_to_all.22 = f16[16,112,256]{2,1,0:T(8,128)(2,1)S(1)} all-to-all(f16[16,112,256]{2,1,0:T(8,128)(2,1)S(1)} %fusion.2), channel_id=1, replica_groups=mesh['z'=8,'xl'=2,'y'=4,'c'=2,'xh'=2] {'xl','y','xh'}, dimensions={0} | all-to-all | bytes 1835008 | tf_op jit(solution)/shard_map/all_to_all | solution.py:449
  73.3 0.3 multiply_reduce_fusion
  73.6 0.4 collective-permute-start.8
  74.0 2.1 %collective-permute-start.9 = (f32[112,256]{1,0:T(8,128)S(1)}, f32[112,256]{1,0:T(8,128)S(1)}, u32[]{:S(2)}, u32[]{:S(2)}) collective-permute-start(f32[112,256]{1,0:T(8,128)S(1)} %multiply_reduce_fusion), channel_id=1, source_target_pairs={{0,96},{1,97},{2,98},{3,99},{4,100},{5,101},{6,102},{7,103},{8,104... | collective-permute-start | bytes 344072 | tf_op jit(solution)/shard_map/ppermute | solution.py:35
  76.1 1.2 collective-permute-start.7
  77.3 1.1 collective-permute-done.8
  78.4 8.4 %collective-permute-done.9 = f32[112,256]{1,0:T(8,128)S(1)} collective-permute-done((f32[112,256]{1,0:T(8,128)S(1)}, f32[112,256]{1,0:T(8,128)S(1)}, u32[]{:S(2)}, u32[]{:S(2)}) %collective-permute-start.9) | collective-permute-done | bytes 114720 | tf_op jit(solution)/shard_map/ppermute | solution.py:35
  86.8 0.0 collective-permute-done.7
  86.9 1.3 %collective-permute-start.10 = (f32[112,256]{1,0:T(8,128)S(1)}, f32[112,256]{1,0:T(8,128)S(1)}, u32[]{:S(2)}, u32[]{:S(2)}) collective-permute-start(f32[112,256]{1,0:T(8,128)S(1)} %add_add_fusion), channel_id=1, source_target_pairs={{0,224},{1,225},{2,226},{3,227},{4,228},{5,229},{6,230},{7,231},{8... | collective-permute-start | bytes 344072 | tf_op jit(solution)/shard_map/ppermute | solution.py:35
  88.1 5.9 %collective-permute-done.10 = f32[112,256]{1,0:T(8,128)S(1)} collective-permute-done((f32[112,256]{1,0:T(8,128)S(1)}, f32[112,256]{1,0:T(8,128)S(1)}, u32[]{:S(2)}, u32[]{:S(2)}) %collective-permute-start.10) | collective-permute-done | bytes 114720 | tf_op jit(solution)/shard_map/ppermute | solution.py:35
  94.0 0.1 select_convert_fusion
  94.1 0.1 broadcast_in_dim.66
  94.2 17.1 %all_to_all.23 = f16[16,112,256]{2,1,0:T(8,128)(2,1)S(1)} all-to-all(f16[16,112,256]{2,1,0:T(8,128)(2,1)S(1)} %broadcast_in_dim.66), channel_id=1, replica_groups=mesh['z'=8,'xl'=2,'y'=4,'c'=2,'xh'=2] {'xl','y','xh'}, dimensions={0} | all-to-all | bytes 1835008 | tf_op jit(solution)/shard_map/all_to_all | solution.py:459
  111.3 3.1 %collective-permute-start.11 = (f16[16,112,256]{2,1,0:T(8,128)(2,1)S(1)}, f16[16,112,256]{2,1,0:T(8,128)(2,1)S(1)}, u32[]{:S(2)}, u32[]{:S(2)}) collective-permute-start(f16[16,112,256]{2,1,0:T(8,128)(2,1)S(1)} %all_to_all.23), channel_id=1, source_target_pairs={{0,2},{1,3},{2,0},{3,1},{4,6},{5,7},{6,4},{7,5},{8,10},{9,11},{10,... | collective-permute-start | bytes 2752520 | tf_op jit(solution)/shard_map/ppermute | solution.py:35
  114.4 0.2 convert_element_type.22.half
  114.6 1.9 %collective-permute-done.11 = f16[16,112,256]{2,1,0:T(8,128)(2,1)S(1)} collective-permute-done((f16[16,112,256]{2,1,0:T(8,128)(2,1)S(1)}, f16[16,112,256]{2,1,0:T(8,128)(2,1)S(1)}, u32[]{:S(2)}, u32[]{:S(2)}) %collective-permute-start.11) | collective-permute-done | bytes 917536 | tf_op jit(solution)/shard_map/ppermute | solution.py:35
  116.5 0.2 convert_element_type.23.far
  116.7 3.0 %shard_map.122 = (f32[9,100,256]{2,1,0:T(8,128)}, f32[9,256,256]{2,1,0:T(8,128)}, f32[100,256]{1,0:T(8,128)}, f32[32,256]{1,0:T(8,128)}, f32[1,128]{1,0:T(1,128)}) custom-call(f32[16,112,256]{2,1,0:T(8,128)S(1)} %convert_element_type.22.half, f32[16,112,256]{2,1,0:T(8,128)S(1)} %convert_element_type.23.far), custom_call_target="tpu_custom_call" | custom-call | tf_op jit(solution)/shard_map/pallas_call | solution.py:424
  (15 shorter events, 0.1 us)
Async XLA Ops:
  0.6 1.0 copy-start.1
  1.7 0.9 copy-start.2
  2.6 0.9 copy-start.3
  3.5 0.8 copy-start.4
  4.3 0.8 copy-start.5
  5.1 0.7 copy-start.6
  5.7 0.7 copy-start.7
  6.4 27.1 %copy-start = (bf16[9,256,256]{2,1,0:T(8,128)(2,1)S(1)}, bf16[9,256,256]{2,1,0:T(8,128)(2,1)}, u32[]{:S(2)}) copy-start(bf16[9,256,256]{2,1,0:T(8,128)(2,1)} %w_mid.1) | copy-start | bytes 3538948
  7.9 10.9 %collective-permute-start = (f32[32,256]{1,0:T(8,128)S(1)}, f32[32,256]{1,0:T(8,128)S(1)}, u32[]{:S(2)}, u32[]{:S(2)}) collective-permute-start(f32[32,256]{1,0:T(8,128)S(1)} %get-tuple-element.21), channel_id=1, source_target_pairs={{0,1},{1,0},{2,3},{3,2},{4,5},{5,4},{6,7},{7,6},{8,9},{9,8},{10,11... | collective-permute-start | bytes 98312 | tf_op jit(solution)/shard_map/ppermute | solution.py:35
  10.7 14.3 %all-to-all-start = ((s32[16,1,32]{2,1,0:T(1,128)}), s32[16,1,32]{2,1,0:T(1,128)S(1)}, u32[]{:S(2)}, u32[]{:S(2)}) async-start(s32[16,1,32]{2,1,0:T(1,128)} %bitcast.1), calls=%async_computation | async-start | bytes 16384 | tf_op jit(solution)/shard_map/all_to_all | solution.py:476
  25.0 6.6 %collective-permute-start.1 = (bf16[64,256]{1,0:T(8,128)(2,1)S(1)}, bf16[64,256]{1,0:T(8,128)(2,1)S(1)}, u32[]{:S(2)}, u32[]{:S(2)}) collective-permute-start(bf16[64,256]{1,0:T(8,128)(2,1)S(1)} %shard_map.120.own), channel_id=1, source_target_pairs={{0,4},{1,5},{2,6},{3,7},{4,8},{5,9},{6,10},{7,11},{8,12},{9,13},{1... | collective-permute-start | bytes 98312 | tf_op jit(solution)/shard_map/ppermute | solution.py:35
  26.3 5.3 %collective-permute-start.2 = (bf16[64,256]{1,0:T(8,128)(2,1)S(1)}, bf16[64,256]{1,0:T(8,128)(2,1)S(1)}, u32[]{:S(2)}, u32[]{:S(2)}) collective-permute-start(bf16[64,256]{1,0:T(8,128)(2,1)S(1)} %shard_map.120.own), channel_id=1, source_target_pairs={{0,2},{1,3},{2,4},{3,5},{4,6},{5,7},{6,8},{7,9},{8,10},{9,11},{10,... | collective-permute-start | bytes 98312 | tf_op jit(solution)/shard_map/ppermute | solution.py:35
  30.1 3.3 %collective-permute-start.3 = (bf16[64,256]{1,0:T(8,128)(2,1)S(1)}, bf16[64,256]{1,0:T(8,128)(2,1)S(1)}, u32[]{:S(2)}, u32[]{:S(2)}) collective-permute-start(bf16[64,256]{1,0:T(8,128)(2,1)S(1)} %shard_map.120.own), channel_id=1, source_target_pairs={{0,14},{1,15},{2,0},{3,1},{4,2},{5,3},{6,4},{7,5},{8,6},{9,7},{10,... | collective-permute-start | bytes 98312 | tf_op jit(solution)/shard_map/ppermute | solution.py:35
  30.1 3.3 %collective-permute-start.4 = (bf16[64,256]{1,0:T(8,128)(2,1)S(1)}, bf16[64,256]{1,0:T(8,128)(2,1)S(1)}, u32[]{:S(2)}, u32[]{:S(2)}) collective-permute-start(bf16[64,256]{1,0:T(8,128)(2,1)S(1)} %shard_map.120.own), channel_id=1, source_target_pairs={{0,12},{1,13},{2,14},{3,15},{4,0},{5,1},{6,2},{7,3},{8,4},{9,5},{1... | collective-permute-start | bytes 98312 | tf_op jit(solution)/shard_map/ppermute | solution.py:35
  48.7 6.0 %collective-permute-start.5 = (f32[16,112,256]{2,1,0:T(8,128)S(1)}, f32[16,112,256]{2,1,0:T(8,128)S(1)}, u32[]{:S(2)}, u32[]{:S(2)}) collective-permute-start(f32[16,112,256]{2,1,0:T(8,128)S(1)} %slice_bitcast_fusion), channel_id=1, source_target_pairs={{0,2},{1,3},{2,0},{3,1},{4,6},{5,7},{6,4},{7,5},{8,10},{9,11},{10,... | collective-permute-start | bytes 5505032 | tf_op jit(solution)/shard_map/ppermute | solution.py:35
  51.2 3.4 %collective-permute-start.6 = (f32[8,256]{1,0:T(8,128)S(1)}, f32[8,256]{1,0:T(8,128)S(1)}, u32[]{:S(2)}, u32[]{:S(2)}) collective-permute-start(f32[8,256]{1,0:T(8,128)S(1)} %get-tuple-element.29), channel_id=1, source_target_pairs={{0,2},{1,3},{2,0},{3,1},{4,6},{5,7},{6,4},{7,5},{8,10},{9,11},{10,... | collective-permute-start | bytes 24584 | tf_op jit(solution)/shard_map/ppermute | solution.py:35
  73.6 4.7 %collective-permute-start.8 = (f32[112,256]{1,0:T(8,128)S(1)}, f32[112,256]{1,0:T(8,128)S(1)}, u32[]{:S(2)}, u32[]{:S(2)}) collective-permute-start(f32[112,256]{1,0:T(8,128)S(1)} %multiply_reduce_fusion), channel_id=1, source_target_pairs={{0,64},{1,65},{2,66},{3,67},{4,68},{5,69},{6,70},{7,71},{8,72},{9,... | collective-permute-start | bytes 344072 | tf_op jit(solution)/shard_map/ppermute | solution.py:35
  74.0 12.8 %collective-permute-start.9 = (f32[112,256]{1,0:T(8,128)S(1)}, f32[112,256]{1,0:T(8,128)S(1)}, u32[]{:S(2)}, u32[]{:S(2)}) collective-permute-start(f32[112,256]{1,0:T(8,128)S(1)} %multiply_reduce_fusion), channel_id=1, source_target_pairs={{0,96},{1,97},{2,98},{3,99},{4,100},{5,101},{6,102},{7,103},{8,104... | collective-permute-start | bytes 344072 | tf_op jit(solution)/shard_map/ppermute | solution.py:35
  76.1 10.7 %collective-permute-start.7 = (f32[112,256]{1,0:T(8,128)S(1)}, f32[112,256]{1,0:T(8,128)S(1)}, u32[]{:S(2)}, u32[]{:S(2)}) collective-permute-start(f32[112,256]{1,0:T(8,128)S(1)} %multiply_reduce_fusion), channel_id=1, source_target_pairs={{0,32},{1,33},{2,34},{3,35},{4,36},{5,37},{6,38},{7,39},{8,40},{9,... | collective-permute-start | bytes 344072 | tf_op jit(solution)/shard_map/ppermute | solution.py:35
  86.9 7.1 %collective-permute-start.10 = (f32[112,256]{1,0:T(8,128)S(1)}, f32[112,256]{1,0:T(8,128)S(1)}, u32[]{:S(2)}, u32[]{:S(2)}) collective-permute-start(f32[112,256]{1,0:T(8,128)S(1)} %add_add_fusion), channel_id=1, source_target_pairs={{0,224},{1,225},{2,226},{3,227},{4,228},{5,229},{6,230},{7,231},{8... | collective-permute-start | bytes 344072 | tf_op jit(solution)/shard_map/ppermute | solution.py:35
  111.3 5.2 %collective-permute-start.11 = (f16[16,112,256]{2,1,0:T(8,128)(2,1)S(1)}, f16[16,112,256]{2,1,0:T(8,128)(2,1)S(1)}, u32[]{:S(2)}, u32[]{:S(2)}) collective-permute-start(f16[16,112,256]{2,1,0:T(8,128)(2,1)S(1)} %all_to_all.23), channel_id=1, source_target_pairs={{0,2},{1,3},{2,0},{3,1},{4,6},{5,7},{6,4},{7,5},{8,10},{9,11},{10,... | collective-permute-start | bytes 2752520 | tf_op jit(solution)/shard_map/ppermute | solution.py:35

commit v6 on v5

--- a/solution.py
+++ b/solution.py
@@ -236,14 +236,14 @@
     lane = lax.broadcasted_iota(jnp.int32, (M, 128), 1)
     loss = jnp.sum(jnp.sum(jnp.where(lane < V, loss, 0.0), axis=0, keepdims=True), axis=1, keepdims=True)
 
-    def up_row(r, carry):
-        base = pl.multiple_of(r * NR, M)
-        up = jnp.dot(DO[pl.ds(base, NR), 0:V], w_out[...], preferred_element_type=f32)
-        UP[pl.ds(base, NR), :] = up
-        DM[pl.ds(base, NR), :] = (up * SL[pl.ds(base, NR), :]).astype(bf16)
+    UP[...] = jnp.dot(DO[:, 0:V], w_out[...], preferred_element_type=f32)
+
+    def mid_cell(i, carry):
+        at = pl.multiple_of(i * 2 * M, M)
+        DM[pl.ds(at, 2 * M), :] = (UP[pl.ds(at, 2 * M), :] * SL[pl.ds(at, 2 * M), :]).astype(bf16)
         return carry
 
-    lax.fori_loop(0, 4, up_row, 0)
+    lax.fori_loop(0, 54, mid_cell, 0, unroll=6)
     DM[108 * M : 112 * M, :] = jnp.zeros((4 * M, C), bf16)
 
     wcat = jnp.concatenate([w_mid[t] for t in range(9)], axis=1)
@@ -418,7 +418,7 @@
     vmem = pl.BlockSpec(memory_space=pltpu.VMEM)
     left = pl.BlockSpec(memory_space=pl.ANY)
     ins = [
-        pltpu.with_memory_space_constraint(v, pltpu.VMEM) if i in kept else v
+        pltpu.with_memory_space_constraint(v, pltpu.VMEM if i in kept else pltpu.HBM)
         for i, v in enumerate(ins)
     ]
     return pl.pallas_call(
@@ -497,7 +497,7 @@
             pltpu.VMEM((M, C), f32),
         ],
         (n2, n1, win, s1, s2, seeds, w_in, w_mid, w_out, w_noise),
-        kept=(0, 1, 2, 3, 4, 5, 6, 8, 9),
+        kept=range(10),
         limit=32,
     )
     half, far = sum_all(g[0], g[1], e)

time: 120 us -> 116 us (0.967)
  local copies, waits for them, and re-layouts: 5.95 us -> 0.21 us
  Pallas kernels: 19.7 us -> 21.1 us
    unnamed x17 -> x3, local copies, waits for them, and re-layouts: 5.75 us -> 0.01 us
    pallas_call x4, Pallas kernels: 19.7 us -> 21.1 us  [call(): pl.pallas_call(kernel, out_shape=[pltpu.VMEM(o[0], o[1]) if len(o) > 2 el...]
where the time goes in v6:
time: 116 us; the launch traced here: 115 us
  blocking collectives  35.2 us (30%)
  waiting for transfers between devices  28.7 us (25%)
  starting transfers between devices  27.9 us (24%)
  Pallas kernels  21.1 us (18%)
  other arithmetic  1.39 us (1%)
    ppermute x12, waiting for transfers between devices, send(): return lax.ppermute(v, AX, perm(f))  22.6 us
    pallas_call x4, Pallas kernels, call(): pl.pallas_call(kernel, out_shape=[pltpu.VMEM(o[0], o[1]) if len(o) > 2 el...  21.1 us
    ppermute x12, starting transfers between devices, send(): return lax.ppermute(v, AX, perm(f))  19.9 us
    all_to_all x1, blocking collectives, sum_all(): got = lax.all_to_all(s.astype(f16), xy, 0, 0, tiled=True)  18.1 us
    all_to_all x1, blocking collectives, sum_all(): lax.all_to_all(jnp.broadcast_to(s[None], (16,) + s.shape), xy, 0, 0, tile...  17.1 us
    all_to_all x1, starting transfers between devices, body(): seeds = lax.all_to_all(seeds, ('z', 'xl'), 0, 0, tiled=True)  8.05 us
    all_to_all x1, waiting for transfers between devices, body(): seeds = lax.all_to_all(seeds, ('z', 'xl'), 0, 0, tiled=True)  6.14 us
  transfers between devices with their start and end apart: 13, of which 7 were waited for; matrix products, arithmetic and copies ran while one was open for 0% of the time, Pallas kernels for 0%

profile of v6, /device:TPU:33, one launch (start us, length us, event | category | flops | bytes accessed | tf_op | source)
XLA Modules:
  0.0 115.3 jit_solution(16206915258115668577)
XLA Ops:
  0.6 0.0 copy-start
  0.6 2.7 %shard_map.119 = (f32[2,384,256]{2,1,0:T(8,128)S(1)}, f32[32,256]{1,0:T(8,128)S(1)}, s32[16,32]{1,0:T(8,128)}, bf16[9,100,256]{2,1,0:T(8,128)(2,1)S(1)}, bf16[10...) custom-call(bf16[100,2,360]{2,1,0:T(2,128)(2,1)} %state.1, bf16[100,2,360]{2,1,0:T(2,128)(2,1)} %target.1, s32[2,360]{1,0:T(2,128)} %land.1, ...), custom_call_target="tpu_custom_call" | custom-call | tf_op jit(solution)/shard_map/pallas_call | solution.py:424
  3.4 2.8 %collective-permute-start = (f32[32,256]{1,0:T(8,128)S(1)}, f32[32,256]{1,0:T(8,128)S(1)}, u32[]{:S(2)}, u32[]{:S(2)}) collective-permute-start(f32[32,256]{1,0:T(8,128)S(1)} %get-tuple-element.21), channel_id=1, source_target_pairs={{0,1},{1,0},{2,3},{3,2},{4,5},{5,4},{6,7},{7,6},{8,9},{9,8},{10,11... | collective-permute-start | bytes 98312 | tf_op jit(solution)/shard_map/ppermute | solution.py:35
  6.2 8.1 %all-to-all-start = ((s32[16,1,32]{2,1,0:T(1,128)}), s32[16,1,32]{2,1,0:T(1,128)S(1)}, u32[]{:S(2)}, u32[]{:S(2)}) async-start(s32[16,1,32]{2,1,0:T(1,128)} %bitcast.1), calls=%async_computation | async-start | bytes 16384 | tf_op jit(solution)/shard_map/all_to_all | solution.py:476
  14.3 0.0 collective-permute-done.edge
  14.3 0.1 shard_map.120.own
  14.4 6.1 %all-to-all-done = s32[16,1,32]{2,1,0:T(1,128)S(1)} async-done(((s32[16,1,32]{2,1,0:T(1,128)}), s32[16,1,32]{2,1,0:T(1,128)S(1)}, u32[]{:S(2)}, u32[]{:S(2)}) %all-to-all-start) | async-done | bytes 2080 | tf_op jit(solution)/shard_map/all_to_all | solution.py:476
  20.5 1.3 %collective-permute-start.1 = (bf16[64,256]{1,0:T(8,128)(2,1)S(1)}, bf16[64,256]{1,0:T(8,128)(2,1)S(1)}, u32[]{:S(2)}, u32[]{:S(2)}) collective-permute-start(bf16[64,256]{1,0:T(8,128)(2,1)S(1)} %shard_map.120.own), channel_id=1, source_target_pairs={{0,4},{1,5},{2,6},{3,7},{4,8},{5,9},{6,10},{7,11},{8,12},{9,13},{1... | collective-permute-start | bytes 98312 | tf_op jit(solution)/shard_map/ppermute | solution.py:35
  21.8 3.8 %collective-permute-start.2 = (bf16[64,256]{1,0:T(8,128)(2,1)S(1)}, bf16[64,256]{1,0:T(8,128)(2,1)S(1)}, u32[]{:S(2)}, u32[]{:S(2)}) collective-permute-start(bf16[64,256]{1,0:T(8,128)(2,1)S(1)} %shard_map.120.own), channel_id=1, source_target_pairs={{0,2},{1,3},{2,4},{3,5},{4,6},{5,7},{6,8},{7,9},{8,10},{9,11},{10,... | collective-permute-start | bytes 98312 | tf_op jit(solution)/shard_map/ppermute | solution.py:35
  25.6 0.0 collective-permute-start.3
  25.6 1.4 %collective-permute-start.4 = (bf16[64,256]{1,0:T(8,128)(2,1)S(1)}, bf16[64,256]{1,0:T(8,128)(2,1)S(1)}, u32[]{:S(2)}, u32[]{:S(2)}) collective-permute-start(bf16[64,256]{1,0:T(8,128)(2,1)S(1)} %shard_map.120.own), channel_id=1, source_target_pairs={{0,12},{1,13},{2,14},{3,15},{4,0},{5,1},{6,2},{7,3},{8,4},{9,5},{1... | collective-permute-start | bytes 98312 | tf_op jit(solution)/shard_map/ppermute | solution.py:35
  27.1 0.0 collective-permute-done.1.n2
  27.1 0.0 collective-permute-done.2.n1
  27.1 1.9 %collective-permute-done.3.s1 = bf16[64,256]{1,0:T(8,128)(2,1)S(1)} collective-permute-done((bf16[64,256]{1,0:T(8,128)(2,1)S(1)}, bf16[64,256]{1,0:T(8,128)(2,1)S(1)}, u32[]{:S(2)}, u32[]{:S(2)}) %collective-permute-start.3) | collective-permute-done | bytes 32800 | tf_op jit(solution)/shard_map/ppermute | solution.py:35
  29.0 0.0 collective-permute-done.4.s2
  29.0 0.0 copy-done
  29.0 15.3 %shard_map.121 = (f32[2,16,112,256]{3,2,1,0:T(8,128)S(1)}, f32[8,256]{1,0:T(8,128)S(1)}) custom-call(bf16[64,256]{1,0:T(8,128)(2,1)S(1)} %collective-permute-done.1.n2, bf16[64,256]{1,0:T(8,128)(2,1)S(1)} %collective-permute-done.2.n1, bf16[64,256]{1,0:T(8,128)(2,1)S(1)} %shard_map.120.own, bf16[64,256]{1,0:T(8,128)(2,1)S(1)} %collective-permute-done.3.s1, ...), custom_call_target="tpu_custom_call" | custom-call | tf_op jit(solution)/shard_map/pallas_call | solution.py:424
  44.2 0.1 slice_bitcast_fusion
  44.4 2.4 %collective-permute-start.5 = (f32[16,112,256]{2,1,0:T(8,128)S(1)}, f32[16,112,256]{2,1,0:T(8,128)S(1)}, u32[]{:S(2)}, u32[]{:S(2)}) collective-permute-start(f32[16,112,256]{2,1,0:T(8,128)S(1)} %slice_bitcast_fusion), channel_id=1, source_target_pairs={{0,2},{1,3},{2,0},{3,1},{4,6},{5,7},{6,4},{7,5},{8,10},{9,11},{10,... | collective-permute-start | bytes 5505032 | tf_op jit(solution)/shard_map/ppermute | solution.py:35
  46.8 0.1 collective-permute-start.6
  46.9 3.3 %collective-permute-done.6 = f32[8,256]{1,0:T(8,128)S(1)} collective-permute-done((f32[8,256]{1,0:T(8,128)S(1)}, f32[8,256]{1,0:T(8,128)S(1)}, u32[]{:S(2)}, u32[]{:S(2)}) %collective-permute-start.6) | collective-permute-done | bytes 8224 | tf_op jit(solution)/shard_map/ppermute | solution.py:35
  50.2 0.1 broadcast_select_fusion
  50.3 0.0 collective-permute-done.5
  50.4 0.4 fusion.2
  50.8 18.1 %all_to_all.22 = f16[16,112,256]{2,1,0:T(8,128)(2,1)S(1)} all-to-all(f16[16,112,256]{2,1,0:T(8,128)(2,1)S(1)} %fusion.2), channel_id=1, replica_groups=mesh['z'=8,'xl'=2,'y'=4,'c'=2,'xh'=2] {'xl','y','xh'}, dimensions={0} | all-to-all | bytes 1835008 | tf_op jit(solution)/shard_map/all_to_all | solution.py:449
  69.0 0.3 multiply_reduce_fusion
  69.3 0.4 collective-permute-start.8
  69.7 2.0 %collective-permute-start.9 = (f32[112,256]{1,0:T(8,128)S(1)}, f32[112,256]{1,0:T(8,128)S(1)}, u32[]{:S(2)}, u32[]{:S(2)}) collective-permute-start(f32[112,256]{1,0:T(8,128)S(1)} %multiply_reduce_fusion), channel_id=1, source_target_pairs={{0,96},{1,97},{2,98},{3,99},{4,100},{5,101},{6,102},{7,103},{8,104... | collective-permute-start | bytes 344072 | tf_op jit(solution)/shard_map/ppermute | solution.py:35
  71.7 1.2 %collective-permute-start.7 = (f32[112,256]{1,0:T(8,128)S(1)}, f32[112,256]{1,0:T(8,128)S(1)}, u32[]{:S(2)}, u32[]{:S(2)}) collective-permute-start(f32[112,256]{1,0:T(8,128)S(1)} %multiply_reduce_fusion), channel_id=1, source_target_pairs={{0,32},{1,33},{2,34},{3,35},{4,36},{5,37},{6,38},{7,39},{8,40},{9,... | collective-permute-start | bytes 344072 | tf_op jit(solution)/shard_map/ppermute | solution.py:35
  72.9 1.1 collective-permute-done.8
  74.0 8.4 %collective-permute-done.9 = f32[112,256]{1,0:T(8,128)S(1)} collective-permute-done((f32[112,256]{1,0:T(8,128)S(1)}, f32[112,256]{1,0:T(8,128)S(1)}, u32[]{:S(2)}, u32[]{:S(2)}) %collective-permute-start.9) | collective-permute-done | bytes 114720 | tf_op jit(solution)/shard_map/ppermute | solution.py:35
  82.5 0.0 collective-permute-done.7
  82.5 1.3 %collective-permute-start.10 = (f32[112,256]{1,0:T(8,128)S(1)}, f32[112,256]{1,0:T(8,128)S(1)}, u32[]{:S(2)}, u32[]{:S(2)}) collective-permute-start(f32[112,256]{1,0:T(8,128)S(1)} %add_add_fusion), channel_id=1, source_target_pairs={{0,224},{1,225},{2,226},{3,227},{4,228},{5,229},{6,230},{7,231},{8... | collective-permute-start | bytes 344072 | tf_op jit(solution)/shard_map/ppermute | solution.py:35
  83.8 5.9 %collective-permute-done.10 = f32[112,256]{1,0:T(8,128)S(1)} collective-permute-done((f32[112,256]{1,0:T(8,128)S(1)}, f32[112,256]{1,0:T(8,128)S(1)}, u32[]{:S(2)}, u32[]{:S(2)}) %collective-permute-start.10) | collective-permute-done | bytes 114720 | tf_op jit(solution)/shard_map/ppermute | solution.py:35
  89.7 0.1 select_convert_fusion
  89.8 0.1 broadcast_in_dim.66
  89.8 17.1 %all_to_all.23 = f16[16,112,256]{2,1,0:T(8,128)(2,1)S(1)} all-to-all(f16[16,112,256]{2,1,0:T(8,128)(2,1)S(1)} %broadcast_in_dim.66), channel_id=1, replica_groups=mesh['z'=8,'xl'=2,'y'=4,'c'=2,'xh'=2] {'xl','y','xh'}, dimensions={0} | all-to-all | bytes 1835008 | tf_op jit(solution)/shard_map/all_to_all | solution.py:459
  106.9 3.1 %collective-permute-start.11 = (f16[16,112,256]{2,1,0:T(8,128)(2,1)S(1)}, f16[16,112,256]{2,1,0:T(8,128)(2,1)S(1)}, u32[]{:S(2)}, u32[]{:S(2)}) collective-permute-start(f16[16,112,256]{2,1,0:T(8,128)(2,1)S(1)} %all_to_all.23), channel_id=1, source_target_pairs={{0,2},{1,3},{2,0},{3,1},{4,6},{5,7},{6,4},{7,5},{8,10},{9,11},{10,... | collective-permute-start | bytes 2752520 | tf_op jit(solution)/shard_map/ppermute | solution.py:35
  110.0 0.2 convert_element_type.22.half
  110.2 1.9 %collective-permute-done.11 = f16[16,112,256]{2,1,0:T(8,128)(2,1)S(1)} collective-permute-done((f16[16,112,256]{2,1,0:T(8,128)(2,1)S(1)}, f16[16,112,256]{2,1,0:T(8,128)(2,1)S(1)}, u32[]{:S(2)}, u32[]{:S(2)}) %collective-permute-start.11) | collective-permute-done | bytes 917536 | tf_op jit(solution)/shard_map/ppermute | solution.py:35
  112.1 0.2 convert_element_type.23.far
  112.3 3.0 %shard_map.122 = (f32[9,100,256]{2,1,0:T(8,128)}, f32[9,256,256]{2,1,0:T(8,128)}, f32[100,256]{1,0:T(8,128)}, f32[32,256]{1,0:T(8,128)}, f32[1,128]{1,0:T(1,128)}) custom-call(f32[16,112,256]{2,1,0:T(8,128)S(1)} %convert_element_type.22.half, f32[16,112,256]{2,1,0:T(8,128)S(1)} %convert_element_type.23.far), custom_call_target="tpu_custom_call" | custom-call | tf_op jit(solution)/shard_map/pallas_call | solution.py:424
  (7 shorter events, 0.1 us)
Async XLA Ops:
  0.6 28.4 %copy-start = (bf16[9,256,256]{2,1,0:T(8,128)(2,1)S(1)}, bf16[9,256,256]{2,1,0:T(8,128)(2,1)}, u32[]{:S(2)}) copy-start(bf16[9,256,256]{2,1,0:T(8,128)(2,1)} %w_mid.1) | copy-start | bytes 3538948
  3.4 10.9 %collective-permute-start = (f32[32,256]{1,0:T(8,128)S(1)}, f32[32,256]{1,0:T(8,128)S(1)}, u32[]{:S(2)}, u32[]{:S(2)}) collective-permute-start(f32[32,256]{1,0:T(8,128)S(1)} %get-tuple-element.21), channel_id=1, source_target_pairs={{0,1},{1,0},{2,3},{3,2},{4,5},{5,4},{6,7},{7,6},{8,9},{9,8},{10,11... | collective-permute-start | bytes 98312 | tf_op jit(solution)/shard_map/ppermute | solution.py:35
  6.2 14.3 %all-to-all-start = ((s32[16,1,32]{2,1,0:T(1,128)}), s32[16,1,32]{2,1,0:T(1,128)S(1)}, u32[]{:S(2)}, u32[]{:S(2)}) async-start(s32[16,1,32]{2,1,0:T(1,128)} %bitcast.1), calls=%async_computation | async-start | bytes 16384 | tf_op jit(solution)/shard_map/all_to_all | solution.py:476
  20.5 6.6 %collective-permute-start.1 = (bf16[64,256]{1,0:T(8,128)(2,1)S(1)}, bf16[64,256]{1,0:T(8,128)(2,1)S(1)}, u32[]{:S(2)}, u32[]{:S(2)}) collective-permute-start(bf16[64,256]{1,0:T(8,128)(2,1)S(1)} %shard_map.120.own), channel_id=1, source_target_pairs={{0,4},{1,5},{2,6},{3,7},{4,8},{5,9},{6,10},{7,11},{8,12},{9,13},{1... | collective-permute-start | bytes 98312 | tf_op jit(solution)/shard_map/ppermute | solution.py:35
  21.8 5.3 %collective-permute-start.2 = (bf16[64,256]{1,0:T(8,128)(2,1)S(1)}, bf16[64,256]{1,0:T(8,128)(2,1)S(1)}, u32[]{:S(2)}, u32[]{:S(2)}) collective-permute-start(bf16[64,256]{1,0:T(8,128)(2,1)S(1)} %shard_map.120.own), channel_id=1, source_target_pairs={{0,2},{1,3},{2,4},{3,5},{4,6},{5,7},{6,8},{7,9},{8,10},{9,11},{10,... | collective-permute-start | bytes 98312 | tf_op jit(solution)/shard_map/ppermute | solution.py:35
  25.6 3.3 %collective-permute-start.3 = (bf16[64,256]{1,0:T(8,128)(2,1)S(1)}, bf16[64,256]{1,0:T(8,128)(2,1)S(1)}, u32[]{:S(2)}, u32[]{:S(2)}) collective-permute-start(bf16[64,256]{1,0:T(8,128)(2,1)S(1)} %shard_map.120.own), channel_id=1, source_target_pairs={{0,14},{1,15},{2,0},{3,1},{4,2},{5,3},{6,4},{7,5},{8,6},{9,7},{10,... | collective-permute-start | bytes 98312 | tf_op jit(solution)/shard_map/ppermute | solution.py:35
  25.6 3.3 %collective-permute-start.4 = (bf16[64,256]{1,0:T(8,128)(2,1)S(1)}, bf16[64,256]{1,0:T(8,128)(2,1)S(1)}, u32[]{:S(2)}, u32[]{:S(2)}) collective-permute-start(bf16[64,256]{1,0:T(8,128)(2,1)S(1)} %shard_map.120.own), channel_id=1, source_target_pairs={{0,12},{1,13},{2,14},{3,15},{4,0},{5,1},{6,2},{7,3},{8,4},{9,5},{1... | collective-permute-start | bytes 98312 | tf_op jit(solution)/shard_map/ppermute | solution.py:35
  44.4 6.0 %collective-permute-start.5 = (f32[16,112,256]{2,1,0:T(8,128)S(1)}, f32[16,112,256]{2,1,0:T(8,128)S(1)}, u32[]{:S(2)}, u32[]{:S(2)}) collective-permute-start(f32[16,112,256]{2,1,0:T(8,128)S(1)} %slice_bitcast_fusion), channel_id=1, source_target_pairs={{0,2},{1,3},{2,0},{3,1},{4,6},{5,7},{6,4},{7,5},{8,10},{9,11},{10,... | collective-permute-start | bytes 5505032 | tf_op jit(solution)/shard_map/ppermute | solution.py:35
  46.8 3.4 %collective-permute-start.6 = (f32[8,256]{1,0:T(8,128)S(1)}, f32[8,256]{1,0:T(8,128)S(1)}, u32[]{:S(2)}, u32[]{:S(2)}) collective-permute-start(f32[8,256]{1,0:T(8,128)S(1)} %get-tuple-element.29), channel_id=1, source_target_pairs={{0,2},{1,3},{2,0},{3,1},{4,6},{5,7},{6,4},{7,5},{8,10},{9,11},{10,... | collective-permute-start | bytes 24584 | tf_op jit(solution)/shard_map/ppermute | solution.py:35
  69.3 4.7 %collective-permute-start.8 = (f32[112,256]{1,0:T(8,128)S(1)}, f32[112,256]{1,0:T(8,128)S(1)}, u32[]{:S(2)}, u32[]{:S(2)}) collective-permute-start(f32[112,256]{1,0:T(8,128)S(1)} %multiply_reduce_fusion), channel_id=1, source_target_pairs={{0,64},{1,65},{2,66},{3,67},{4,68},{5,69},{6,70},{7,71},{8,72},{9,... | collective-permute-start | bytes 344072 | tf_op jit(solution)/shard_map/ppermute | solution.py:35
  69.7 12.8 %collective-permute-start.9 = (f32[112,256]{1,0:T(8,128)S(1)}, f32[112,256]{1,0:T(8,128)S(1)}, u32[]{:S(2)}, u32[]{:S(2)}) collective-permute-start(f32[112,256]{1,0:T(8,128)S(1)} %multiply_reduce_fusion), channel_id=1, source_target_pairs={{0,96},{1,97},{2,98},{3,99},{4,100},{5,101},{6,102},{7,103},{8,104... | collective-permute-start | bytes 344072 | tf_op jit(solution)/shard_map/ppermute | solution.py:35
  71.7 10.7 %collective-permute-start.7 = (f32[112,256]{1,0:T(8,128)S(1)}, f32[112,256]{1,0:T(8,128)S(1)}, u32[]{:S(2)}, u32[]{:S(2)}) collective-permute-start(f32[112,256]{1,0:T(8,128)S(1)} %multiply_reduce_fusion), channel_id=1, source_target_pairs={{0,32},{1,33},{2,34},{3,35},{4,36},{5,37},{6,38},{7,39},{8,40},{9,... | collective-permute-start | bytes 344072 | tf_op jit(solution)/shard_map/ppermute | solution.py:35
  82.5 7.1 %collective-permute-start.10 = (f32[112,256]{1,0:T(8,128)S(1)}, f32[112,256]{1,0:T(8,128)S(1)}, u32[]{:S(2)}, u32[]{:S(2)}) collective-permute-start(f32[112,256]{1,0:T(8,128)S(1)} %add_add_fusion), channel_id=1, source_target_pairs={{0,224},{1,225},{2,226},{3,227},{4,228},{5,229},{6,230},{7,231},{8... | collective-permute-start | bytes 344072 | tf_op jit(solution)/shard_map/ppermute | solution.py:35
  106.9 5.2 %collective-permute-start.11 = (f16[16,112,256]{2,1,0:T(8,128)(2,1)S(1)}, f16[16,112,256]{2,1,0:T(8,128)(2,1)S(1)}, u32[]{:S(2)}, u32[]{:S(2)}) collective-permute-start(f16[16,112,256]{2,1,0:T(8,128)(2,1)S(1)} %all_to_all.23), channel_id=1, source_target_pairs={{0,2},{1,3},{2,0},{3,1},{4,6},{5,7},{6,4},{7,5},{8,10},{9,11},{10,... | collective-permute-start | bytes 2752520 | tf_op jit(solution)/shard_map/ppermute | solution.py:35

commit v7 on v6

--- a/solution.py
+++ b/solution.py
@@ -436,6 +436,20 @@
 f16 = jnp.float16
 
 
+def is_last():
+    return (jnp.arange(BR, dtype=jnp.int32) == BR - 1)[:, None]
+
+
+def coded(s):
+    e = exponent(s[BR - 1 : BR, :])
+    return jnp.where(is_last(), e, s * jnp.exp2(14.0 - e)).astype(f16)
+
+
+def decoded(msg):
+    q = jnp.exp2(msg[..., BR - 1 : BR, :].astype(f32) - 14.0)
+    return jnp.where(is_last(), 2.0**14, msg.astype(f32)) * q
+
+
 def sum_all(mine, theirs, e):
     xy = ("xl", "y", "xh")
 
@@ -443,19 +457,17 @@
         return (z, xl, lat ^ 1, xh)
 
     e = (jnp.maximum(e, send(e, other)) + 1.0)[0:1]
-    last = (jnp.arange(BR, dtype=jnp.int32) == BR - 1)[:, None]
-    tag = jnp.where(last, e, 0.0)
+    tag = jnp.where(is_last(), e, 0.0)
     s = (mine + send(theirs, other)) * jnp.exp2(14.0 - e)[None] + tag[None]
     got = lax.all_to_all(s.astype(f16), xy, 0, 0, tiled=True)
-    q = jnp.exp2(got[:, BR - 1 : BR, :].astype(f32) - 14.0)
-    s = jnp.sum(jnp.where(last[None], 2.0**14, got.astype(f32)) * q, axis=0)
-    r1, r2, r3 = (
-        send(s, lambda z, xl, lat, xh, k=k: (z ^ k, xl, lat, xh)) for k in (1, 2, 3)
-    )
-    s = (s + r1) + (r2 + r3)
-    s = s + send(s, lambda z, xl, lat, xh: (7 - z, xl, lat, xh))
-    e = exponent(s[BR - 1 : BR, :])
-    s = jnp.where(last, e, s * jnp.exp2(14.0 - e)).astype(f16)
+    s = jnp.sum(decoded(got), axis=0)
+    s = coded(s)
+    r0, r1, r2, r3 = (
+        decoded(send(s, lambda z, xl, lat, xh, k=k: (z ^ k, xl, lat, xh)) if k else s)
+        for k in range(4)
+    )
+    s = coded((r0 + r1) + (r2 + r3))
+    s = coded(decoded(s) + decoded(send(s, lambda z, xl, lat, xh: (7 - z, xl, lat, xh))))
     half = lax.all_to_all(jnp.broadcast_to(s[None], (16,) + s.shape), xy, 0, 0, tiled=True)
     far = send(half, other)
     return half.astype(f32), far.astype(f32)

time: 116 us -> 109 us (0.940)
  waiting for transfers between devices: 28.7 us -> 21.3 us
  blocking collectives: 35.2 us -> 32.7 us
  starting transfers between devices: 27.9 us -> 30.3 us
    ppermute x12, waiting for transfers between devices: 22.6 us -> 15.2 us  [send(): return lax.ppermute(v, AX, perm(f))]
    all_to_all x1, blocking collectives: 17.1 us -> 14.5 us  [sum_all(): lax.all_to_all(jnp.broadcast_to(s[None], (16,) + s.shape), xy, 0, 0, tile...]
    ppermute x12, starting transfers between devices: 19.9 us -> 22.3 us  [send(): return lax.ppermute(v, AX, perm(f))]
where the time goes in v7:
time: 109 us; the launch traced here: 108 us
  blocking collectives  32.7 us (30%)
  starting transfers between devices  30.3 us (28%)
  waiting for transfers between devices  21.3 us (20%)
  Pallas kernels  21.1 us (19%)
  other arithmetic  1.85 us (2%)
    ppermute x12, starting transfers between devices, send(): return lax.ppermute(v, AX, perm(f))  22.3 us
    pallas_call x4, Pallas kernels, call(): pl.pallas_call(kernel, out_shape=[pltpu.VMEM(o[0], o[1]) if len(o) > 2 el...  21.1 us
    all_to_all x1, blocking collectives, sum_all(): got = lax.all_to_all(s.astype(f16), xy, 0, 0, tiled=True)  18.1 us
    ppermute x12, waiting for transfers between devices, send(): return lax.ppermute(v, AX, perm(f))  15.2 us
    all_to_all x1, blocking collectives, sum_all(): lax.all_to_all(jnp.broadcast_to(s[None], (16,) + s.shape), xy, 0, 0, tile...  14.5 us
    all_to_all x1, starting transfers between devices, body(): seeds = lax.all_to_all(seeds, ('z', 'xl'), 0, 0, tiled=True)  8.05 us
    all_to_all x1, waiting for transfers between devices, body(): seeds = lax.all_to_all(seeds, ('z', 'xl'), 0, 0, tiled=True)  6.14 us
  transfers between devices with their start and end apart: 13, of which 7 were waited for; matrix products, arithmetic and copies ran while one was open for 0% of the time, Pallas kernels for 0%

profile of v7, /device:TPU:33, one launch (start us, length us, event | category | flops | bytes accessed | tf_op | source)
XLA Modules:
  0.0 108.4 jit_solution(3965102585417898514)
XLA Ops:
  0.6 0.0 copy-start
  0.6 2.7 %shard_map.119 = (f32[2,384,256]{2,1,0:T(8,128)S(1)}, f32[32,256]{1,0:T(8,128)S(1)}, s32[16,32]{1,0:T(8,128)}, bf16[9,100,256]{2,1,0:T(8,128)(2,1)S(1)}, bf16[10...) custom-call(bf16[100,2,360]{2,1,0:T(2,128)(2,1)} %state.1, bf16[100,2,360]{2,1,0:T(2,128)(2,1)} %target.1, s32[2,360]{1,0:T(2,128)} %land.1, ...), custom_call_target="tpu_custom_call" | custom-call | tf_op jit(solution)/shard_map/pallas_call | solution.py:424
  3.4 2.8 %collective-permute-start = (f32[32,256]{1,0:T(8,128)S(1)}, f32[32,256]{1,0:T(8,128)S(1)}, u32[]{:S(2)}, u32[]{:S(2)}) collective-permute-start(f32[32,256]{1,0:T(8,128)S(1)} %get-tuple-element.21), channel_id=1, source_target_pairs={{0,1},{1,0},{2,3},{3,2},{4,5},{5,4},{6,7},{7,6},{8,9},{9,8},{10,11... | collective-permute-start | bytes 98312 | tf_op jit(solution)/shard_map/ppermute | solution.py:35
  6.2 8.1 %all-to-all-start = ((s32[16,1,32]{2,1,0:T(1,128)}), s32[16,1,32]{2,1,0:T(1,128)S(1)}, u32[]{:S(2)}, u32[]{:S(2)}) async-start(s32[16,1,32]{2,1,0:T(1,128)} %bitcast.1), calls=%async_computation | async-start | bytes 16384 | tf_op jit(solution)/shard_map/all_to_all | solution.py:488
  14.3 0.0 collective-permute-done.edge
  14.3 0.1 shard_map.120.own
  14.4 6.1 %all-to-all-done = s32[16,1,32]{2,1,0:T(1,128)S(1)} async-done(((s32[16,1,32]{2,1,0:T(1,128)}), s32[16,1,32]{2,1,0:T(1,128)S(1)}, u32[]{:S(2)}, u32[]{:S(2)}) %all-to-all-start) | async-done | bytes 2080 | tf_op jit(solution)/shard_map/all_to_all | solution.py:488
  20.5 1.3 %collective-permute-start.1 = (bf16[64,256]{1,0:T(8,128)(2,1)S(1)}, bf16[64,256]{1,0:T(8,128)(2,1)S(1)}, u32[]{:S(2)}, u32[]{:S(2)}) collective-permute-start(bf16[64,256]{1,0:T(8,128)(2,1)S(1)} %shard_map.120.own), channel_id=1, source_target_pairs={{0,4},{1,5},{2,6},{3,7},{4,8},{5,9},{6,10},{7,11},{8,12},{9,13},{1... | collective-permute-start | bytes 98312 | tf_op jit(solution)/shard_map/ppermute | solution.py:35
  21.8 3.8 %collective-permute-start.2 = (bf16[64,256]{1,0:T(8,128)(2,1)S(1)}, bf16[64,256]{1,0:T(8,128)(2,1)S(1)}, u32[]{:S(2)}, u32[]{:S(2)}) collective-permute-start(bf16[64,256]{1,0:T(8,128)(2,1)S(1)} %shard_map.120.own), channel_id=1, source_target_pairs={{0,2},{1,3},{2,4},{3,5},{4,6},{5,7},{6,8},{7,9},{8,10},{9,11},{10,... | collective-permute-start | bytes 98312 | tf_op jit(solution)/shard_map/ppermute | solution.py:35
  25.6 0.0 collective-permute-start.3
  25.6 1.4 %collective-permute-start.4 = (bf16[64,256]{1,0:T(8,128)(2,1)S(1)}, bf16[64,256]{1,0:T(8,128)(2,1)S(1)}, u32[]{:S(2)}, u32[]{:S(2)}) collective-permute-start(bf16[64,256]{1,0:T(8,128)(2,1)S(1)} %shard_map.120.own), channel_id=1, source_target_pairs={{0,12},{1,13},{2,14},{3,15},{4,0},{5,1},{6,2},{7,3},{8,4},{9,5},{1... | collective-permute-start | bytes 98312 | tf_op jit(solution)/shard_map/ppermute | solution.py:35
  27.1 0.0 collective-permute-done.1.n2
  27.1 0.0 collective-permute-done.2.n1
  27.1 1.9 %collective-permute-done.3.s1 = bf16[64,256]{1,0:T(8,128)(2,1)S(1)} collective-permute-done((bf16[64,256]{1,0:T(8,128)(2,1)S(1)}, bf16[64,256]{1,0:T(8,128)(2,1)S(1)}, u32[]{:S(2)}, u32[]{:S(2)}) %collective-permute-start.3) | collective-permute-done | bytes 32800 | tf_op jit(solution)/shard_map/ppermute | solution.py:35
  29.0 0.0 collective-permute-done.4.s2
  29.0 0.0 copy-done
  29.0 15.3 %shard_map.121 = (f32[2,16,112,256]{3,2,1,0:T(8,128)S(1)}, f32[8,256]{1,0:T(8,128)S(1)}) custom-call(bf16[64,256]{1,0:T(8,128)(2,1)S(1)} %collective-permute-done.1.n2, bf16[64,256]{1,0:T(8,128)(2,1)S(1)} %collective-permute-done.2.n1, bf16[64,256]{1,0:T(8,128)(2,1)S(1)} %shard_map.120.own, bf16[64,256]{1,0:T(8,128)(2,1)S(1)} %collective-permute-done.3.s1, ...), custom_call_target="tpu_custom_call" | custom-call | tf_op jit(solution)/shard_map/pallas_call | solution.py:424
  44.2 0.1 slice_bitcast_fusion
  44.4 2.4 %collective-permute-start.5 = (f32[16,112,256]{2,1,0:T(8,128)S(1)}, f32[16,112,256]{2,1,0:T(8,128)S(1)}, u32[]{:S(2)}, u32[]{:S(2)}) collective-permute-start(f32[16,112,256]{2,1,0:T(8,128)S(1)} %slice_bitcast_fusion), channel_id=1, source_target_pairs={{0,2},{1,3},{2,0},{3,1},{4,6},{5,7},{6,4},{7,5},{8,10},{9,11},{10,... | collective-permute-start | bytes 5505032 | tf_op jit(solution)/shard_map/ppermute | solution.py:35
  46.8 0.1 collective-permute-start.6
  46.9 3.3 %collective-permute-done.6 = f32[8,256]{1,0:T(8,128)S(1)} collective-permute-done((f32[8,256]{1,0:T(8,128)S(1)}, f32[8,256]{1,0:T(8,128)S(1)}, u32[]{:S(2)}, u32[]{:S(2)}) %collective-permute-start.6) | collective-permute-done | bytes 8224 | tf_op jit(solution)/shard_map/ppermute | solution.py:35
  50.3 0.1 broadcast_select_fusion
  50.3 0.0 collective-permute-done.5
  50.4 0.4 fusion.2
  50.8 18.1 %all_to_all.22 = f16[16,112,256]{2,1,0:T(8,128)(2,1)S(1)} all-to-all(f16[16,112,256]{2,1,0:T(8,128)(2,1)S(1)} %fusion.2), channel_id=1, replica_groups=mesh['z'=8,'xl'=2,'y'=4,'c'=2,'xh'=2] {'xl','y','xh'}, dimensions={0} | all-to-all | bytes 1835008 | tf_op jit(solution)/shard_map/all_to_all | solution.py:462
  69.0 0.3 multiply_reduce_fusion
  69.3 0.1 select_convert_fusion.2
  69.4 0.4 collective-permute-start.9
  69.8 3.0 %collective-permute-start.8 = (f16[112,256]{1,0:T(8,128)(2,1)S(1)}, f16[112,256]{1,0:T(8,128)(2,1)S(1)}, u32[]{:S(2)}, u32[]{:S(2)}) collective-permute-start(f16[112,256]{1,0:T(8,128)(2,1)S(1)} %select_convert_fusion.2), channel_id=1, source_target_pairs={{0,64},{1,65},{2,66},{3,67},{4,68},{5,69},{6,70},{7,71},{8,72},{9,... | collective-permute-start | bytes 172040 | tf_op jit(solution)/shard_map/ppermute | solution.py:35
  72.7 0.0 collective-permute-start.7
  72.8 0.0 collective-permute-done.9
  72.8 2.2 %collective-permute-done.8 = f16[112,256]{1,0:T(8,128)(2,1)S(1)} collective-permute-done((f16[112,256]{1,0:T(8,128)(2,1)S(1)}, f16[112,256]{1,0:T(8,128)(2,1)S(1)}, u32[]{:S(2)}, u32[]{:S(2)}) %collective-permute-start.8) | collective-permute-done | bytes 57376 | tf_op jit(solution)/shard_map/ppermute | solution.py:35
  75.0 1.0 collective-permute-done.7
  76.0 0.1 add_add_fusion
  76.1 0.1 select_convert_fusion.1
  76.2 1.3 %collective-permute-start.10 = (f16[112,256]{1,0:T(8,128)(2,1)S(1)}, f16[112,256]{1,0:T(8,128)(2,1)S(1)}, u32[]{:S(2)}, u32[]{:S(2)}) collective-permute-start(f16[112,256]{1,0:T(8,128)(2,1)S(1)} %select_convert_fusion.1), channel_id=1, source_target_pairs={{0,224},{1,225},{2,226},{3,227},{4,228},{5,229},{6,230},{7,231},{8... | collective-permute-start | bytes 172040 | tf_op jit(solution)/shard_map/ppermute | solution.py:35
  77.5 4.8 %collective-permute-done.10 = f16[112,256]{1,0:T(8,128)(2,1)S(1)} collective-permute-done((f16[112,256]{1,0:T(8,128)(2,1)S(1)}, f16[112,256]{1,0:T(8,128)(2,1)S(1)}, u32[]{:S(2)}, u32[]{:S(2)}) %collective-permute-start.10) | collective-permute-done | bytes 57376 | tf_op jit(solution)/shard_map/ppermute | solution.py:35
  82.4 0.1 multiply_add_fusion
  82.5 0.1 select_convert_fusion
  82.6 0.1 broadcast_in_dim.147
  82.7 14.5 %all_to_all.23 = f16[16,112,256]{2,1,0:T(8,128)(2,1)S(1)} all-to-all(f16[16,112,256]{2,1,0:T(8,128)(2,1)S(1)} %broadcast_in_dim.147), channel_id=1, replica_groups=mesh['z'=8,'xl'=2,'y'=4,'c'=2,'xh'=2] {'xl','y','xh'}, dimensions={0} | all-to-all | bytes 1835008 | tf_op jit(solution)/shard_map/all_to_all | solution.py:471
  97.2 5.7 %collective-permute-start.11 = (f16[16,112,256]{2,1,0:T(8,128)(2,1)S(1)}, f16[16,112,256]{2,1,0:T(8,128)(2,1)S(1)}, u32[]{:S(2)}, u32[]{:S(2)}) collective-permute-start(f16[16,112,256]{2,1,0:T(8,128)(2,1)S(1)} %all_to_all.23), channel_id=1, source_target_pairs={{0,2},{1,3},{2,0},{3,1},{4,6},{5,7},{6,4},{7,5},{8,10},{9,11},{10,... | collective-permute-start | bytes 2752520 | tf_op jit(solution)/shard_map/ppermute | solution.py:35
  102.9 0.2 convert_element_type.78.half
  103.1 1.9 %collective-permute-done.11 = f16[16,112,256]{2,1,0:T(8,128)(2,1)S(1)} collective-permute-done((f16[16,112,256]{2,1,0:T(8,128)(2,1)S(1)}, f16[16,112,256]{2,1,0:T(8,128)(2,1)S(1)}, u32[]{:S(2)}, u32[]{:S(2)}) %collective-permute-start.11) | collective-permute-done | bytes 917536 | tf_op jit(solution)/shard_map/ppermute | solution.py:35
  105.0 0.2 convert_element_type.79.far
  105.2 3.0 %shard_map.122 = (f32[9,100,256]{2,1,0:T(8,128)}, f32[9,256,256]{2,1,0:T(8,128)}, f32[100,256]{1,0:T(8,128)}, f32[32,256]{1,0:T(8,128)}, f32[1,128]{1,0:T(1,128)}) custom-call(f32[16,112,256]{2,1,0:T(8,128)S(1)} %convert_element_type.78.half, f32[16,112,256]{2,1,0:T(8,128)S(1)} %convert_element_type.79.far), custom_call_target="tpu_custom_call" | custom-call | tf_op jit(solution)/shard_map/pallas_call | solution.py:424
  (13 shorter events, 0.2 us)
Async XLA Ops:
  0.6 28.4 %copy-start = (bf16[9,256,256]{2,1,0:T(8,128)(2,1)S(1)}, bf16[9,256,256]{2,1,0:T(8,128)(2,1)}, u32[]{:S(2)}) copy-start(bf16[9,256,256]{2,1,0:T(8,128)(2,1)} %w_mid.1) | copy-start | bytes 3538948
  3.4 10.9 %collective-permute-start = (f32[32,256]{1,0:T(8,128)S(1)}, f32[32,256]{1,0:T(8,128)S(1)}, u32[]{:S(2)}, u32[]{:S(2)}) collective-permute-start(f32[32,256]{1,0:T(8,128)S(1)} %get-tuple-element.21), channel_id=1, source_target_pairs={{0,1},{1,0},{2,3},{3,2},{4,5},{5,4},{6,7},{7,6},{8,9},{9,8},{10,11... | collective-permute-start | bytes 98312 | tf_op jit(solution)/shard_map/ppermute | solution.py:35
  6.2 14.3 %all-to-all-start = ((s32[16,1,32]{2,1,0:T(1,128)}), s32[16,1,32]{2,1,0:T(1,128)S(1)}, u32[]{:S(2)}, u32[]{:S(2)}) async-start(s32[16,1,32]{2,1,0:T(1,128)} %bitcast.1), calls=%async_computation | async-start | bytes 16384 | tf_op jit(solution)/shard_map/all_to_all | solution.py:488
  20.5 6.6 %collective-permute-start.1 = (bf16[64,256]{1,0:T(8,128)(2,1)S(1)}, bf16[64,256]{1,0:T(8,128)(2,1)S(1)}, u32[]{:S(2)}, u32[]{:S(2)}) collective-permute-start(bf16[64,256]{1,0:T(8,128)(2,1)S(1)} %shard_map.120.own), channel_id=1, source_target_pairs={{0,4},{1,5},{2,6},{3,7},{4,8},{5,9},{6,10},{7,11},{8,12},{9,13},{1... | collective-permute-start | bytes 98312 | tf_op jit(solution)/shard_map/ppermute | solution.py:35
  21.8 5.3 %collective-permute-start.2 = (bf16[64,256]{1,0:T(8,128)(2,1)S(1)}, bf16[64,256]{1,0:T(8,128)(2,1)S(1)}, u32[]{:S(2)}, u32[]{:S(2)}) collective-permute-start(bf16[64,256]{1,0:T(8,128)(2,1)S(1)} %shard_map.120.own), channel_id=1, source_target_pairs={{0,2},{1,3},{2,4},{3,5},{4,6},{5,7},{6,8},{7,9},{8,10},{9,11},{10,... | collective-permute-start | bytes 98312 | tf_op jit(solution)/shard_map/ppermute | solution.py:35
  25.6 3.3 %collective-permute-start.3 = (bf16[64,256]{1,0:T(8,128)(2,1)S(1)}, bf16[64,256]{1,0:T(8,128)(2,1)S(1)}, u32[]{:S(2)}, u32[]{:S(2)}) collective-permute-start(bf16[64,256]{1,0:T(8,128)(2,1)S(1)} %shard_map.120.own), channel_id=1, source_target_pairs={{0,14},{1,15},{2,0},{3,1},{4,2},{5,3},{6,4},{7,5},{8,6},{9,7},{10,... | collective-permute-start | bytes 98312 | tf_op jit(solution)/shard_map/ppermute | solution.py:35
  25.6 3.3 %collective-permute-start.4 = (bf16[64,256]{1,0:T(8,128)(2,1)S(1)}, bf16[64,256]{1,0:T(8,128)(2,1)S(1)}, u32[]{:S(2)}, u32[]{:S(2)}) collective-permute-start(bf16[64,256]{1,0:T(8,128)(2,1)S(1)} %shard_map.120.own), channel_id=1, source_target_pairs={{0,12},{1,13},{2,14},{3,15},{4,0},{5,1},{6,2},{7,3},{8,4},{9,5},{1... | collective-permute-start | bytes 98312 | tf_op jit(solution)/shard_map/ppermute | solution.py:35
  44.4 6.0 %collective-permute-start.5 = (f32[16,112,256]{2,1,0:T(8,128)S(1)}, f32[16,112,256]{2,1,0:T(8,128)S(1)}, u32[]{:S(2)}, u32[]{:S(2)}) collective-permute-start(f32[16,112,256]{2,1,0:T(8,128)S(1)} %slice_bitcast_fusion), channel_id=1, source_target_pairs={{0,2},{1,3},{2,0},{3,1},{4,6},{5,7},{6,4},{7,5},{8,10},{9,11},{10,... | collective-permute-start | bytes 5505032 | tf_op jit(solution)/shard_map/ppermute | solution.py:35
  46.8 3.4 %collective-permute-start.6 = (f32[8,256]{1,0:T(8,128)S(1)}, f32[8,256]{1,0:T(8,128)S(1)}, u32[]{:S(2)}, u32[]{:S(2)}) collective-permute-start(f32[8,256]{1,0:T(8,128)S(1)} %get-tuple-element.29), channel_id=1, source_target_pairs={{0,2},{1,3},{2,0},{3,1},{4,6},{5,7},{6,4},{7,5},{8,10},{9,11},{10,... | collective-permute-start | bytes 24584 | tf_op jit(solution)/shard_map/ppermute | solution.py:35
  69.4 3.4 %collective-permute-start.9 = (f16[112,256]{1,0:T(8,128)(2,1)S(1)}, f16[112,256]{1,0:T(8,128)(2,1)S(1)}, u32[]{:S(2)}, u32[]{:S(2)}) collective-permute-start(f16[112,256]{1,0:T(8,128)(2,1)S(1)} %select_convert_fusion.2), channel_id=1, source_target_pairs={{0,96},{1,97},{2,98},{3,99},{4,100},{5,101},{6,102},{7,103},{8,104... | collective-permute-start | bytes 172040 | tf_op jit(solution)/shard_map/ppermute | solution.py:35
  69.8 5.2 %collective-permute-start.8 = (f16[112,256]{1,0:T(8,128)(2,1)S(1)}, f16[112,256]{1,0:T(8,128)(2,1)S(1)}, u32[]{:S(2)}, u32[]{:S(2)}) collective-permute-start(f16[112,256]{1,0:T(8,128)(2,1)S(1)} %select_convert_fusion.2), channel_id=1, source_target_pairs={{0,64},{1,65},{2,66},{3,67},{4,68},{5,69},{6,70},{7,71},{8,72},{9,... | collective-permute-start | bytes 172040 | tf_op jit(solution)/shard_map/ppermute | solution.py:35
  72.7 3.2 %collective-permute-start.7 = (f16[112,256]{1,0:T(8,128)(2,1)S(1)}, f16[112,256]{1,0:T(8,128)(2,1)S(1)}, u32[]{:S(2)}, u32[]{:S(2)}) collective-permute-start(f16[112,256]{1,0:T(8,128)(2,1)S(1)} %select_convert_fusion.2), channel_id=1, source_target_pairs={{0,32},{1,33},{2,34},{3,35},{4,36},{5,37},{6,38},{7,39},{8,40},{9,... | collective-permute-start | bytes 172040 | tf_op jit(solution)/shard_map/ppermute | solution.py:35
  76.2 6.1 %collective-permute-start.10 = (f16[112,256]{1,0:T(8,128)(2,1)S(1)}, f16[112,256]{1,0:T(8,128)(2,1)S(1)}, u32[]{:S(2)}, u32[]{:S(2)}) collective-permute-start(f16[112,256]{1,0:T(8,128)(2,1)S(1)} %select_convert_fusion.1), channel_id=1, source_target_pairs={{0,224},{1,225},{2,226},{3,227},{4,228},{5,229},{6,230},{7,231},{8... | collective-permute-start | bytes 172040 | tf_op jit(solution)/shard_map/ppermute | solution.py:35
  97.2 7.8 %collective-permute-start.11 = (f16[16,112,256]{2,1,0:T(8,128)(2,1)S(1)}, f16[16,112,256]{2,1,0:T(8,128)(2,1)S(1)}, u32[]{:S(2)}, u32[]{:S(2)}) collective-permute-start(f16[16,112,256]{2,1,0:T(8,128)(2,1)S(1)} %all_to_all.23), channel_id=1, source_target_pairs={{0,2},{1,3},{2,0},{3,1},{4,6},{5,7},{6,4},{7,5},{8,10},{9,11},{10,... | collective-permute-start | bytes 2752520 | tf_op jit(solution)/shard_map/ppermute | solution.py:35

commit v8 on v7

--- a/solution.py
+++ b/solution.py
@@ -157,14 +157,17 @@
             HID[pl.ds(pl.multiple_of((r * WH + i) * M, M), M), :] = h.astype(bf16)
             return carry
 
-        lax.fori_loop(0, WH, hid_cell, 0, unroll=9)
+        lax.fori_loop(0, WH, hid_cell, 0, unroll=27)
 
     NR = WH * M
 
+    MC = 54 * M
+
     def mid_row(r, carry):
+        base = pl.multiple_of(r * MC, M)
         lhs = jnp.concatenate(
             [
-                HID[pl.ds(pl.multiple_of(((r + a) * WH + b) * M, M), NR), :]
+                HID[pl.ds(pl.multiple_of(base + (a * WH + b) * M, M), MC), :]
                 for a in range(3)
                 for b in range(3)
             ],
@@ -172,17 +175,16 @@
         )
         pre = jnp.dot(lhs, w_mid[...].reshape(9 * C, C), preferred_element_type=f32)
         act, slope = gelu_both(pre)
-        hid = HID[pl.ds(pl.multiple_of(((r + 1) * WH + 1) * M, M), NR), :].astype(f32)
-        base = pl.multiple_of(r * NR, M)
+        hid = HID[pl.ds(pl.multiple_of(base + (WH + 1) * M, M), MC), :].astype(f32)
         ho = (act + hid).astype(bf16)
-        HO[pl.ds(base, NR), :] = ho
-        SL[pl.ds(base, NR), :] = slope
-        OUT[pl.ds(base, NR), 0:V] = lax.dot_general(
+        HO[pl.ds(base, MC), :] = ho
+        SL[pl.ds(base, MC), :] = slope
+        OUT[pl.ds(base, MC), 0:V] = lax.dot_general(
             ho, w_out[...], (((1,), (1,)), ((), ())), preferred_element_type=f32
         )
         return carry
 
-    lax.fori_loop(0, 4, mid_row, 0)
+    lax.fori_loop(0, 2, mid_row, 0)
 
     def cell_terms(r, i, with_loss):
         base = pl.multiple_of((r * WH + i) * M, M)
@@ -225,14 +227,14 @@
             mine = (i >= 1) & ((i < 23) | ((i == 23) & (own22 > 0)))
             return total + jnp.where(mine, 1.0, 0.0) * term
 
-        loss = lax.fori_loop(0, WH, loss_cell, loss, unroll=3)
+        loss = lax.fori_loop(0, WH, loss_cell, loss, unroll=9)
     for r in (0, 3):
 
         def grad_cell(i, carry, r=r):
             cell_terms(r, i, False)
             return carry
 
-        lax.fori_loop(0, WH, grad_cell, 0, unroll=3)
+        lax.fori_loop(0, WH, grad_cell, 0, unroll=9)
     lane = lax.broadcasted_iota(jnp.int32, (M, 128), 1)
     loss = jnp.sum(jnp.sum(jnp.where(lane < V, loss, 0.0), axis=0, keepdims=True), axis=1, keepdims=True)
 
@@ -273,7 +275,7 @@
             DS[pl.ds(r * 32 + i + 2, 1), :] = jnp.sum(d, axis=0, keepdims=True)
             return total + d
 
-        dsum = lax.fori_loop(0, 23, in_cell, dsum)
+        dsum = lax.fori_loop(0, 23, in_cell, dsum, unroll=4)
 
     def store(k, lo, hi, value):
         g_out[(k // 16) ^ core, k % 16, lo:hi, :] = value

time: 109 us -> 107 us (0.982)
  Pallas kernels: 21.1 us -> 19.4 us
    pallas_call x4, Pallas kernels: 21.1 us -> 19.4 us  [call(): pl.pallas_call(kernel, out_shape=[pltpu.VMEM(o[0], o[1]) if len(o) > 2 el...]
where the time goes in v8:
time: 107 us
  blocking collectives  32.7 us (31%)
  starting transfers between devices  30.3 us (28%)
  waiting for transfers between devices  21.3 us (20%)
  Pallas kernels  19.4 us (18%)
  other arithmetic  1.85 us (2%)
    ppermute x12, starting transfers between devices, send(): return lax.ppermute(v, AX, perm(f))  22.2 us
    pallas_call x4, Pallas kernels, call(): pl.pallas_call(kernel, out_shape=[pltpu.VMEM(o[0], o[1]) if len(o) > 2 el...  19.4 us
    all_to_all x1, blocking collectives, sum_all(): got = lax.all_to_all(s.astype(f16), xy, 0, 0, tiled=True)  18.1 us
    ppermute x12, waiting for transfers between devices, send(): return lax.ppermute(v, AX, perm(f))  15.2 us
    all_to_all x1, blocking collectives, sum_all(): lax.all_to_all(jnp.broadcast_to(s[None], (16,) + s.shape), xy, 0, 0, tile...  14.5 us
    all_to_all x1, starting transfers between devices, body(): seeds = lax.all_to_all(seeds, ('z', 'xl'), 0, 0, tiled=True)  8.05 us
    all_to_all x1, waiting for transfers between devices, body(): seeds = lax.all_to_all(seeds, ('z', 'xl'), 0, 0, tiled=True)  6.14 us
  transfers between devices with their start and end apart: 13, of which 7 were waited for; matrix products, arithmetic and copies ran while one was open for 0% of the time, Pallas kernels for 0%

profile of v8, /device:TPU:33, one launch (start us, length us, event | category | flops | bytes accessed | tf_op | source)
XLA Modules:
  0.0 106.7 jit_solution(8131067320281757385)
XLA Ops:
  0.6 0.0 copy-start
  0.6 2.7 %shard_map.119 = (f32[2,384,256]{2,1,0:T(8,128)S(1)}, f32[32,256]{1,0:T(8,128)S(1)}, s32[16,32]{1,0:T(8,128)}, bf16[9,100,256]{2,1,0:T(8,128)(2,1)S(1)}, bf16[10...) custom-call(bf16[100,2,360]{2,1,0:T(2,128)(2,1)} %state.1, bf16[100,2,360]{2,1,0:T(2,128)(2,1)} %target.1, s32[2,360]{1,0:T(2,128)} %land.1, ...), custom_call_target="tpu_custom_call" | custom-call | tf_op jit(solution)/shard_map/pallas_call | solution.py:426
  3.4 2.8 %collective-permute-start = (f32[32,256]{1,0:T(8,128)S(1)}, f32[32,256]{1,0:T(8,128)S(1)}, u32[]{:S(2)}, u32[]{:S(2)}) collective-permute-start(f32[32,256]{1,0:T(8,128)S(1)} %get-tuple-element.21), channel_id=1, source_target_pairs={{0,1},{1,0},{2,3},{3,2},{4,5},{5,4},{6,7},{7,6},{8,9},{9,8},{10,11... | collective-permute-start | bytes 98312 | tf_op jit(solution)/shard_map/ppermute | solution.py:35
  6.2 8.1 %all-to-all-start = ((s32[16,1,32]{2,1,0:T(1,128)}), s32[16,1,32]{2,1,0:T(1,128)S(1)}, u32[]{:S(2)}, u32[]{:S(2)}) async-start(s32[16,1,32]{2,1,0:T(1,128)} %bitcast.1), calls=%async_computation | async-start | bytes 16384 | tf_op jit(solution)/shard_map/all_to_all | solution.py:490
  14.3 0.0 collective-permute-done.edge
  14.3 0.1 shard_map.120.own
  14.4 6.1 %all-to-all-done = s32[16,1,32]{2,1,0:T(1,128)S(1)} async-done(((s32[16,1,32]{2,1,0:T(1,128)}), s32[16,1,32]{2,1,0:T(1,128)S(1)}, u32[]{:S(2)}, u32[]{:S(2)}) %all-to-all-start) | async-done | bytes 2080 | tf_op jit(solution)/shard_map/all_to_all | solution.py:490
  20.5 1.3 %collective-permute-start.1 = (bf16[64,256]{1,0:T(8,128)(2,1)S(1)}, bf16[64,256]{1,0:T(8,128)(2,1)S(1)}, u32[]{:S(2)}, u32[]{:S(2)}) collective-permute-start(bf16[64,256]{1,0:T(8,128)(2,1)S(1)} %shard_map.120.own), channel_id=1, source_target_pairs={{0,4},{1,5},{2,6},{3,7},{4,8},{5,9},{6,10},{7,11},{8,12},{9,13},{1... | collective-permute-start | bytes 98312 | tf_op jit(solution)/shard_map/ppermute | solution.py:35
  21.8 3.8 %collective-permute-start.2 = (bf16[64,256]{1,0:T(8,128)(2,1)S(1)}, bf16[64,256]{1,0:T(8,128)(2,1)S(1)}, u32[]{:S(2)}, u32[]{:S(2)}) collective-permute-start(bf16[64,256]{1,0:T(8,128)(2,1)S(1)} %shard_map.120.own), channel_id=1, source_target_pairs={{0,2},{1,3},{2,4},{3,5},{4,6},{5,7},{6,8},{7,9},{8,10},{9,11},{10,... | collective-permute-start | bytes 98312 | tf_op jit(solution)/shard_map/ppermute | solution.py:35
  25.6 0.0 collective-permute-start.3
  25.6 1.4 %collective-permute-start.4 = (bf16[64,256]{1,0:T(8,128)(2,1)S(1)}, bf16[64,256]{1,0:T(8,128)(2,1)S(1)}, u32[]{:S(2)}, u32[]{:S(2)}) collective-permute-start(bf16[64,256]{1,0:T(8,128)(2,1)S(1)} %shard_map.120.own), channel_id=1, source_target_pairs={{0,12},{1,13},{2,14},{3,15},{4,0},{5,1},{6,2},{7,3},{8,4},{9,5},{1... | collective-permute-start | bytes 98312 | tf_op jit(solution)/shard_map/ppermute | solution.py:35
  27.1 0.0 collective-permute-done.1.n2
  27.1 0.0 collective-permute-done.2.n1
  27.1 1.9 %collective-permute-done.3.s1 = bf16[64,256]{1,0:T(8,128)(2,1)S(1)} collective-permute-done((bf16[64,256]{1,0:T(8,128)(2,1)S(1)}, bf16[64,256]{1,0:T(8,128)(2,1)S(1)}, u32[]{:S(2)}, u32[]{:S(2)}) %collective-permute-start.3) | collective-permute-done | bytes 32800 | tf_op jit(solution)/shard_map/ppermute | solution.py:35
  29.0 0.0 collective-permute-done.4.s2
  29.0 0.0 copy-done
  29.0 13.6 %shard_map.121 = (f32[2,16,112,256]{3,2,1,0:T(8,128)S(1)}, f32[8,256]{1,0:T(8,128)S(1)}) custom-call(bf16[64,256]{1,0:T(8,128)(2,1)S(1)} %collective-permute-done.1.n2, bf16[64,256]{1,0:T(8,128)(2,1)S(1)} %collective-permute-done.2.n1, bf16[64,256]{1,0:T(8,128)(2,1)S(1)} %shard_map.120.own, bf16[64,256]{1,0:T(8,128)(2,1)S(1)} %collective-permute-done.3.s1, ...), custom_call_target="tpu_custom_call" | custom-call | tf_op jit(solution)/shard_map/pallas_call | solution.py:426
  42.6 0.1 slice_bitcast_fusion
  42.7 2.4 %collective-permute-start.5 = (f32[16,112,256]{2,1,0:T(8,128)S(1)}, f32[16,112,256]{2,1,0:T(8,128)S(1)}, u32[]{:S(2)}, u32[]{:S(2)}) collective-permute-start(f32[16,112,256]{2,1,0:T(8,128)S(1)} %slice_bitcast_fusion), channel_id=1, source_target_pairs={{0,2},{1,3},{2,0},{3,1},{4,6},{5,7},{6,4},{7,5},{8,10},{9,11},{10,... | collective-permute-start | bytes 5505032 | tf_op jit(solution)/shard_map/ppermute | solution.py:35
  45.2 0.1 collective-permute-start.6
  45.3 3.3 %collective-permute-done.6 = f32[8,256]{1,0:T(8,128)S(1)} collective-permute-done((f32[8,256]{1,0:T(8,128)S(1)}, f32[8,256]{1,0:T(8,128)S(1)}, u32[]{:S(2)}, u32[]{:S(2)}) %collective-permute-start.6) | collective-permute-done | bytes 8224 | tf_op jit(solution)/shard_map/ppermute | solution.py:35
  48.6 0.1 broadcast_select_fusion
  48.7 0.0 collective-permute-done.5
  48.7 0.4 fusion.2
  49.1 18.1 %all_to_all.22 = f16[16,112,256]{2,1,0:T(8,128)(2,1)S(1)} all-to-all(f16[16,112,256]{2,1,0:T(8,128)(2,1)S(1)} %fusion.2), channel_id=1, replica_groups=mesh['z'=8,'xl'=2,'y'=4,'c'=2,'xh'=2] {'xl','y','xh'}, dimensions={0} | all-to-all | bytes 1835008 | tf_op jit(solution)/shard_map/all_to_all | solution.py:464
  67.3 0.3 multiply_reduce_fusion
  67.7 0.1 select_convert_fusion.2
  67.8 0.4 collective-permute-start.9
  68.1 3.0 %collective-permute-start.8 = (f16[112,256]{1,0:T(8,128)(2,1)S(1)}, f16[112,256]{1,0:T(8,128)(2,1)S(1)}, u32[]{:S(2)}, u32[]{:S(2)}) collective-permute-start(f16[112,256]{1,0:T(8,128)(2,1)S(1)} %select_convert_fusion.2), channel_id=1, source_target_pairs={{0,64},{1,65},{2,66},{3,67},{4,68},{5,69},{6,70},{7,71},{8,72},{9,... | collective-permute-start | bytes 172040 | tf_op jit(solution)/shard_map/ppermute | solution.py:35
  71.1 0.0 collective-permute-start.7
  71.1 0.0 collective-permute-done.9
  71.1 2.2 %collective-permute-done.8 = f16[112,256]{1,0:T(8,128)(2,1)S(1)} collective-permute-done((f16[112,256]{1,0:T(8,128)(2,1)S(1)}, f16[112,256]{1,0:T(8,128)(2,1)S(1)}, u32[]{:S(2)}, u32[]{:S(2)}) %collective-permute-start.8) | collective-permute-done | bytes 57376 | tf_op jit(solution)/shard_map/ppermute | solution.py:35
  73.3 1.0 collective-permute-done.7
  74.3 0.1 add_add_fusion
  74.5 0.1 select_convert_fusion.1
  74.6 1.3 %collective-permute-start.10 = (f16[112,256]{1,0:T(8,128)(2,1)S(1)}, f16[112,256]{1,0:T(8,128)(2,1)S(1)}, u32[]{:S(2)}, u32[]{:S(2)}) collective-permute-start(f16[112,256]{1,0:T(8,128)(2,1)S(1)} %select_convert_fusion.1), channel_id=1, source_target_pairs={{0,224},{1,225},{2,226},{3,227},{4,228},{5,229},{6,230},{7,231},{8... | collective-permute-start | bytes 172040 | tf_op jit(solution)/shard_map/ppermute | solution.py:35
  75.9 4.8 %collective-permute-done.10 = f16[112,256]{1,0:T(8,128)(2,1)S(1)} collective-permute-done((f16[112,256]{1,0:T(8,128)(2,1)S(1)}, f16[112,256]{1,0:T(8,128)(2,1)S(1)}, u32[]{:S(2)}, u32[]{:S(2)}) %collective-permute-start.10) | collective-permute-done | bytes 57376 | tf_op jit(solution)/shard_map/ppermute | solution.py:35
  80.7 0.1 multiply_add_fusion
  80.8 0.1 select_convert_fusion
  80.9 0.1 broadcast_in_dim.147
  81.0 14.5 %all_to_all.23 = f16[16,112,256]{2,1,0:T(8,128)(2,1)S(1)} all-to-all(f16[16,112,256]{2,1,0:T(8,128)(2,1)S(1)} %broadcast_in_dim.147), channel_id=1, replica_groups=mesh['z'=8,'xl'=2,'y'=4,'c'=2,'xh'=2] {'xl','y','xh'}, dimensions={0} | all-to-all | bytes 1835008 | tf_op jit(solution)/shard_map/all_to_all | solution.py:473
  95.5 5.7 %collective-permute-start.11 = (f16[16,112,256]{2,1,0:T(8,128)(2,1)S(1)}, f16[16,112,256]{2,1,0:T(8,128)(2,1)S(1)}, u32[]{:S(2)}, u32[]{:S(2)}) collective-permute-start(f16[16,112,256]{2,1,0:T(8,128)(2,1)S(1)} %all_to_all.23), channel_id=1, source_target_pairs={{0,2},{1,3},{2,0},{3,1},{4,6},{5,7},{6,4},{7,5},{8,10},{9,11},{10,... | collective-permute-start | bytes 2752520 | tf_op jit(solution)/shard_map/ppermute | solution.py:35
  101.3 0.2 convert_element_type.78.half
  101.4 1.9 %collective-permute-done.11 = f16[16,112,256]{2,1,0:T(8,128)(2,1)S(1)} collective-permute-done((f16[16,112,256]{2,1,0:T(8,128)(2,1)S(1)}, f16[16,112,256]{2,1,0:T(8,128)(2,1)S(1)}, u32[]{:S(2)}, u32[]{:S(2)}) %collective-permute-start.11) | collective-permute-done | bytes 917536 | tf_op jit(solution)/shard_map/ppermute | solution.py:35
  103.4 0.2 convert_element_type.79.far
  103.5 3.0 %shard_map.122 = (f32[9,100,256]{2,1,0:T(8,128)}, f32[9,256,256]{2,1,0:T(8,128)}, f32[100,256]{1,0:T(8,128)}, f32[32,256]{1,0:T(8,128)}, f32[1,128]{1,0:T(1,128)}) custom-call(f32[16,112,256]{2,1,0:T(8,128)S(1)} %convert_element_type.78.half, f32[16,112,256]{2,1,0:T(8,128)S(1)} %convert_element_type.79.far), custom_call_target="tpu_custom_call" | custom-call | tf_op jit(solution)/shard_map/pallas_call | solution.py:426
  (13 shorter events, 0.2 us)
Async XLA Ops:
  0.6 28.4 %copy-start = (bf16[9,256,256]{2,1,0:T(8,128)(2,1)S(1)}, bf16[9,256,256]{2,1,0:T(8,128)(2,1)}, u32[]{:S(2)}) copy-start(bf16[9,256,256]{2,1,0:T(8,128)(2,1)} %w_mid.1) | copy-start | bytes 3538948
  3.4 10.9 %collective-permute-start = (f32[32,256]{1,0:T(8,128)S(1)}, f32[32,256]{1,0:T(8,128)S(1)}, u32[]{:S(2)}, u32[]{:S(2)}) collective-permute-start(f32[32,256]{1,0:T(8,128)S(1)} %get-tuple-element.21), channel_id=1, source_target_pairs={{0,1},{1,0},{2,3},{3,2},{4,5},{5,4},{6,7},{7,6},{8,9},{9,8},{10,11... | collective-permute-start | bytes 98312 | tf_op jit(solution)/shard_map/ppermute | solution.py:35
  6.2 14.3 %all-to-all-start = ((s32[16,1,32]{2,1,0:T(1,128)}), s32[16,1,32]{2,1,0:T(1,128)S(1)}, u32[]{:S(2)}, u32[]{:S(2)}) async-start(s32[16,1,32]{2,1,0:T(1,128)} %bitcast.1), calls=%async_computation | async-start | bytes 16384 | tf_op jit(solution)/shard_map/all_to_all | solution.py:490
  20.5 6.6 %collective-permute-start.1 = (bf16[64,256]{1,0:T(8,128)(2,1)S(1)}, bf16[64,256]{1,0:T(8,128)(2,1)S(1)}, u32[]{:S(2)}, u32[]{:S(2)}) collective-permute-start(bf16[64,256]{1,0:T(8,128)(2,1)S(1)} %shard_map.120.own), channel_id=1, source_target_pairs={{0,4},{1,5},{2,6},{3,7},{4,8},{5,9},{6,10},{7,11},{8,12},{9,13},{1... | collective-permute-start | bytes 98312 | tf_op jit(solution)/shard_map/ppermute | solution.py:35
  21.8 5.3 %collective-permute-start.2 = (bf16[64,256]{1,0:T(8,128)(2,1)S(1)}, bf16[64,256]{1,0:T(8,128)(2,1)S(1)}, u32[]{:S(2)}, u32[]{:S(2)}) collective-permute-start(bf16[64,256]{1,0:T(8,128)(2,1)S(1)} %shard_map.120.own), channel_id=1, source_target_pairs={{0,2},{1,3},{2,4},{3,5},{4,6},{5,7},{6,8},{7,9},{8,10},{9,11},{10,... | collective-permute-start | bytes 98312 | tf_op jit(solution)/shard_map/ppermute | solution.py:35
  25.6 3.3 %collective-permute-start.3 = (bf16[64,256]{1,0:T(8,128)(2,1)S(1)}, bf16[64,256]{1,0:T(8,128)(2,1)S(1)}, u32[]{:S(2)}, u32[]{:S(2)}) collective-permute-start(bf16[64,256]{1,0:T(8,128)(2,1)S(1)} %shard_map.120.own), channel_id=1, source_target_pairs={{0,14},{1,15},{2,0},{3,1},{4,2},{5,3},{6,4},{7,5},{8,6},{9,7},{10,... | collective-permute-start | bytes 98312 | tf_op jit(solution)/shard_map/ppermute | solution.py:35
  25.6 3.3 %collective-permute-start.4 = (bf16[64,256]{1,0:T(8,128)(2,1)S(1)}, bf16[64,256]{1,0:T(8,128)(2,1)S(1)}, u32[]{:S(2)}, u32[]{:S(2)}) collective-permute-start(bf16[64,256]{1,0:T(8,128)(2,1)S(1)} %shard_map.120.own), channel_id=1, source_target_pairs={{0,12},{1,13},{2,14},{3,15},{4,0},{5,1},{6,2},{7,3},{8,4},{9,5},{1... | collective-permute-start | bytes 98312 | tf_op jit(solution)/shard_map/ppermute | solution.py:35
  42.7 6.0 %collective-permute-start.5 = (f32[16,112,256]{2,1,0:T(8,128)S(1)}, f32[16,112,256]{2,1,0:T(8,128)S(1)}, u32[]{:S(2)}, u32[]{:S(2)}) collective-permute-start(f32[16,112,256]{2,1,0:T(8,128)S(1)} %slice_bitcast_fusion), channel_id=1, source_target_pairs={{0,2},{1,3},{2,0},{3,1},{4,6},{5,7},{6,4},{7,5},{8,10},{9,11},{10,... | collective-permute-start | bytes 5505032 | tf_op jit(solution)/shard_map/ppermute | solution.py:35
  45.2 3.4 %collective-permute-start.6 = (f32[8,256]{1,0:T(8,128)S(1)}, f32[8,256]{1,0:T(8,128)S(1)}, u32[]{:S(2)}, u32[]{:S(2)}) collective-permute-start(f32[8,256]{1,0:T(8,128)S(1)} %get-tuple-element.29), channel_id=1, source_target_pairs={{0,2},{1,3},{2,0},{3,1},{4,6},{5,7},{6,4},{7,5},{8,10},{9,11},{10,... | collective-permute-start | bytes 24584 | tf_op jit(solution)/shard_map/ppermute | solution.py:35
  67.8 3.4 %collective-permute-start.9 = (f16[112,256]{1,0:T(8,128)(2,1)S(1)}, f16[112,256]{1,0:T(8,128)(2,1)S(1)}, u32[]{:S(2)}, u32[]{:S(2)}) collective-permute-start(f16[112,256]{1,0:T(8,128)(2,1)S(1)} %select_convert_fusion.2), channel_id=1, source_target_pairs={{0,96},{1,97},{2,98},{3,99},{4,100},{5,101},{6,102},{7,103},{8,104... | collective-permute-start | bytes 172040 | tf_op jit(solution)/shard_map/ppermute | solution.py:35
  68.1 5.2 %collective-permute-start.8 = (f16[112,256]{1,0:T(8,128)(2,1)S(1)}, f16[112,256]{1,0:T(8,128)(2,1)S(1)}, u32[]{:S(2)}, u32[]{:S(2)}) collective-permute-start(f16[112,256]{1,0:T(8,128)(2,1)S(1)} %select_convert_fusion.2), channel_id=1, source_target_pairs={{0,64},{1,65},{2,66},{3,67},{4,68},{5,69},{6,70},{7,71},{8,72},{9,... | collective-permute-start | bytes 172040 | tf_op jit(solution)/shard_map/ppermute | solution.py:35
  71.1 3.2 %collective-permute-start.7 = (f16[112,256]{1,0:T(8,128)(2,1)S(1)}, f16[112,256]{1,0:T(8,128)(2,1)S(1)}, u32[]{:S(2)}, u32[]{:S(2)}) collective-permute-start(f16[112,256]{1,0:T(8,128)(2,1)S(1)} %select_convert_fusion.2), channel_id=1, source_target_pairs={{0,32},{1,33},{2,34},{3,35},{4,36},{5,37},{6,38},{7,39},{8,40},{9,... | collective-permute-start | bytes 172040 | tf_op jit(solution)/shard_map/ppermute | solution.py:35
  74.6 6.1 %collective-permute-start.10 = (f16[112,256]{1,0:T(8,128)(2,1)S(1)}, f16[112,256]{1,0:T(8,128)(2,1)S(1)}, u32[]{:S(2)}, u32[]{:S(2)}) collective-permute-start(f16[112,256]{1,0:T(8,128)(2,1)S(1)} %select_convert_fusion.1), channel_id=1, source_target_pairs={{0,224},{1,225},{2,226},{3,227},{4,228},{5,229},{6,230},{7,231},{8... | collective-permute-start | bytes 172040 | tf_op jit(solution)/shard_map/ppermute | solution.py:35
  95.5 7.8 %collective-permute-start.11 = (f16[16,112,256]{2,1,0:T(8,128)(2,1)S(1)}, f16[16,112,256]{2,1,0:T(8,128)(2,1)S(1)}, u32[]{:S(2)}, u32[]{:S(2)}) collective-permute-start(f16[16,112,256]{2,1,0:T(8,128)(2,1)S(1)} %all_to_all.23), channel_id=1, source_target_pairs={{0,2},{1,3},{2,0},{3,1},{4,6},{5,7},{6,4},{7,5},{8,10},{9,11},{10,... | collective-permute-start | bytes 2752520 | tf_op jit(solution)/shard_map/ppermute | solution.py:35

commit v9 on v8

--- a/solution.py
+++ b/solution.py
@@ -114,17 +114,22 @@
 
 
 def main_kernel(
-    n2, n1, own, s1, s2, seeds, w_in, w_mid, w_out, w_noise, g_out, e_out,
+    n2, next_chip, own, near, s2, seeds, w_in, w_mid, w_out, w_noise, g_out, e_out,
     S, T, SB, PB, HID, HO, SL, UP, OUT, DO, DM, INC, DS, QB, BIAS,
 ):
     own22 = member_index() % 2
     lat = lat_index()
     core = lax.axis_index("c")
-    rows = ((n2, 1, -2), (n1, 0, -1), (n1, 1, -1), (own, 0, 0), (own, 1, 0),
-            (s1, 0, 1), (s1, 1, 1), (s2, 0, 2))
-    for k, (ref, r, d) in enumerate(rows):
-        inside = (lat + d >= 0) & (lat + d < 8)
-        row = ref[WP * r : WP * r + WP, :].astype(f32) * jnp.where(inside, 1.0, 0.0)
+    rows = (
+        (n2, n2, 1, -2), (next_chip, near, 0, -1), (next_chip, near, 1, -1), (own, own, 0, 0),
+        (own, own, 1, 0), (near, next_chip, 0, 1), (near, next_chip, 1, 1), (s2, s2, 0, 2),
+    )
+    for k, (first, second, r, d) in enumerate(rows):
+        inside = jnp.where((lat + d >= 0) & (lat + d < 8), 1.0, 0.0)
+        row = first[WP * r : WP * r + WP, :].astype(f32)
+        if second is not first:
+            row = jnp.where(core == 0, row, second[WP * r : WP * r + WP, :].astype(f32))
+        row = row * inside
         S[WP * k : WP * k + WP, :] = row[:, 0:128]
         T[WP * k : WP * k + WP, :] = row[:, 128:256]
     S[256:264, :] = jnp.zeros((8, 128), f32)
@@ -490,7 +495,9 @@
     seeds = lax.all_to_all(seeds, ("z", "xl"), 0, 0, tiled=True)
     (win,) = call(window_kernel, [((2 * WP, 256), bf16, 1)], [], (x, edge), kept=(0, 1))
     win, seeds = lax.optimization_barrier((win, seeds))
-    n2, n1, s1, s2 = (lat_shift(win, d) for d in (2, 1, -1, -2))
+    n2, s2 = (lat_shift(win, d) for d in (2, -2))
+    near = send(win, lambda z, xl, lat, xh: (z, xl, lat ^ 1, xh))
+    next_chip = send(win, lambda z, xl, lat, xh: (z, xl, (lat + 2 * (lat % 2) - 1) % 8, xh))
     g, e = call(
         main_kernel, [((2, 16, BR, C), f32, 1), ((8, C), f32, 1)],
         [
@@ -510,7 +517,7 @@
             pltpu.VMEM((264, 128), f32),
             pltpu.VMEM((M, C), f32),
         ],
-        (n2, n1, win, s1, s2, seeds, w_in, w_mid, w_out, w_noise),
+        (n2, next_chip, win, near, s2, seeds, w_in, w_mid, w_out, w_noise),
         kept=range(10),
         limit=32,
     )

time: 107 us -> 107 us (level)
  blocking collectives: 32.7 us -> 33.8 us
    all_to_all x1, blocking collectives: 18.1 us -> 19.3 us  [sum_all(): got = lax.all_to_all(s.astype(f16), xy, 0, 0, tiled=True)]
  transfers between devices with their start and end apart: 13 -> 13, of which waited for: 7 -> 8; matrix products, arithmetic and copies ran while one was open for 0% -> 0% of each run, Pallas kernels for 0% -> 0%
where the time goes in v9:
time: 107 us
  blocking collectives  33.8 us (32%)
  starting transfers between devices  29.6 us (28%)
  waiting for transfers between devices  20.8 us (19%)
  Pallas kernels  19.4 us (18%)
  other arithmetic  1.85 us (2%)
    ppermute x12, starting transfers between devices, send(): return lax.ppermute(v, AX, perm(f))  21.5 us
    pallas_call x4, Pallas kernels, call(): pl.pallas_call(kernel, out_shape=[pltpu.VMEM(o[0], o[1]) if len(o) > 2 el...  19.4 us
    all_to_all x1, blocking collectives, sum_all(): got = lax.all_to_all(s.astype(f16), xy, 0, 0, tiled=True)  19.3 us
    ppermute x12, waiting for transfers between devices, send(): return lax.ppermute(v, AX, perm(f))  14.6 us
    all_to_all x1, blocking collectives, sum_all(): lax.all_to_all(jnp.broadcast_to(s[None], (16,) + s.shape), xy, 0, 0, tile...  14.5 us
    all_to_all x1, starting transfers between devices, body(): seeds = lax.all_to_all(seeds, ('z', 'xl'), 0, 0, tiled=True)  8.05 us
    all_to_all x1, waiting for transfers between devices, body(): seeds = lax.all_to_all(seeds, ('z', 'xl'), 0, 0, tiled=True)  6.14 us
  transfers between devices with their start and end apart: 13, of which 8 were waited for; matrix products, arithmetic and copies ran while one was open for 0% of the time, Pallas kernels for 0%

profile of v9, /device:TPU:33, one launch (start us, length us, event | category | flops | bytes accessed | tf_op | source)
XLA Modules:
  0.0 106.6 jit_solution(2086667246291156599)
XLA Ops:
  0.6 0.0 copy-start
  0.6 2.7 %shard_map.119 = (f32[2,384,256]{2,1,0:T(8,128)S(1)}, f32[32,256]{1,0:T(8,128)S(1)}, s32[16,32]{1,0:T(8,128)}, bf16[9,100,256]{2,1,0:T(8,128)(2,1)S(1)}, bf16[10...) custom-call(bf16[100,2,360]{2,1,0:T(2,128)(2,1)} %state.1, bf16[100,2,360]{2,1,0:T(2,128)(2,1)} %target.1, s32[2,360]{1,0:T(2,128)} %land.1, ...), custom_call_target="tpu_custom_call" | custom-call | tf_op jit(solution)/shard_map/pallas_call | solution.py:431
  3.4 2.8 %collective-permute-start = (f32[32,256]{1,0:T(8,128)S(1)}, f32[32,256]{1,0:T(8,128)S(1)}, u32[]{:S(2)}, u32[]{:S(2)}) collective-permute-start(f32[32,256]{1,0:T(8,128)S(1)} %get-tuple-element.21), channel_id=1, source_target_pairs={{0,1},{1,0},{2,3},{3,2},{4,5},{5,4},{6,7},{7,6},{8,9},{9,8},{10,11... | collective-permute-start | bytes 98312 | tf_op jit(solution)/shard_map/ppermute | solution.py:35
  6.2 8.1 %all-to-all-start = ((s32[16,1,32]{2,1,0:T(1,128)}), s32[16,1,32]{2,1,0:T(1,128)S(1)}, u32[]{:S(2)}, u32[]{:S(2)}) async-start(s32[16,1,32]{2,1,0:T(1,128)} %bitcast.1), calls=%async_computation | async-start | bytes 16384 | tf_op jit(solution)/shard_map/all_to_all | solution.py:495
  14.3 0.0 collective-permute-done.edge
  14.3 0.1 shard_map.120.own
  14.4 6.1 %all-to-all-done = s32[16,1,32]{2,1,0:T(1,128)S(1)} async-done(((s32[16,1,32]{2,1,0:T(1,128)}), s32[16,1,32]{2,1,0:T(1,128)S(1)}, u32[]{:S(2)}, u32[]{:S(2)}) %all-to-all-start) | async-done | bytes 2080 | tf_op jit(solution)/shard_map/all_to_all | solution.py:495
  20.5 1.3 %collective-permute-start.1 = (bf16[64,256]{1,0:T(8,128)(2,1)S(1)}, bf16[64,256]{1,0:T(8,128)(2,1)S(1)}, u32[]{:S(2)}, u32[]{:S(2)}) collective-permute-start(bf16[64,256]{1,0:T(8,128)(2,1)S(1)} %shard_map.120.own), channel_id=1, source_target_pairs={{0,4},{1,5},{2,6},{3,7},{4,8},{5,9},{6,10},{7,11},{8,12},{9,13},{1... | collective-permute-start | bytes 98312 | tf_op jit(solution)/shard_map/ppermute | solution.py:35
  21.8 3.8 %collective-permute-start.2 = (bf16[64,256]{1,0:T(8,128)(2,1)S(1)}, bf16[64,256]{1,0:T(8,128)(2,1)S(1)}, u32[]{:S(2)}, u32[]{:S(2)}) collective-permute-start(bf16[64,256]{1,0:T(8,128)(2,1)S(1)} %shard_map.120.own), channel_id=1, source_target_pairs={{0,14},{1,15},{2,4},{3,5},{4,2},{5,3},{6,8},{7,9},{8,6},{9,7},{10,... | collective-permute-start | bytes 98312 | tf_op jit(solution)/shard_map/ppermute | solution.py:35
  25.6 0.0 collective-permute-start.3
  25.6 1.4 %collective-permute-start.4 = (bf16[64,256]{1,0:T(8,128)(2,1)S(1)}, bf16[64,256]{1,0:T(8,128)(2,1)S(1)}, u32[]{:S(2)}, u32[]{:S(2)}) collective-permute-start(bf16[64,256]{1,0:T(8,128)(2,1)S(1)} %shard_map.120.own), channel_id=1, source_target_pairs={{0,12},{1,13},{2,14},{3,15},{4,0},{5,1},{6,2},{7,3},{8,4},{9,5},{1... | collective-permute-start | bytes 98312 | tf_op jit(solution)/shard_map/ppermute | solution.py:35
  27.0 0.0 collective-permute-done.1.n2
  27.0 0.5 collective-permute-done.2.next_chip
  27.5 0.0 collective-permute-done.3.near
  27.5 1.1 %collective-permute-done.4.s2 = bf16[64,256]{1,0:T(8,128)(2,1)S(1)} collective-permute-done((bf16[64,256]{1,0:T(8,128)(2,1)S(1)}, bf16[64,256]{1,0:T(8,128)(2,1)S(1)}, u32[]{:S(2)}, u32[]{:S(2)}) %collective-permute-start.4) | collective-permute-done | bytes 32800 | tf_op jit(solution)/shard_map/ppermute | solution.py:35
  28.6 0.0 copy-done
  28.6 13.6 %shard_map.121 = (f32[2,16,112,256]{3,2,1,0:T(8,128)S(1)}, f32[8,256]{1,0:T(8,128)S(1)}) custom-call(bf16[64,256]{1,0:T(8,128)(2,1)S(1)} %collective-permute-done.1.n2, bf16[64,256]{1,0:T(8,128)(2,1)S(1)} %collective-permute-done.2.next_chip, bf16[64,256]{1,0:T(8,128)(2,1)S(1)} %shard_map.120.own, bf16[64,256]{1,0:T(8,128)(2,1)S(1)} %collective-permute-done.3.near, ...), custom_call_target="tpu_custom_call" | custom-call | tf_op jit(solution)/shard_map/pallas_call | solution.py:431
  42.2 0.1 slice_bitcast_fusion
  42.4 1.5 %collective-permute-start.5 = (f32[16,112,256]{2,1,0:T(8,128)S(1)}, f32[16,112,256]{2,1,0:T(8,128)S(1)}, u32[]{:S(2)}, u32[]{:S(2)}) collective-permute-start(f32[16,112,256]{2,1,0:T(8,128)S(1)} %slice_bitcast_fusion), channel_id=1, source_target_pairs={{0,2},{1,3},{2,0},{3,1},{4,6},{5,7},{6,4},{7,5},{8,10},{9,11},{10,... | collective-permute-start | bytes 5505032 | tf_op jit(solution)/shard_map/ppermute | solution.py:35
  43.9 0.3 collective-permute-start.6
  44.2 3.1 %collective-permute-done.6 = f32[8,256]{1,0:T(8,128)S(1)} collective-permute-done((f32[8,256]{1,0:T(8,128)S(1)}, f32[8,256]{1,0:T(8,128)S(1)}, u32[]{:S(2)}, u32[]{:S(2)}) %collective-permute-start.6) | collective-permute-done | bytes 8224 | tf_op jit(solution)/shard_map/ppermute | solution.py:35
  47.3 0.1 broadcast_select_fusion
  47.4 0.0 collective-permute-done.5
  47.4 0.4 fusion.2
  47.9 19.3 %all_to_all.22 = f16[16,112,256]{2,1,0:T(8,128)(2,1)S(1)} all-to-all(f16[16,112,256]{2,1,0:T(8,128)(2,1)S(1)} %fusion.2), channel_id=1, replica_groups=mesh['z'=8,'xl'=2,'y'=4,'c'=2,'xh'=2] {'xl','y','xh'}, dimensions={0} | all-to-all | bytes 1835008 | tf_op jit(solution)/shard_map/all_to_all | solution.py:469
  67.2 0.3 multiply_reduce_fusion
  67.6 0.1 select_convert_fusion.2
  67.7 0.4 collective-permute-start.9
  68.0 3.0 %collective-permute-start.8 = (f16[112,256]{1,0:T(8,128)(2,1)S(1)}, f16[112,256]{1,0:T(8,128)(2,1)S(1)}, u32[]{:S(2)}, u32[]{:S(2)}) collective-permute-start(f16[112,256]{1,0:T(8,128)(2,1)S(1)} %select_convert_fusion.2), channel_id=1, source_target_pairs={{0,64},{1,65},{2,66},{3,67},{4,68},{5,69},{6,70},{7,71},{8,72},{9,... | collective-permute-start | bytes 172040 | tf_op jit(solution)/shard_map/ppermute | solution.py:35
  71.0 0.0 collective-permute-start.7
  71.0 0.0 collective-permute-done.9
  71.1 2.2 %collective-permute-done.8 = f16[112,256]{1,0:T(8,128)(2,1)S(1)} collective-permute-done((f16[112,256]{1,0:T(8,128)(2,1)S(1)}, f16[112,256]{1,0:T(8,128)(2,1)S(1)}, u32[]{:S(2)}, u32[]{:S(2)}) %collective-permute-start.8) | collective-permute-done | bytes 57376 | tf_op jit(solution)/shard_map/ppermute | solution.py:35
  73.3 1.0 collective-permute-done.7
  74.2 0.1 add_add_fusion
  74.4 0.1 select_convert_fusion.1
  74.5 1.3 %collective-permute-start.10 = (f16[112,256]{1,0:T(8,128)(2,1)S(1)}, f16[112,256]{1,0:T(8,128)(2,1)S(1)}, u32[]{:S(2)}, u32[]{:S(2)}) collective-permute-start(f16[112,256]{1,0:T(8,128)(2,1)S(1)} %select_convert_fusion.1), channel_id=1, source_target_pairs={{0,224},{1,225},{2,226},{3,227},{4,228},{5,229},{6,230},{7,231},{8... | collective-permute-start | bytes 172040 | tf_op jit(solution)/shard_map/ppermute | solution.py:35
  75.8 4.8 %collective-permute-done.10 = f16[112,256]{1,0:T(8,128)(2,1)S(1)} collective-permute-done((f16[112,256]{1,0:T(8,128)(2,1)S(1)}, f16[112,256]{1,0:T(8,128)(2,1)S(1)}, u32[]{:S(2)}, u32[]{:S(2)}) %collective-permute-start.10) | collective-permute-done | bytes 57376 | tf_op jit(solution)/shard_map/ppermute | solution.py:35
  80.6 0.1 multiply_add_fusion
  80.8 0.1 select_convert_fusion
  80.8 0.1 broadcast_in_dim.147
  80.9 14.5 %all_to_all.23 = f16[16,112,256]{2,1,0:T(8,128)(2,1)S(1)} all-to-all(f16[16,112,256]{2,1,0:T(8,128)(2,1)S(1)} %broadcast_in_dim.147), channel_id=1, replica_groups=mesh['z'=8,'xl'=2,'y'=4,'c'=2,'xh'=2] {'xl','y','xh'}, dimensions={0} | all-to-all | bytes 1835008 | tf_op jit(solution)/shard_map/all_to_all | solution.py:478
  95.5 5.7 %collective-permute-start.11 = (f16[16,112,256]{2,1,0:T(8,128)(2,1)S(1)}, f16[16,112,256]{2,1,0:T(8,128)(2,1)S(1)}, u32[]{:S(2)}, u32[]{:S(2)}) collective-permute-start(f16[16,112,256]{2,1,0:T(8,128)(2,1)S(1)} %all_to_all.23), channel_id=1, source_target_pairs={{0,2},{1,3},{2,0},{3,1},{4,6},{5,7},{6,4},{7,5},{8,10},{9,11},{10,... | collective-permute-start | bytes 2752520 | tf_op jit(solution)/shard_map/ppermute | solution.py:35
  101.2 0.2 convert_element_type.78.half
  101.4 1.9 %collective-permute-done.11 = f16[16,112,256]{2,1,0:T(8,128)(2,1)S(1)} collective-permute-done((f16[16,112,256]{2,1,0:T(8,128)(2,1)S(1)}, f16[16,112,256]{2,1,0:T(8,128)(2,1)S(1)}, u32[]{:S(2)}, u32[]{:S(2)}) %collective-permute-start.11) | collective-permute-done | bytes 917536 | tf_op jit(solution)/shard_map/ppermute | solution.py:35
  103.3 0.2 convert_element_type.79.far
  103.5 3.0 %shard_map.122 = (f32[9,100,256]{2,1,0:T(8,128)}, f32[9,256,256]{2,1,0:T(8,128)}, f32[100,256]{1,0:T(8,128)}, f32[32,256]{1,0:T(8,128)}, f32[1,128]{1,0:T(1,128)}) custom-call(f32[16,112,256]{2,1,0:T(8,128)S(1)} %convert_element_type.78.half, f32[16,112,256]{2,1,0:T(8,128)S(1)} %convert_element_type.79.far), custom_call_target="tpu_custom_call" | custom-call | tf_op jit(solution)/shard_map/pallas_call | solution.py:431
  (13 shorter events, 0.2 us)
Async XLA Ops:
  0.6 28.0 %copy-start = (bf16[9,256,256]{2,1,0:T(8,128)(2,1)S(1)}, bf16[9,256,256]{2,1,0:T(8,128)(2,1)}, u32[]{:S(2)}) copy-start(bf16[9,256,256]{2,1,0:T(8,128)(2,1)} %w_mid.1) | copy-start | bytes 3538948
  3.4 10.9 %collective-permute-start = (f32[32,256]{1,0:T(8,128)S(1)}, f32[32,256]{1,0:T(8,128)S(1)}, u32[]{:S(2)}, u32[]{:S(2)}) collective-permute-start(f32[32,256]{1,0:T(8,128)S(1)} %get-tuple-element.21), channel_id=1, source_target_pairs={{0,1},{1,0},{2,3},{3,2},{4,5},{5,4},{6,7},{7,6},{8,9},{9,8},{10,11... | collective-permute-start | bytes 98312 | tf_op jit(solution)/shard_map/ppermute | solution.py:35
  6.2 14.3 %all-to-all-start = ((s32[16,1,32]{2,1,0:T(1,128)}), s32[16,1,32]{2,1,0:T(1,128)S(1)}, u32[]{:S(2)}, u32[]{:S(2)}) async-start(s32[16,1,32]{2,1,0:T(1,128)} %bitcast.1), calls=%async_computation | async-start | bytes 16384 | tf_op jit(solution)/shard_map/all_to_all | solution.py:495
  20.5 6.5 %collective-permute-start.1 = (bf16[64,256]{1,0:T(8,128)(2,1)S(1)}, bf16[64,256]{1,0:T(8,128)(2,1)S(1)}, u32[]{:S(2)}, u32[]{:S(2)}) collective-permute-start(bf16[64,256]{1,0:T(8,128)(2,1)S(1)} %shard_map.120.own), channel_id=1, source_target_pairs={{0,4},{1,5},{2,6},{3,7},{4,8},{5,9},{6,10},{7,11},{8,12},{9,13},{1... | collective-permute-start | bytes 98312 | tf_op jit(solution)/shard_map/ppermute | solution.py:35
  21.8 5.7 %collective-permute-start.2 = (bf16[64,256]{1,0:T(8,128)(2,1)S(1)}, bf16[64,256]{1,0:T(8,128)(2,1)S(1)}, u32[]{:S(2)}, u32[]{:S(2)}) collective-permute-start(bf16[64,256]{1,0:T(8,128)(2,1)S(1)} %shard_map.120.own), channel_id=1, source_target_pairs={{0,14},{1,15},{2,4},{3,5},{4,2},{5,3},{6,8},{7,9},{8,6},{9,7},{10,... | collective-permute-start | bytes 98312 | tf_op jit(solution)/shard_map/ppermute | solution.py:35
  25.6 1.9 %collective-permute-start.3 = (bf16[64,256]{1,0:T(8,128)(2,1)S(1)}, bf16[64,256]{1,0:T(8,128)(2,1)S(1)}, u32[]{:S(2)}, u32[]{:S(2)}) collective-permute-start(bf16[64,256]{1,0:T(8,128)(2,1)S(1)} %shard_map.120.own), channel_id=1, source_target_pairs={{0,2},{1,3},{2,0},{3,1},{4,6},{5,7},{6,4},{7,5},{8,10},{9,11},{10,... | collective-permute-start | bytes 98312 | tf_op jit(solution)/shard_map/ppermute | solution.py:35
  25.6 3.0 %collective-permute-start.4 = (bf16[64,256]{1,0:T(8,128)(2,1)S(1)}, bf16[64,256]{1,0:T(8,128)(2,1)S(1)}, u32[]{:S(2)}, u32[]{:S(2)}) collective-permute-start(bf16[64,256]{1,0:T(8,128)(2,1)S(1)} %shard_map.120.own), channel_id=1, source_target_pairs={{0,12},{1,13},{2,14},{3,15},{4,0},{5,1},{6,2},{7,3},{8,4},{9,5},{1... | collective-permute-start | bytes 98312 | tf_op jit(solution)/shard_map/ppermute | solution.py:35
  42.4 5.1 %collective-permute-start.5 = (f32[16,112,256]{2,1,0:T(8,128)S(1)}, f32[16,112,256]{2,1,0:T(8,128)S(1)}, u32[]{:S(2)}, u32[]{:S(2)}) collective-permute-start(f32[16,112,256]{2,1,0:T(8,128)S(1)} %slice_bitcast_fusion), channel_id=1, source_target_pairs={{0,2},{1,3},{2,0},{3,1},{4,6},{5,7},{6,4},{7,5},{8,10},{9,11},{10,... | collective-permute-start | bytes 5505032 | tf_op jit(solution)/shard_map/ppermute | solution.py:35
  43.9 3.4 %collective-permute-start.6 = (f32[8,256]{1,0:T(8,128)S(1)}, f32[8,256]{1,0:T(8,128)S(1)}, u32[]{:S(2)}, u32[]{:S(2)}) collective-permute-start(f32[8,256]{1,0:T(8,128)S(1)} %get-tuple-element.29), channel_id=1, source_target_pairs={{0,2},{1,3},{2,0},{3,1},{4,6},{5,7},{6,4},{7,5},{8,10},{9,11},{10,... | collective-permute-start | bytes 24584 | tf_op jit(solution)/shard_map/ppermute | solution.py:35
  67.7 3.4 %collective-permute-start.9 = (f16[112,256]{1,0:T(8,128)(2,1)S(1)}, f16[112,256]{1,0:T(8,128)(2,1)S(1)}, u32[]{:S(2)}, u32[]{:S(2)}) collective-permute-start(f16[112,256]{1,0:T(8,128)(2,1)S(1)} %select_convert_fusion.2), channel_id=1, source_target_pairs={{0,96},{1,97},{2,98},{3,99},{4,100},{5,101},{6,102},{7,103},{8,104... | collective-permute-start | bytes 172040 | tf_op jit(solution)/shard_map/ppermute | solution.py:35
  68.0 5.2 %collective-permute-start.8 = (f16[112,256]{1,0:T(8,128)(2,1)S(1)}, f16[112,256]{1,0:T(8,128)(2,1)S(1)}, u32[]{:S(2)}, u32[]{:S(2)}) collective-permute-start(f16[112,256]{1,0:T(8,128)(2,1)S(1)} %select_convert_fusion.2), channel_id=1, source_target_pairs={{0,64},{1,65},{2,66},{3,67},{4,68},{5,69},{6,70},{7,71},{8,72},{9,... | collective-permute-start | bytes 172040 | tf_op jit(solution)/shard_map/ppermute | solution.py:35
  71.0 3.2 %collective-permute-start.7 = (f16[112,256]{1,0:T(8,128)(2,1)S(1)}, f16[112,256]{1,0:T(8,128)(2,1)S(1)}, u32[]{:S(2)}, u32[]{:S(2)}) collective-permute-start(f16[112,256]{1,0:T(8,128)(2,1)S(1)} %select_convert_fusion.2), channel_id=1, source_target_pairs={{0,32},{1,33},{2,34},{3,35},{4,36},{5,37},{6,38},{7,39},{8,40},{9,... | collective-permute-start | bytes 172040 | tf_op jit(solution)/shard_map/ppermute | solution.py:35
  74.5 6.1 %collective-permute-start.10 = (f16[112,256]{1,0:T(8,128)(2,1)S(1)}, f16[112,256]{1,0:T(8,128)(2,1)S(1)}, u32[]{:S(2)}, u32[]{:S(2)}) collective-permute-start(f16[112,256]{1,0:T(8,128)(2,1)S(1)} %select_convert_fusion.1), channel_id=1, source_target_pairs={{0,224},{1,225},{2,226},{3,227},{4,228},{5,229},{6,230},{7,231},{8... | collective-permute-start | bytes 172040 | tf_op jit(solution)/shard_map/ppermute | solution.py:35
  95.5 7.8 %collective-permute-start.11 = (f16[16,112,256]{2,1,0:T(8,128)(2,1)S(1)}, f16[16,112,256]{2,1,0:T(8,128)(2,1)S(1)}, u32[]{:S(2)}, u32[]{:S(2)}) collective-permute-start(f16[16,112,256]{2,1,0:T(8,128)(2,1)S(1)} %all_to_all.23), channel_id=1, source_target_pairs={{0,2},{1,3},{2,0},{3,1},{4,6},{5,7},{6,4},{7,5},{8,10},{9,11},{10,... | collective-permute-start | bytes 2752520 | tf_op jit(solution)/shard_map/ppermute | solution.py:35

commit v10 on v8

--- a/solution.py
+++ b/solution.py
@@ -356,7 +356,7 @@
     return jnp.ceil(jnp.log2(jnp.maximum(bound, 1e-30)))
 
 
-def final_kernel(half, far, o_in, o_mid, o_out, o_noise, o_loss, t, u, out_sems):
+def final_kernel(half, far, o_in, o_mid, o_out, o_noise, o_loss, t, u, w, out_sems):
     core = lax.axis_index("c")
     for slot, ref in ((core, half), (1 - core, far)):
         for k in range(16):
@@ -405,7 +405,7 @@
     pieces = [get(9 * C + V * k, V) for k in range(9)]
     scale = scale_of(pieces, 9 * V * C)
     for k in range(9):
-        emit(pieces[k], scale, o_in.at[k], None, 0)
+        emit(pieces[k], scale, w.at[k], o_in.at[k], 9 + k)
     pieces = get(9 * C + 9 * V, V)
     emit(pieces, scale_of([pieces], V * C), o_out, None, 0)
     pieces = [(k, 1, k, ROWS) for k in range(NB)]
@@ -521,10 +521,11 @@
         [
             pltpu.VMEM((NB, BR, C), f32),
             pltpu.VMEM((9, C, C), f32),
-            pltpu.SemaphoreType.DMA((9,)),
+            pltpu.VMEM((9, V, C), f32),
+            pltpu.SemaphoreType.DMA((18,)),
         ],
         (half, far),
-        {("out", 1)},
+        {("out", 0), ("out", 1)},
         kept=(0, 1),
     )
     return o_in, o_mid, o_out, o_noise, o_loss[0, 0]

time: 107 us -> 107 us (level)
  no operation moved by 1% of the time
where the time goes in v10:
time: 107 us
  blocking collectives  32.7 us (31%)
  starting transfers between devices  30.3 us (28%)
  waiting for transfers between devices  21.3 us (20%)
  Pallas kernels  19.5 us (18%)
  other arithmetic  1.85 us (2%)
    ppermute x12, starting transfers between devices, send(): return lax.ppermute(v, AX, perm(f))  22.2 us
    pallas_call x4, Pallas kernels, call(): pl.pallas_call(kernel, out_shape=[pltpu.VMEM(o[0], o[1]) if len(o) > 2 el...  19.5 us
    all_to_all x1, blocking collectives, sum_all(): got = lax.all_to_all(s.astype(f16), xy, 0, 0, tiled=True)  18.1 us
    ppermute x12, waiting for transfers between devices, send(): return lax.ppermute(v, AX, perm(f))  15.2 us
    all_to_all x1, blocking collectives, sum_all(): lax.all_to_all(jnp.broadcast_to(s[None], (16,) + s.shape), xy, 0, 0, tile...  14.5 us
    all_to_all x1, starting transfers between devices, body(): seeds = lax.all_to_all(seeds, ('z', 'xl'), 0, 0, tiled=True)  8.05 us
    all_to_all x1, waiting for transfers between devices, body(): seeds = lax.all_to_all(seeds, ('z', 'xl'), 0, 0, tiled=True)  6.14 us
  transfers between devices with their start and end apart: 13, of which 7 were waited for; matrix products, arithmetic and copies ran while one was open for 0% of the time, Pallas kernels for 0%

profile of v10, /device:TPU:33, one launch (start us, length us, event | category | flops | bytes accessed | tf_op | source)
XLA Modules:
  0.0 106.8 jit_solution(9514098107750031063)
XLA Ops:
  0.6 0.0 copy-start
  0.6 2.7 %shard_map.119 = (f32[2,384,256]{2,1,0:T(8,128)S(1)}, f32[32,256]{1,0:T(8,128)S(1)}, s32[16,32]{1,0:T(8,128)}, bf16[9,100,256]{2,1,0:T(8,128)(2,1)S(1)}, bf16[10...) custom-call(bf16[100,2,360]{2,1,0:T(2,128)(2,1)} %state.1, bf16[100,2,360]{2,1,0:T(2,128)(2,1)} %target.1, s32[2,360]{1,0:T(2,128)} %land.1, ...), custom_call_target="tpu_custom_call" | custom-call | tf_op jit(solution)/shard_map/pallas_call | solution.py:426
  3.4 2.8 %collective-permute-start = (f32[32,256]{1,0:T(8,128)S(1)}, f32[32,256]{1,0:T(8,128)S(1)}, u32[]{:S(2)}, u32[]{:S(2)}) collective-permute-start(f32[32,256]{1,0:T(8,128)S(1)} %get-tuple-element.21), channel_id=1, source_target_pairs={{0,1},{1,0},{2,3},{3,2},{4,5},{5,4},{6,7},{7,6},{8,9},{9,8},{10,11... | collective-permute-start | bytes 98312 | tf_op jit(solution)/shard_map/ppermute | solution.py:35
  6.2 8.1 %all-to-all-start = ((s32[16,1,32]{2,1,0:T(1,128)}), s32[16,1,32]{2,1,0:T(1,128)S(1)}, u32[]{:S(2)}, u32[]{:S(2)}) async-start(s32[16,1,32]{2,1,0:T(1,128)} %bitcast.1), calls=%async_computation | async-start | bytes 16384 | tf_op jit(solution)/shard_map/all_to_all | solution.py:490
  14.3 0.0 collective-permute-done.edge
  14.3 0.1 shard_map.120.own
  14.4 6.1 %all-to-all-done = s32[16,1,32]{2,1,0:T(1,128)S(1)} async-done(((s32[16,1,32]{2,1,0:T(1,128)}), s32[16,1,32]{2,1,0:T(1,128)S(1)}, u32[]{:S(2)}, u32[]{:S(2)}) %all-to-all-start) | async-done | bytes 2080 | tf_op jit(solution)/shard_map/all_to_all | solution.py:490
  20.5 1.3 %collective-permute-start.1 = (bf16[64,256]{1,0:T(8,128)(2,1)S(1)}, bf16[64,256]{1,0:T(8,128)(2,1)S(1)}, u32[]{:S(2)}, u32[]{:S(2)}) collective-permute-start(bf16[64,256]{1,0:T(8,128)(2,1)S(1)} %shard_map.120.own), channel_id=1, source_target_pairs={{0,4},{1,5},{2,6},{3,7},{4,8},{5,9},{6,10},{7,11},{8,12},{9,13},{1... | collective-permute-start | bytes 98312 | tf_op jit(solution)/shard_map/ppermute | solution.py:35
  21.8 3.8 %collective-permute-start.2 = (bf16[64,256]{1,0:T(8,128)(2,1)S(1)}, bf16[64,256]{1,0:T(8,128)(2,1)S(1)}, u32[]{:S(2)}, u32[]{:S(2)}) collective-permute-start(bf16[64,256]{1,0:T(8,128)(2,1)S(1)} %shard_map.120.own), channel_id=1, source_target_pairs={{0,2},{1,3},{2,4},{3,5},{4,6},{5,7},{6,8},{7,9},{8,10},{9,11},{10,... | collective-permute-start | bytes 98312 | tf_op jit(solution)/shard_map/ppermute | solution.py:35
  25.6 0.0 collective-permute-start.3
  25.6 1.4 %collective-permute-start.4 = (bf16[64,256]{1,0:T(8,128)(2,1)S(1)}, bf16[64,256]{1,0:T(8,128)(2,1)S(1)}, u32[]{:S(2)}, u32[]{:S(2)}) collective-permute-start(bf16[64,256]{1,0:T(8,128)(2,1)S(1)} %shard_map.120.own), channel_id=1, source_target_pairs={{0,12},{1,13},{2,14},{3,15},{4,0},{5,1},{6,2},{7,3},{8,4},{9,5},{1... | collective-permute-start | bytes 98312 | tf_op jit(solution)/shard_map/ppermute | solution.py:35
  27.1 0.0 collective-permute-done.1.n2
  27.1 0.0 collective-permute-done.2.n1
  27.1 1.9 %collective-permute-done.3.s1 = bf16[64,256]{1,0:T(8,128)(2,1)S(1)} collective-permute-done((bf16[64,256]{1,0:T(8,128)(2,1)S(1)}, bf16[64,256]{1,0:T(8,128)(2,1)S(1)}, u32[]{:S(2)}, u32[]{:S(2)}) %collective-permute-start.3) | collective-permute-done | bytes 32800 | tf_op jit(solution)/shard_map/ppermute | solution.py:35
  29.0 0.0 collective-permute-done.4.s2
  29.0 0.0 copy-done
  29.0 13.6 %shard_map.121 = (f32[2,16,112,256]{3,2,1,0:T(8,128)S(1)}, f32[8,256]{1,0:T(8,128)S(1)}) custom-call(bf16[64,256]{1,0:T(8,128)(2,1)S(1)} %collective-permute-done.1.n2, bf16[64,256]{1,0:T(8,128)(2,1)S(1)} %collective-permute-done.2.n1, bf16[64,256]{1,0:T(8,128)(2,1)S(1)} %shard_map.120.own, bf16[64,256]{1,0:T(8,128)(2,1)S(1)} %collective-permute-done.3.s1, ...), custom_call_target="tpu_custom_call" | custom-call | tf_op jit(solution)/shard_map/pallas_call | solution.py:426
  42.6 0.1 slice_bitcast_fusion
  42.7 2.4 %collective-permute-start.5 = (f32[16,112,256]{2,1,0:T(8,128)S(1)}, f32[16,112,256]{2,1,0:T(8,128)S(1)}, u32[]{:S(2)}, u32[]{:S(2)}) collective-permute-start(f32[16,112,256]{2,1,0:T(8,128)S(1)} %slice_bitcast_fusion), channel_id=1, source_target_pairs={{0,2},{1,3},{2,0},{3,1},{4,6},{5,7},{6,4},{7,5},{8,10},{9,11},{10,... | collective-permute-start | bytes 5505032 | tf_op jit(solution)/shard_map/ppermute | solution.py:35
  45.2 0.1 collective-permute-start.6
  45.3 3.3 %collective-permute-done.6 = f32[8,256]{1,0:T(8,128)S(1)} collective-permute-done((f32[8,256]{1,0:T(8,128)S(1)}, f32[8,256]{1,0:T(8,128)S(1)}, u32[]{:S(2)}, u32[]{:S(2)}) %collective-permute-start.6) | collective-permute-done | bytes 8224 | tf_op jit(solution)/shard_map/ppermute | solution.py:35
  48.6 0.1 broadcast_select_fusion
  48.7 0.0 collective-permute-done.5
  48.7 0.4 fusion.2
  49.1 18.1 %all_to_all.22 = f16[16,112,256]{2,1,0:T(8,128)(2,1)S(1)} all-to-all(f16[16,112,256]{2,1,0:T(8,128)(2,1)S(1)} %fusion.2), channel_id=1, replica_groups=mesh['z'=8,'xl'=2,'y'=4,'c'=2,'xh'=2] {'xl','y','xh'}, dimensions={0} | all-to-all | bytes 1835008 | tf_op jit(solution)/shard_map/all_to_all | solution.py:464
  67.3 0.3 multiply_reduce_fusion
  67.7 0.1 select_convert_fusion.2
  67.8 0.4 collective-permute-start.9
  68.1 3.0 %collective-permute-start.8 = (f16[112,256]{1,0:T(8,128)(2,1)S(1)}, f16[112,256]{1,0:T(8,128)(2,1)S(1)}, u32[]{:S(2)}, u32[]{:S(2)}) collective-permute-start(f16[112,256]{1,0:T(8,128)(2,1)S(1)} %select_convert_fusion.2), channel_id=1, source_target_pairs={{0,64},{1,65},{2,66},{3,67},{4,68},{5,69},{6,70},{7,71},{8,72},{9,... | collective-permute-start | bytes 172040 | tf_op jit(solution)/shard_map/ppermute | solution.py:35
  71.1 0.0 collective-permute-start.7
  71.1 0.0 collective-permute-done.9
  71.1 2.2 %collective-permute-done.8 = f16[112,256]{1,0:T(8,128)(2,1)S(1)} collective-permute-done((f16[112,256]{1,0:T(8,128)(2,1)S(1)}, f16[112,256]{1,0:T(8,128)(2,1)S(1)}, u32[]{:S(2)}, u32[]{:S(2)}) %collective-permute-start.8) | collective-permute-done | bytes 57376 | tf_op jit(solution)/shard_map/ppermute | solution.py:35
  73.3 1.0 collective-permute-done.7
  74.3 0.1 add_add_fusion
  74.5 0.1 select_convert_fusion.1
  74.6 1.3 %collective-permute-start.10 = (f16[112,256]{1,0:T(8,128)(2,1)S(1)}, f16[112,256]{1,0:T(8,128)(2,1)S(1)}, u32[]{:S(2)}, u32[]{:S(2)}) collective-permute-start(f16[112,256]{1,0:T(8,128)(2,1)S(1)} %select_convert_fusion.1), channel_id=1, source_target_pairs={{0,224},{1,225},{2,226},{3,227},{4,228},{5,229},{6,230},{7,231},{8... | collective-permute-start | bytes 172040 | tf_op jit(solution)/shard_map/ppermute | solution.py:35
  75.9 4.8 %collective-permute-done.10 = f16[112,256]{1,0:T(8,128)(2,1)S(1)} collective-permute-done((f16[112,256]{1,0:T(8,128)(2,1)S(1)}, f16[112,256]{1,0:T(8,128)(2,1)S(1)}, u32[]{:S(2)}, u32[]{:S(2)}) %collective-permute-start.10) | collective-permute-done | bytes 57376 | tf_op jit(solution)/shard_map/ppermute | solution.py:35
  80.7 0.1 multiply_add_fusion
  80.8 0.1 select_convert_fusion
  80.9 0.1 broadcast_in_dim.147
  81.0 14.5 %all_to_all.23 = f16[16,112,256]{2,1,0:T(8,128)(2,1)S(1)} all-to-all(f16[16,112,256]{2,1,0:T(8,128)(2,1)S(1)} %broadcast_in_dim.147), channel_id=1, replica_groups=mesh['z'=8,'xl'=2,'y'=4,'c'=2,'xh'=2] {'xl','y','xh'}, dimensions={0} | all-to-all | bytes 1835008 | tf_op jit(solution)/shard_map/all_to_all | solution.py:473
  95.5 5.7 %collective-permute-start.11 = (f16[16,112,256]{2,1,0:T(8,128)(2,1)S(1)}, f16[16,112,256]{2,1,0:T(8,128)(2,1)S(1)}, u32[]{:S(2)}, u32[]{:S(2)}) collective-permute-start(f16[16,112,256]{2,1,0:T(8,128)(2,1)S(1)} %all_to_all.23), channel_id=1, source_target_pairs={{0,2},{1,3},{2,0},{3,1},{4,6},{5,7},{6,4},{7,5},{8,10},{9,11},{10,... | collective-permute-start | bytes 2752520 | tf_op jit(solution)/shard_map/ppermute | solution.py:35
  101.3 0.2 convert_element_type.78.half
  101.4 1.9 %collective-permute-done.11 = f16[16,112,256]{2,1,0:T(8,128)(2,1)S(1)} collective-permute-done((f16[16,112,256]{2,1,0:T(8,128)(2,1)S(1)}, f16[16,112,256]{2,1,0:T(8,128)(2,1)S(1)}, u32[]{:S(2)}, u32[]{:S(2)}) %collective-permute-start.11) | collective-permute-done | bytes 917536 | tf_op jit(solution)/shard_map/ppermute | solution.py:35
  103.4 0.2 convert_element_type.79.far
  103.5 3.1 %shard_map.122 = (f32[9,100,256]{2,1,0:T(8,128)}, f32[9,256,256]{2,1,0:T(8,128)}, f32[100,256]{1,0:T(8,128)}, f32[32,256]{1,0:T(8,128)}, f32[1,128]{1,0:T(1,128)}) custom-call(f32[16,112,256]{2,1,0:T(8,128)S(1)} %convert_element_type.78.half, f32[16,112,256]{2,1,0:T(8,128)S(1)} %convert_element_type.79.far), custom_call_target="tpu_custom_call" | custom-call | tf_op jit(solution)/shard_map/pallas_call | solution.py:426
  (13 shorter events, 0.2 us)
Async XLA Ops:
  0.6 28.4 %copy-start = (bf16[9,256,256]{2,1,0:T(8,128)(2,1)S(1)}, bf16[9,256,256]{2,1,0:T(8,128)(2,1)}, u32[]{:S(2)}) copy-start(bf16[9,256,256]{2,1,0:T(8,128)(2,1)} %w_mid.1) | copy-start | bytes 3538948
  3.4 10.9 %collective-permute-start = (f32[32,256]{1,0:T(8,128)S(1)}, f32[32,256]{1,0:T(8,128)S(1)}, u32[]{:S(2)}, u32[]{:S(2)}) collective-permute-start(f32[32,256]{1,0:T(8,128)S(1)} %get-tuple-element.21), channel_id=1, source_target_pairs={{0,1},{1,0},{2,3},{3,2},{4,5},{5,4},{6,7},{7,6},{8,9},{9,8},{10,11... | collective-permute-start | bytes 98312 | tf_op jit(solution)/shard_map/ppermute | solution.py:35
  6.2 14.3 %all-to-all-start = ((s32[16,1,32]{2,1,0:T(1,128)}), s32[16,1,32]{2,1,0:T(1,128)S(1)}, u32[]{:S(2)}, u32[]{:S(2)}) async-start(s32[16,1,32]{2,1,0:T(1,128)} %bitcast.1), calls=%async_computation | async-start | bytes 16384 | tf_op jit(solution)/shard_map/all_to_all | solution.py:490
  20.5 6.6 %collective-permute-start.1 = (bf16[64,256]{1,0:T(8,128)(2,1)S(1)}, bf16[64,256]{1,0:T(8,128)(2,1)S(1)}, u32[]{:S(2)}, u32[]{:S(2)}) collective-permute-start(bf16[64,256]{1,0:T(8,128)(2,1)S(1)} %shard_map.120.own), channel_id=1, source_target_pairs={{0,4},{1,5},{2,6},{3,7},{4,8},{5,9},{6,10},{7,11},{8,12},{9,13},{1... | collective-permute-start | bytes 98312 | tf_op jit(solution)/shard_map/ppermute | solution.py:35
  21.8 5.3 %collective-permute-start.2 = (bf16[64,256]{1,0:T(8,128)(2,1)S(1)}, bf16[64,256]{1,0:T(8,128)(2,1)S(1)}, u32[]{:S(2)}, u32[]{:S(2)}) collective-permute-start(bf16[64,256]{1,0:T(8,128)(2,1)S(1)} %shard_map.120.own), channel_id=1, source_target_pairs={{0,2},{1,3},{2,4},{3,5},{4,6},{5,7},{6,8},{7,9},{8,10},{9,11},{10,... | collective-permute-start | bytes 98312 | tf_op jit(solution)/shard_map/ppermute | solution.py:35
  25.6 3.3 %collective-permute-start.3 = (bf16[64,256]{1,0:T(8,128)(2,1)S(1)}, bf16[64,256]{1,0:T(8,128)(2,1)S(1)}, u32[]{:S(2)}, u32[]{:S(2)}) collective-permute-start(bf16[64,256]{1,0:T(8,128)(2,1)S(1)} %shard_map.120.own), channel_id=1, source_target_pairs={{0,14},{1,15},{2,0},{3,1},{4,2},{5,3},{6,4},{7,5},{8,6},{9,7},{10,... | collective-permute-start | bytes 98312 | tf_op jit(solution)/shard_map/ppermute | solution.py:35
  25.6 3.3 %collective-permute-start.4 = (bf16[64,256]{1,0:T(8,128)(2,1)S(1)}, bf16[64,256]{1,0:T(8,128)(2,1)S(1)}, u32[]{:S(2)}, u32[]{:S(2)}) collective-permute-start(bf16[64,256]{1,0:T(8,128)(2,1)S(1)} %shard_map.120.own), channel_id=1, source_target_pairs={{0,12},{1,13},{2,14},{3,15},{4,0},{5,1},{6,2},{7,3},{8,4},{9,5},{1... | collective-permute-start | bytes 98312 | tf_op jit(solution)/shard_map/ppermute | solution.py:35
  42.7 6.0 %collective-permute-start.5 = (f32[16,112,256]{2,1,0:T(8,128)S(1)}, f32[16,112,256]{2,1,0:T(8,128)S(1)}, u32[]{:S(2)}, u32[]{:S(2)}) collective-permute-start(f32[16,112,256]{2,1,0:T(8,128)S(1)} %slice_bitcast_fusion), channel_id=1, source_target_pairs={{0,2},{1,3},{2,0},{3,1},{4,6},{5,7},{6,4},{7,5},{8,10},{9,11},{10,... | collective-permute-start | bytes 5505032 | tf_op jit(solution)/shard_map/ppermute | solution.py:35
  45.2 3.4 %collective-permute-start.6 = (f32[8,256]{1,0:T(8,128)S(1)}, f32[8,256]{1,0:T(8,128)S(1)}, u32[]{:S(2)}, u32[]{:S(2)}) collective-permute-start(f32[8,256]{1,0:T(8,128)S(1)} %get-tuple-element.29), channel_id=1, source_target_pairs={{0,2},{1,3},{2,0},{3,1},{4,6},{5,7},{6,4},{7,5},{8,10},{9,11},{10,... | collective-permute-start | bytes 24584 | tf_op jit(solution)/shard_map/ppermute | solution.py:35
  67.8 3.4 %collective-permute-start.9 = (f16[112,256]{1,0:T(8,128)(2,1)S(1)}, f16[112,256]{1,0:T(8,128)(2,1)S(1)}, u32[]{:S(2)}, u32[]{:S(2)}) collective-permute-start(f16[112,256]{1,0:T(8,128)(2,1)S(1)} %select_convert_fusion.2), channel_id=1, source_target_pairs={{0,96},{1,97},{2,98},{3,99},{4,100},{5,101},{6,102},{7,103},{8,104... | collective-permute-start | bytes 172040 | tf_op jit(solution)/shard_map/ppermute | solution.py:35
  68.1 5.2 %collective-permute-start.8 = (f16[112,256]{1,0:T(8,128)(2,1)S(1)}, f16[112,256]{1,0:T(8,128)(2,1)S(1)}, u32[]{:S(2)}, u32[]{:S(2)}) collective-permute-start(f16[112,256]{1,0:T(8,128)(2,1)S(1)} %select_convert_fusion.2), channel_id=1, source_target_pairs={{0,64},{1,65},{2,66},{3,67},{4,68},{5,69},{6,70},{7,71},{8,72},{9,... | collective-permute-start | bytes 172040 | tf_op jit(solution)/shard_map/ppermute | solution.py:35
  71.1 3.2 %collective-permute-start.7 = (f16[112,256]{1,0:T(8,128)(2,1)S(1)}, f16[112,256]{1,0:T(8,128)(2,1)S(1)}, u32[]{:S(2)}, u32[]{:S(2)}) collective-permute-start(f16[112,256]{1,0:T(8,128)(2,1)S(1)} %select_convert_fusion.2), channel_id=1, source_target_pairs={{0,32},{1,33},{2,34},{3,35},{4,36},{5,37},{6,38},{7,39},{8,40},{9,... | collective-permute-start | bytes 172040 | tf_op jit(solution)/shard_map/ppermute | solution.py:35
  74.6 6.1 %collective-permute-start.10 = (f16[112,256]{1,0:T(8,128)(2,1)S(1)}, f16[112,256]{1,0:T(8,128)(2,1)S(1)}, u32[]{:S(2)}, u32[]{:S(2)}) collective-permute-start(f16[112,256]{1,0:T(8,128)(2,1)S(1)} %select_convert_fusion.1), channel_id=1, source_target_pairs={{0,224},{1,225},{2,226},{3,227},{4,228},{5,229},{6,230},{7,231},{8... | collective-permute-start | bytes 172040 | tf_op jit(solution)/shard_map/ppermute | solution.py:35
  95.5 7.8 %collective-permute-start.11 = (f16[16,112,256]{2,1,0:T(8,128)(2,1)S(1)}, f16[16,112,256]{2,1,0:T(8,128)(2,1)S(1)}, u32[]{:S(2)}, u32[]{:S(2)}) collective-permute-start(f16[16,112,256]{2,1,0:T(8,128)(2,1)S(1)} %all_to_all.23), channel_id=1, source_target_pairs={{0,2},{1,3},{2,0},{3,1},{4,6},{5,7},{6,4},{7,5},{8,10},{9,11},{10,... | collective-permute-start | bytes 2752520 | tf_op jit(solution)/shard_map/ppermute | solution.py:35
